TPU v7x, 32 devices: a whole 2x2x4 slice. The times are simulated.
32 devices in a mesh: seq: 8 (over y, x, core), head: 4 (over z).
Axes of the slice: x: 2, y: 2, z: 4, core: 2. Of those that a mesh axis runs over, the one named last changes fastest.
Arguments:
- queries: float32 [1024, 2048], P('seq', 'head'), may hold values from -24 to 24
- keys: float32 [1024, 512], P('seq', 'head'), may hold values from -24 to 24
- values: float32 [1024, 512], P('seq', 'head'), may hold values from -6 to 6
- grad_out: float32 [1024, 2048], P('seq', 'head'), may hold values from -6 to 6
- out_weight: float32 [2048, 2048], P('head'), may hold values from -0.125 to 0.125
Outputs:
- grad_q: float32 [1024, 2048], P('seq', 'head')
- grad_k: float32 [1024, 512], P('seq', 'head')
- grad_v: float32 [1024, 512], P('seq', 'head')
- grad_wo: float32 [2048, 2048], P('head', 'seq')
All inputs are finite; a program needn't handle non-finite values.
Results may differ from a plain program's by a relative error of at most 0.0003.
Values sent between devices are 32-bit elements; how exact they have to be, the bound alone decides.
No kernel may reach another device: no remote copies, remote signals or barrier semaphores. Data moves between devices by JAX's collectives and lax.ppermute only.
A program may use at most 128 MiB of HBM per device.

v0:
```python
import functools
import math

import jax
import jax.numpy as jnp
from jax import lax
from jax.experimental import pallas as pl
from jax.experimental.pallas import tpu as pltpu
from jax.sharding import PartitionSpec as P

HD = 128
GROUP = 4
CORES = 2
MASKED = -1e30
F32 = jnp.float32
BF16 = jnp.bfloat16

NN = (((1,), (0,)), ((), ()))
NT = (((1,), (1,)), ((), ()))


def mm(a, b, dims=NN):
    return lax.dot_general(a, b, dims, preferred_element_type=F32)


def two(x):
    hi = x.astype(BF16)
    return hi, (x - hi.astype(F32)).astype(BF16)


def three(x):
    first = x.astype(BF16)
    rest = x - first.astype(F32)
    second = rest.astype(BF16)
    return first, second, (rest - second.astype(F32)).astype(BF16)


def cost(flops, size):
    return pl.CostEstimate(flops=flops, transcendentals=0, bytes_accessed=size)


def params():
    return pltpu.CompilerParams(vmem_limit_bytes=48 * 1024 * 1024)


def load_blocks(refs, dst, column):
    row = 0
    for ref in refs:
        count = ref.shape[0]
        dst[row : row + count, :] = ref[:, column : column + HD]
        row += count


def forward_kernel(score_scale, q_ref, *refs):
    pieces = refs[:-6]
    attn_ref, exp_ref, inv_ref, keys, values, score = refs[-6:]
    tokens = q_ref.shape[0]
    rows = GROUP * tokens
    total = keys.shape[0]
    blocks = total // tokens
    chips = blocks // CORES
    me = lax.axis_index("seq")
    load_blocks(pieces, keys, 0)
    load_blocks(pieces, values, HD)
    q1, q2, q3 = three(stacked_queries(q_ref))
    q11 = jnp.concatenate([q1, q1], axis=1)
    q22 = jnp.concatenate([q2, q2], axis=1)
    q13 = jnp.concatenate([q1, q3], axis=1)
    key_row = lax.broadcasted_iota(jnp.int32, (tokens, rows), 0)
    query_row = lax.broadcasted_iota(jnp.int32, (tokens, rows), 1) % tokens
    offset = key_row - query_row

    def scores(b, top):
        own = (b // chips) ^ (me % CORES)
        block = ((me // CORES) ^ (b % chips)) * CORES + own
        at = pl.ds(pl.multiple_of(b * tokens, tokens), tokens)
        k1, k2, k3 = three(keys[at, :])
        k12 = jnp.concatenate([k1, k2], axis=1)
        k31 = jnp.concatenate([k3, k1], axis=1)
        s = mm(k31, q13, NT) + mm(k12, q22, NT) + mm(k12, q11, NT)
        s = jnp.where(offset <= (me - block) * tokens, s * score_scale, MASKED)
        score[at, :] = s
        return jnp.maximum(top, jnp.max(s, axis=0, keepdims=True))

    top = lax.fori_loop(0, blocks, scores, jnp.full((1, rows), MASKED, F32), unroll=2)

    def weigh(b, state):
        norm, acc = state
        at = pl.ds(pl.multiple_of(b * tokens, tokens), tokens)
        e = jnp.exp(score[at, :] - top)
        exp_ref[at, :] = e
        eh, el = two(e)
        vh, vl = two(values[at, :].T)
        both = mm(jnp.concatenate([vh, vl], axis=0), eh)
        acc = acc + (both[:HD] + both[HD:] + mm(vh, el))
        return norm + jnp.sum(e, axis=0, keepdims=True), acc

    norm, acc = lax.fori_loop(
        0, blocks, weigh, (jnp.zeros((1, rows), F32), jnp.zeros((HD, rows), F32)), unroll=2
    )
    inv = 1.0 / norm
    inv_ref[...] = jnp.broadcast_to(inv, inv_ref.shape)
    out = acc * inv
    for g in range(GROUP):
        attn_ref[g * HD : (g + 1) * HD, :] = out[:, g * tokens : (g + 1) * tokens]


def forward(q, pieces, total, score_scale):
    tokens = q.shape[0]
    rows = GROUP * tokens
    return pl.pallas_call(
        functools.partial(forward_kernel, score_scale),
        out_shape=(
            jax.ShapeDtypeStruct((GROUP * HD, tokens), F32),
            jax.ShapeDtypeStruct((total, rows), F32),
            jax.ShapeDtypeStruct((8, rows), F32),
        ),
        scratch_shapes=[
            pltpu.VMEM((total, HD), F32),
            pltpu.VMEM((total, HD), F32),
            pltpu.VMEM((total, rows), F32),
        ],
        compiler_params=params(),
        cost_estimate=cost(36 * total * rows * HD, 8 * total * rows),
        name="attn_fwd",
    )(q, *pieces)


def stacked_queries(q_ref):
    return jnp.concatenate([q_ref[:, g * HD : (g + 1) * HD] for g in range(GROUP)], axis=0)


def stacked_grads(d_ref):
    return jnp.concatenate([d_ref[g * HD : (g + 1) * HD, :] for g in range(GROUP)], axis=1)


def key_grads(score_scale, first, q, d, exp_ref, inv, dp_ref, delta, keys, out_ref, acc):
    rows = q.shape[0]
    tokens = rows // GROUP
    qh, ql = two(q)
    qhl = jnp.concatenate([qh, ql], axis=1)
    dh, dl = two(d)
    dhl = jnp.concatenate([dh, dl], axis=0)

    def grads(b, acc):
        to = pl.ds(pl.multiple_of(b * tokens, tokens), tokens)
        at = pl.ds(pl.multiple_of(first + b * tokens, tokens), tokens)
        p = exp_ref[at, :] * inv
        ds = p * (dp_ref[at, :] - delta) * score_scale
        ph, plo = two(p)
        sh, sl = two(ds)
        kh, kl = two(keys[to, :].T)
        both = mm(jnp.concatenate([kh, kl], axis=0), sh)
        acc = acc + (both[:HD] + both[HD:] + mm(kh, sl))
        dk = mm(sh, qhl)
        out_ref[to, 0:HD] = dk[:, :HD] + dk[:, HD:] + mm(sl, qh)
        dv = mm(ph, dhl, NT)
        out_ref[to, HD : 2 * HD] = dv[:, :HD] + dv[:, HD:] + mm(plo, dh, NT)
        return acc

    return lax.fori_loop(0, out_ref.shape[0] // tokens, grads, acc, unroll=2)


def backward_far_kernel(score_scale, q_ref, d_ref, exp_ref, inv_ref, *refs):
    pieces = refs[:-6]
    acc_ref, dp_ref, delta_ref, send_ref, keys, values = refs[-6:]
    tokens = q_ref.shape[0]
    rows = GROUP * tokens
    total = values.shape[0]
    load_blocks(pieces[-1:], keys, 0)
    load_blocks(pieces, values, HD)
    d = stacked_grads(d_ref)
    dh, dl = two(d)
    dhh = jnp.concatenate([dh, dh], axis=0)
    inv = inv_ref[0:1, :]

    def probs(b, delta):
        at = pl.ds(pl.multiple_of(b * tokens, tokens), tokens)
        vh, vl = two(values[at, :])
        dp = mm(vh, dl) + mm(jnp.concatenate([vh, vl], axis=1), dhh)
        dp_ref[at, :] = dp
        return delta + jnp.sum(exp_ref[at, :] * dp, axis=0, keepdims=True)

    delta = lax.fori_loop(0, total // tokens, probs, jnp.zeros((1, rows), F32), unroll=2) * inv
    delta_ref[...] = jnp.broadcast_to(delta, delta_ref.shape)
    acc_ref[...] = key_grads(
        score_scale,
        total - send_ref.shape[0],
        stacked_queries(q_ref),
        d,
        exp_ref,
        inv,
        dp_ref,
        delta,
        keys,
        send_ref,
        jnp.zeros((HD, rows), F32),
    )


def backward_near_kernel(
    score_scale, q_ref, d_ref, exp_ref, inv_ref, acc_ref, dp_ref, delta_ref, *refs
):
    pieces = refs[:-3]
    dq_ref, keep_ref, keys = refs[-3:]
    tokens = q_ref.shape[0]
    load_blocks(pieces, keys, 0)
    acc = key_grads(
        score_scale,
        0,
        stacked_queries(q_ref),
        stacked_grads(d_ref),
        exp_ref,
        inv_ref[0:1, :],
        dp_ref,
        delta_ref[0:1, :],
        keys,
        keep_ref,
        acc_ref[...],
    )
    for g in range(GROUP):
        dq_ref[:, g * HD : (g + 1) * HD] = acc[:, g * tokens : (g + 1) * tokens].T


def backward_far(q, d_attn, weights, inv, pieces, score_scale):
    total, rows = weights.shape
    half = total // CORES
    return pl.pallas_call(
        functools.partial(backward_far_kernel, score_scale),
        out_shape=(
            jax.ShapeDtypeStruct((HD, rows), F32),
            jax.ShapeDtypeStruct((total, rows), F32),
            jax.ShapeDtypeStruct((8, rows), F32),
            jax.ShapeDtypeStruct((half, 2 * HD), F32),
        ),
        scratch_shapes=[pltpu.VMEM((half, HD), F32), pltpu.VMEM((total, HD), F32)],
        compiler_params=params(),
        cost_estimate=cost(24 * total * rows * HD, 8 * total * rows),
        name="attn_bwd_far",
    )(q, d_attn, weights, inv, *pieces)


def backward_near(q, d_attn, weights, inv, carried, pieces, score_scale):
    total, rows = weights.shape
    half = total // CORES
    return pl.pallas_call(
        functools.partial(backward_near_kernel, score_scale),
        out_shape=(
            jax.ShapeDtypeStruct(q.shape, F32),
            jax.ShapeDtypeStruct((half, 2 * HD), F32),
        ),
        scratch_shapes=[pltpu.VMEM((half, HD), F32)],
        compiler_params=params(),
        cost_estimate=cost(18 * total * rows * HD, 8 * total * rows),
        name="attn_bwd_near",
    )(q, d_attn, weights, inv, *carried, *pieces)


def project_kernel(side, width, w_ref, *refs):
    heads = lax.axis_size("head")
    blocks = ring_pieces(heads)
    pieces = refs[: len(blocks)]
    d_ref = refs[len(blocks)]
    outs = refs[len(blocks) + 1 : -1]
    full = refs[-1]
    tokens, columns = full.shape
    part = columns // heads
    me = lax.axis_index("head")
    for piece, (offset, first, count) in zip(pieces, blocks):
        at = pl.ds(pl.multiple_of(((me + offset) % heads) * part, part), part)
        first, count = first * tokens // 2, count * tokens // 2
        full[first : first + count, at] = piece[...]
    g_hi, g_lo = two(full[...])
    g_both = jnp.concatenate([g_hi, g_lo], axis=0)
    step = 128
    for row in range(0, w_ref.shape[0], step):
        w_hi, w_lo = two(w_ref[row : row + step, :])
        both = mm(w_hi, g_both, NT)
        d_ref[row : row + step, :] = both[:, :tokens] + both[:, tokens:] + mm(w_lo, g_hi, NT)
    if outs:
        seq = lax.axis_index("seq")
        core = seq % CORES
        chip = seq // CORES
        x, y = chip % side, chip // side
        for out, (other_core, j) in zip(outs, column_sets(side)):
            kind = core ^ other_core
            fixed = jnp.where(kind == 0, x, y) ^ j
            moving = jnp.where(kind == 0, y, x)
            for t in range(side):
                i = moving ^ t
                index = jnp.where(kind == 0, i * side + fixed, fixed * side + i)
                at = pl.multiple_of((index * CORES + kind) * width, width)
                out[:, t * width : (t + 1) * width] = full[:, pl.ds(at, width)]


def ring_pieces(heads):
    found = [(0, 0, 2)]
    for step in range(1, heads // 2 + 1):
        if 2 * step == heads:
            found += [(heads - step, 0, 1), (step, 1, 1)]
        else:
            found += [(heads - step, 0, 2), (step, 0, 2)]
    return found


def column_sets(side):
    sets = [(0, 0)]
    for j in range(side):
        if j:
            sets.append((0, j))
        sets.append((1, j))
    return sets


def project(out_weight, pieces, side, width):
    tokens = pieces[0].shape[0]
    rows, columns = out_weight.shape
    shapes = [jax.ShapeDtypeStruct((rows, tokens), F32)]
    if side:
        shapes += [jax.ShapeDtypeStruct((tokens, side * width), F32)] * len(column_sets(side))
    return pl.pallas_call(
        functools.partial(project_kernel, side, width),
        out_shape=tuple(shapes),
        scratch_shapes=[pltpu.VMEM((tokens, columns), F32)],
        compiler_params=params(),
        cost_estimate=cost(24 * tokens * rows * columns, 4 * rows * columns),
        name="project",
    )(out_weight, *pieces)


def weight_kernel(count, *refs):
    attn = refs[:count]
    grad = refs[count : 2 * count]
    outs = refs[2 * count :]
    width = outs[0].shape[1]
    a_hi, a_lo = two(jnp.concatenate([ref[...] for ref in attn], axis=1))
    for t, out in enumerate(outs):
        cut = slice(t * width, (t + 1) * width)
        g_hi, g_lo = two(jnp.concatenate([ref[:, cut] for ref in grad], axis=0))
        out[...] = mm(a_hi, g_lo) + mm(a_lo, g_hi) + mm(a_hi, g_hi)


def weight_grad(attn, grad, side, width):
    rows = attn[0].shape[0]
    return pl.pallas_call(
        functools.partial(weight_kernel, len(attn)),
        out_shape=(jax.ShapeDtypeStruct((rows, width), F32),) * side,
        compiler_params=params(),
        cost_estimate=cost(2 * rows * rows * width * side, 8 * rows * width * side),
        name="weight_grad",
    )(*attn, *grad)


def body(queries, keys, values, grad_out, out_weight):
    tokens = queries.shape[0]
    seq = lax.axis_size("seq")
    heads = lax.axis_size("head")
    chips = seq // CORES
    total = seq * tokens
    width = out_weight.shape[1] // seq
    score_scale = 1.0 / math.sqrt(HD)
    side = math.isqrt(chips)
    exchange = side * side == chips and width % 128 == 0

    def swap(block):
        return lax.ppermute(block, "seq", [(i, i ^ 1) for i in range(seq)])

    def to_chip(block, j):
        return lax.ppermute(block, "seq", [(i, i ^ (CORES * j)) for i in range(seq)])

    def along(block, step):
        return lax.ppermute(block, "head", [(i, (i + step) % heads) for i in range(heads)])

    upper = tokens // 2
    grad_pieces = [grad_out]
    right = left = grad_out
    for step in range(1, heads // 2 + 1):
        if 2 * step == heads:
            right = along(right[:upper], 1)
            left = along(left[upper:], -1)
            grad_pieces += [right, left]
        else:
            right = along(right, 1)
            left = along(left, -1)
            grad_pieces += [right, left]

    own = jnp.concatenate([keys, values], axis=1)
    same = [own]
    for j in range(1, chips):
        same.append(to_chip(own, j))
    pieces = same + [swap(jnp.concatenate(same, axis=0))]

    attn, weights, inv = forward(queries, pieces, total, score_scale)
    d_attn, *column = project(out_weight, grad_pieces, side if exchange else 0, width)

    if exchange:

        def routes(cross, j):
            found = []
            for i in range(seq):
                core, chip = i % CORES, i // CORES
                kind = core ^ cross
                x, y = chip % side, chip // side
                if kind == 0:
                    x ^= j
                else:
                    y ^= j
                found.append((i, (y * side + x) * CORES + kind))
            return found

        sets = column_sets(side)
        moved_grad, moved_attn = [column[0]], [attn]
        for i in range(1, len(sets)):
            moved_attn.append(lax.ppermute(attn, "seq", routes(*sets[i])))
            moved_grad.append(lax.ppermute(column[i], "seq", routes(*sets[i])))
        partial = weight_grad(moved_attn, moved_grad, side, width)

        def final_routes(t):
            found = []
            for i in range(seq):
                core, chip = i % CORES, i // CORES
                x, y = chip % side, chip // side
                if core == 0:
                    y ^= t
                else:
                    x ^= t
                found.append((i, (y * side + x) * CORES + core))
            return found

        grad_wo = partial[0]
        for t in range(1, side):
            moved = lax.ppermute(partial[t], "seq", final_routes(t))
            grad_wo = grad_wo + moved
    else:
        grad_full = lax.all_gather(grad_out, "head", axis=1, tiled=True)
        grad_wo = lax.psum_scatter(
            jnp.dot(grad_full.T, attn.T, precision=lax.Precision.HIGHEST),
            "seq",
            scatter_dimension=0,
            tiled=True,
        ).T

    *carried, send = backward_far(queries, d_attn, weights, inv, pieces, score_scale)
    swapped = swap(send)
    grad_q, keep = backward_near(queries, d_attn, weights, inv, carried, pieces[:-1], score_scale)
    summed = (keep + swapped).reshape(chips, tokens, 2 * HD)
    grad_kv = summed[0]
    for j in range(1, chips):
        moved = to_chip(summed[j], j)
        grad_kv = grad_kv + moved
    return (grad_q, grad_kv[:, :HD], grad_kv[:, HD:], grad_wo)


def solution(mesh):
    in_specs = (
        P("seq", "head"),
        P("seq", "head"),
        P("seq", "head"),
        P("seq", "head"),
        P("head", None),
    )
    out_specs = (P("seq", "head"), P("seq", "head"), P("seq", "head"), P("head", "seq"))
    return jax.shard_map(
        body,
        mesh=mesh,
        in_specs=in_specs,
        out_specs=out_specs,
        check_vma=False,
    )
```

profile of v0, /device:TPU:0, one launch (start us, length us, event | category | flops | bytes accessed | tf_op | source)
XLA Modules:
  0.0 74.2 jit_solution(8017184585956764801)
XLA Ops:
  2.3 3.9 %collective-permute-start.6 = (f32[128,256]{1,0:T(8,128)S(1)}, f32[128,256]{1,0:T(8,128)S(1)}, u32[]{:S(2)}, u32[]{:S(2)}) collective-permute-start(f32[128,256]{1,0:T(8,128)S(1)} %constant_dynamic-update-slice_fusion.refs_0_), channel_id=1, source_target_pairs={{0,24},{4,28},{8,16},{12,20},{16,8},{20,12},{24,0},{28,4},{1,25},{... | collective-permute-start | bytes 393224 | tf_op jit(solution)/shard_map/ppermute | solution.py:369
  6.9 2.0 %collective-permute-start = (f32[128,512]{1,0:T(8,128)}, f32[128,512]{1,0:T(8,128)S(1)}, u32[]{:S(2)}, u32[]{:S(2)}) collective-permute-start(f32[128,512]{1,0:T(8,128)} %refs_0_.1), channel_id=1, source_target_pairs={{0,1},{1,2},{2,3},{3,0},{4,5},{5,6},{6,7},{7,4},{8,9},{9,10},{10,1... | collective-permute-start | bytes 786440 | tf_op jit(solution)/shard_map/ppermute | solution.py:372
  8.9 2.0 %collective-permute-start.1 = (f32[128,512]{1,0:T(8,128)}, f32[128,512]{1,0:T(8,128)S(1)}, u32[]{:S(2)}, u32[]{:S(2)}) collective-permute-start(f32[128,512]{1,0:T(8,128)} %refs_0_.1), channel_id=1, source_target_pairs={{0,3},{1,0},{2,1},{3,2},{4,7},{5,4},{6,5},{7,6},{8,11},{9,8},{10,9... | collective-permute-start | bytes 786440 | tf_op jit(solution)/shard_map/ppermute | solution.py:372
  10.9 1.7 %collective-permute-done.5.refs_2_ = f32[128,256]{1,0:T(8,128)S(1)} collective-permute-done((f32[128,256]{1,0:T(8,128)S(1)}, f32[128,256]{1,0:T(8,128)S(1)}, u32[]{:S(2)}, u32[]{:S(2)}) %collective-permute-start.5) | collective-permute-done | bytes 131104 | tf_op jit(solution)/shard_map/ppermute | solution.py:369
  12.9 5.4 %collective-permute-done.refs_1_ = f32[128,512]{1,0:T(8,128)S(1)} collective-permute-done((f32[128,512]{1,0:T(8,128)}, f32[128,512]{1,0:T(8,128)S(1)}, u32[]{:S(2)}, u32[]{:S(2)}) %collective-permute-start) | collective-permute-done | bytes 262176 | tf_op jit(solution)/shard_map/ppermute | solution.py:372
  19.5 3.2 %collective-permute-done.1.refs_2_ = f32[128,512]{1,0:T(8,128)S(1)} collective-permute-done((f32[128,512]{1,0:T(8,128)}, f32[128,512]{1,0:T(8,128)S(1)}, u32[]{:S(2)}, u32[]{:S(2)}) %collective-permute-start.1) | collective-permute-done | bytes 262176 | tf_op jit(solution)/shard_map/ppermute | solution.py:372
  22.7 2.5 %collective-permute-start.3 = (f32[64,512]{1,0:T(8,128)S(1)}, f32[64,512]{1,0:T(8,128)S(1)}, u32[]{:S(2)}, u32[]{:S(2)}) collective-permute-start(f32[64,512]{1,0:T(8,128)S(1)} %slice.37), channel_id=1, source_target_pairs={{0,3},{1,0},{2,1},{3,2},{4,7},{5,4},{6,5},{7,6},{8,11},{9,8},{10,9... | collective-permute-start | bytes 393224 | tf_op jit(solution)/shard_map/ppermute | solution.py:372
  25.2 1.7 %collective-permute-done.2.refs_3_ = f32[64,512]{1,0:T(8,128)S(1)} collective-permute-done((f32[64,512]{1,0:T(8,128)S(1)}, f32[64,512]{1,0:T(8,128)S(1)}, u32[]{:S(2)}, u32[]{:S(2)}) %collective-permute-start.2) | collective-permute-done | bytes 131104 | tf_op jit(solution)/shard_map/ppermute | solution.py:372
  26.9 1.9 %collective-permute-done.3.refs_4_ = f32[64,512]{1,0:T(8,128)S(1)} collective-permute-done((f32[64,512]{1,0:T(8,128)S(1)}, f32[64,512]{1,0:T(8,128)S(1)}, u32[]{:S(2)}, u32[]{:S(2)}) %collective-permute-start.3) | collective-permute-done | bytes 131104 | tf_op jit(solution)/shard_map/ppermute | solution.py:372
  29.8 4.3 %project.1 = (f32[512,128]{1,0:T(8,128)S(1)}, f32[128,512]{1,0:T(8,128)S(1)}, f32[128,512]{1,0:T(8,128)S(1)}, f32[128,512]{1,0:T(8,128)S(1)}, f32[128,512]{1,0:T(8,128)S(1)}) custom-call(f32[512,2048]{1,0:T(8,128)} %w_ref.1, f32[128,512]{1,0:T(8,128)S(1)} %copy-done.3, f32[128,512]{1,0:T(8,128)S(1)} %collective-permute-done.refs_1_, ...), custom_call_target="tpu_custom_call" | custom-call | flops 3221225472 | bytes 4194304 | tf_op jit(solution)/shard_map/project/pallas_call | solution.py:321
  34.1 4.5 %attn_fwd.1 = (f32[512,128]{1,0:T(8,128)S(1)}, f32[1024,512]{1,0:T(8,128)S(1)}, f32[8,512]{1,0:T(8,128)S(1)}) custom-call(f32[128,512]{1,0:T(8,128)S(1)} %copy-done.2, f32[128,256]{1,0:T(8,128)S(1)} %constant_dynamic-update-slice_fusion.refs_0_, f32[128,256]{1,0:T(8,128)S(1)} %collective-permute-done.4.refs_1_, ...), custom_call_target="tpu_custom_call" | custom-call | flops 2415919104 | bytes 4194304 | tf_op jit(solution)/shard_map/attn_fwd/pallas_call | solution.py:111
  38.6 1.3 %copy-done = f32[1024,512]{1,0:T(8,128)} copy-done((f32[1024,512]{1,0:T(8,128)}, f32[1024,512]{1,0:T(8,128)S(1)}, u32[]{:S(2)}) %copy-start) | copy-done | bytes 2097176
  40.0 4.7 %attn_bwd_far.1 = (f32[128,512]{1,0:T(8,128)S(1)}, f32[1024,512]{1,0:T(8,128)S(1)}, f32[8,512]{1,0:T(8,128)S(1)}, f32[512,256]{1,0:T(8,128)S(1)}) custom-call(f32[128,512]{1,0:T(8,128)S(1)} %copy-done.2, f32[512,128]{1,0:T(8,128)S(1)} %get-tuple-element.20.d_ref, f32[1024,512]{1,0:T(8,128)} %copy-done, f32[8,512]{1,0:T(8,128)S(1)} %get-tuple-element.22.inv_ref, ...), custom_call_target="tpu_custom_call" | custom-call | flops 1610612736 | bytes 4194304 | tf_op jit(solution)/shard_map/attn_bwd_far/pallas_call | solution.py:228
  45.3 1.4 %collective-permute-start.16 = (f32[128,512]{1,0:T(8,128)S(1)}, f32[128,512]{1,0:T(8,128)S(1)}, u32[]{:S(2)}, u32[]{:S(2)}) collective-permute-start(f32[128,512]{1,0:T(8,128)S(1)} %get-tuple-element.32), channel_id=1, source_target_pairs={{0,8},{4,20},{8,0},{12,28},{16,24},{20,4},{24,16},{28,12},{1,9},{5... | collective-permute-start | bytes 786440 | tf_op jit(solution)/shard_map/ppermute | solution.py:415
  46.7 1.9 %collective-permute-start.14 = (f32[512,128]{1,0:T(8,128)S(1)}, f32[512,128]{1,0:T(8,128)S(1)}, u32[]{:S(2)}, u32[]{:S(2)}) collective-permute-start(f32[512,128]{1,0:T(8,128)S(1)} %get-tuple-element.29.refs_0_), channel_id=1, source_target_pairs={{0,20},{4,8},{8,28},{12,0},{16,4},{20,24},{24,12},{28,16},{1,21},{... | collective-permute-start | bytes 786440 | tf_op jit(solution)/shard_map/ppermute | solution.py:414
  48.6 2.6 %attn_bwd_near.1 = (f32[128,512]{1,0:T(8,128)}, f32[512,256]{1,0:T(8,128)S(1)}) custom-call(f32[128,512]{1,0:T(8,128)S(1)} %copy-done.2, f32[512,128]{1,0:T(8,128)S(1)} %get-tuple-element.20.d_ref, f32[1024,512]{1,0:T(8,128)S(1)} %copy-done.1, f32[8,512]{1,0:T(8,128)S(1)} %get-tuple-element.22.inv_ref, f32[128,512]{1,0:T(8,128)S(1)} %get-tuple-element.23.acc_ref, ...), custom_call_target="tpu_custom_call" | custom-call | flops 1207959552 | bytes 4194304 | tf_op jit(solution)/shard_map/attn_bwd_near/pallas_call | solution.py:246
  51.1 1.8 %collective-permute-start.13 = (f32[512,128]{1,0:T(8,128)S(1)}, f32[512,128]{1,0:T(8,128)S(1)}, u32[]{:S(2)}, u32[]{:S(2)}) collective-permute-start(f32[512,128]{1,0:T(8,128)S(1)} %get-tuple-element.29.refs_0_), channel_id=1, source_target_pairs={{0,8},{4,20},{8,0},{12,28},{16,24},{20,4},{24,16},{28,12},{1,9},{5... | collective-permute-start | bytes 786440 | tf_op jit(solution)/shard_map/ppermute | solution.py:414
  53.7 2.2 %collective-permute-start.9 = (f32[128,256]{1,0:T(8,128)S(1)}, f32[128,256]{1,0:T(8,128)S(1)}, u32[]{:S(2)}, u32[]{:S(2)}) collective-permute-start(f32[128,256]{1,0:T(8,128)S(1)} %get-tuple-element.36), channel_id=1, source_target_pairs={{0,8},{4,12},{8,0},{12,4},{16,24},{20,28},{24,16},{28,20},{1,9},{5... | collective-permute-start | bytes 393224 | tf_op jit(solution)/shard_map/ppermute | solution.py:369
  55.8 1.4 %collective-permute-start.11 = (f32[128,256]{1,0:T(8,128)S(1)}, f32[128,256]{1,0:T(8,128)S(1)}, u32[]{:S(2)}, u32[]{:S(2)}) collective-permute-start(f32[128,256]{1,0:T(8,128)S(1)} %get-tuple-element.37), channel_id=1, source_target_pairs={{0,24},{4,28},{8,16},{12,20},{16,8},{20,12},{24,0},{28,4},{1,25},{... | collective-permute-start | bytes 393224 | tf_op jit(solution)/shard_map/ppermute | solution.py:369
  57.2 2.6 %collective-permute-done.14.refs_3_ = f32[512,128]{1,0:T(8,128)S(1)} collective-permute-done((f32[512,128]{1,0:T(8,128)S(1)}, f32[512,128]{1,0:T(8,128)S(1)}, u32[]{:S(2)}, u32[]{:S(2)}) %collective-permute-start.14) | collective-permute-done | bytes 262176 | tf_op jit(solution)/shard_map/ppermute | solution.py:414
  59.9 2.6 %collective-permute-start.10 = (f32[128,256]{1,0:T(8,128)S(1)}, f32[128,256]{1,0:T(8,128)S(1)}, u32[]{:S(2)}, u32[]{:S(2)}) collective-permute-start(f32[128,256]{1,0:T(8,128)S(1)} %get-tuple-element.38), channel_id=1, source_target_pairs={{0,16},{4,20},{8,24},{12,28},{16,0},{20,4},{24,8},{28,12},{1,17},{... | collective-permute-start | bytes 393224 | tf_op jit(solution)/shard_map/ppermute | solution.py:369
  63.5 2.5 %collective-permute-done.11 = f32[128,256]{1,0:T(8,128)S(1)} collective-permute-done((f32[128,256]{1,0:T(8,128)S(1)}, f32[128,256]{1,0:T(8,128)S(1)}, u32[]{:S(2)}, u32[]{:S(2)}) %collective-permute-start.11) | collective-permute-done | bytes 131104 | tf_op jit(solution)/shard_map/ppermute | solution.py:369
  66.0 1.8 %collective-permute-done.10 = f32[128,256]{1,0:T(8,128)S(1)} collective-permute-done((f32[128,256]{1,0:T(8,128)S(1)}, f32[128,256]{1,0:T(8,128)S(1)}, u32[]{:S(2)}, u32[]{:S(2)}) %collective-permute-start.10) | collective-permute-done | bytes 131104 | tf_op jit(solution)/shard_map/ppermute | solution.py:369
  68.4 4.9 %collective-permute-done.18 = f32[512,256]{1,0:T(8,128)S(1)} collective-permute-done((f32[512,256]{1,0:T(8,128)S(1)}, f32[512,256]{1,0:T(8,128)S(1)}, u32[]{:S(2)}, u32[]{:S(2)}) %collective-permute-start.18) | collective-permute-done | bytes 524320 | tf_op jit(solution)/shard_map/ppermute | solution.py:432
  (37 shorter events, 8.7 us)
Async XLA Ops:
  2.3 8.6 %collective-permute-start.6 = (f32[128,256]{1,0:T(8,128)S(1)}, f32[128,256]{1,0:T(8,128)S(1)}, u32[]{:S(2)}, u32[]{:S(2)}) collective-permute-start(f32[128,256]{1,0:T(8,128)S(1)} %constant_dynamic-update-slice_fusion.refs_0_), channel_id=1, source_target_pairs={{0,24},{4,28},{8,16},{12,20},{16,8},{20,12},{24,0},{28,4},{1,25},{... | collective-permute-start | bytes 393224 | tf_op jit(solution)/shard_map/ppermute | solution.py:369
  6.2 6.3 %collective-permute-start.5 = (f32[128,256]{1,0:T(8,128)S(1)}, f32[128,256]{1,0:T(8,128)S(1)}, u32[]{:S(2)}, u32[]{:S(2)}) collective-permute-start(f32[128,256]{1,0:T(8,128)S(1)} %constant_dynamic-update-slice_fusion.refs_0_), channel_id=1, source_target_pairs={{0,16},{4,20},{8,24},{12,28},{16,0},{20,4},{24,8},{28,12},{1,17},{... | collective-permute-start | bytes 393224 | tf_op jit(solution)/shard_map/ppermute | solution.py:369
  6.8 6.0 %collective-permute-start.4 = (f32[128,256]{1,0:T(8,128)S(1)}, f32[128,256]{1,0:T(8,128)S(1)}, u32[]{:S(2)}, u32[]{:S(2)}) collective-permute-start(f32[128,256]{1,0:T(8,128)S(1)} %constant_dynamic-update-slice_fusion.refs_0_), channel_id=1, source_target_pairs={{0,8},{4,12},{8,0},{12,4},{16,24},{20,28},{24,16},{28,20},{1,9},{5... | collective-permute-start | bytes 393224 | tf_op jit(solution)/shard_map/ppermute | solution.py:369
  6.9 11.4 %collective-permute-start = (f32[128,512]{1,0:T(8,128)}, f32[128,512]{1,0:T(8,128)S(1)}, u32[]{:S(2)}, u32[]{:S(2)}) collective-permute-start(f32[128,512]{1,0:T(8,128)} %refs_0_.1), channel_id=1, source_target_pairs={{0,1},{1,2},{2,3},{3,0},{4,5},{5,6},{6,7},{7,4},{8,9},{9,10},{10,1... | collective-permute-start | bytes 786440 | tf_op jit(solution)/shard_map/ppermute | solution.py:372
  8.9 13.8 %collective-permute-start.1 = (f32[128,512]{1,0:T(8,128)}, f32[128,512]{1,0:T(8,128)S(1)}, u32[]{:S(2)}, u32[]{:S(2)}) collective-permute-start(f32[128,512]{1,0:T(8,128)} %refs_0_.1), channel_id=1, source_target_pairs={{0,3},{1,0},{2,1},{3,2},{4,7},{5,4},{6,5},{7,6},{8,11},{9,8},{10,9... | collective-permute-start | bytes 786440 | tf_op jit(solution)/shard_map/ppermute | solution.py:372
  12.8 21.2 %collective-permute-start.7 = (f32[512,256]{1,0:T(8,128)S(1)}, f32[512,256]{1,0:T(8,128)S(1)}, u32[]{:S(2)}, u32[]{:S(2)}) collective-permute-start(f32[512,256]{1,0:T(8,128)S(1)} %pad_maximum_fusion), channel_id=1, source_target_pairs={{0,4},{4,0},{8,12},{12,8},{16,20},{20,16},{24,28},{28,24},{1,5},{5... | collective-permute-start | bytes 1572872 | tf_op jit(solution)/shard_map/ppermute | solution.py:366
  18.3 8.6 %collective-permute-start.2 = (f32[64,512]{1,0:T(8,128)S(1)}, f32[64,512]{1,0:T(8,128)S(1)}, u32[]{:S(2)}, u32[]{:S(2)}) collective-permute-start(f32[64,512]{1,0:T(8,128)S(1)} %slice.36), channel_id=1, source_target_pairs={{0,1},{1,2},{2,3},{3,0},{4,5},{5,6},{6,7},{7,4},{8,9},{9,10},{10,1... | collective-permute-start | bytes 393224 | tf_op jit(solution)/shard_map/ppermute | solution.py:372
  22.7 11.4 %copy-start.2 = (f32[128,512]{1,0:T(8,128)S(1)}, f32[128,512]{1,0:T(8,128)}, u32[]{:S(2)}) copy-start(f32[128,512]{1,0:T(8,128)} %q_ref.5) | copy-start | bytes 786436
  22.7 6.1 %collective-permute-start.3 = (f32[64,512]{1,0:T(8,128)S(1)}, f32[64,512]{1,0:T(8,128)S(1)}, u32[]{:S(2)}, u32[]{:S(2)}) collective-permute-start(f32[64,512]{1,0:T(8,128)S(1)} %slice.37), channel_id=1, source_target_pairs={{0,3},{1,0},{2,1},{3,2},{4,7},{5,4},{6,5},{7,6},{8,11},{9,8},{10,9... | collective-permute-start | bytes 393224 | tf_op jit(solution)/shard_map/ppermute | solution.py:372
  28.8 1.0 %copy-start.3 = (f32[128,512]{1,0:T(8,128)S(1)}, f32[128,512]{1,0:T(8,128)}, u32[]{:S(2)}) copy-start(f32[128,512]{1,0:T(8,128)} %refs_0_.1) | copy-start | bytes 786436
  38.6 1.3 %copy-start = (f32[1024,512]{1,0:T(8,128)}, f32[1024,512]{1,0:T(8,128)S(1)}, u32[]{:S(2)}) copy-start(f32[1024,512]{1,0:T(8,128)S(1)} %get-tuple-element.21.exp_ref) | copy-start | bytes 6291460
  40.0 8.6 %copy-start.1 = (f32[1024,512]{1,0:T(8,128)S(1)}, f32[1024,512]{1,0:T(8,128)}, u32[]{:S(2)}) copy-start(f32[1024,512]{1,0:T(8,128)} %copy-done) | copy-start | bytes 6291460
  44.7 6.4 %collective-permute-start.8 = (f32[512,256]{1,0:T(8,128)S(1)}, f32[512,256]{1,0:T(8,128)S(1)}, u32[]{:S(2)}, u32[]{:S(2)}) collective-permute-start(f32[512,256]{1,0:T(8,128)S(1)} %get-tuple-element.28), channel_id=1, source_target_pairs={{0,4},{4,0},{8,12},{12,8},{16,20},{20,16},{24,28},{28,24},{1,5},{5... | collective-permute-start | bytes 1572872 | tf_op jit(solution)/shard_map/ppermute | solution.py:366
  44.8 8.2 %collective-permute-start.15 = (f32[128,512]{1,0:T(8,128)S(1)}, f32[128,512]{1,0:T(8,128)S(1)}, u32[]{:S(2)}, u32[]{:S(2)}) collective-permute-start(f32[128,512]{1,0:T(8,128)S(1)} %get-tuple-element.31), channel_id=1, source_target_pairs={{0,4},{4,0},{8,12},{12,8},{16,20},{20,16},{24,28},{28,24},{1,5},{5... | collective-permute-start | bytes 786440 | tf_op jit(solution)/shard_map/ppermute | solution.py:415
  45.3 8.4 %collective-permute-start.16 = (f32[128,512]{1,0:T(8,128)S(1)}, f32[128,512]{1,0:T(8,128)S(1)}, u32[]{:S(2)}, u32[]{:S(2)}) collective-permute-start(f32[128,512]{1,0:T(8,128)S(1)} %get-tuple-element.32), channel_id=1, source_target_pairs={{0,8},{4,20},{8,0},{12,28},{16,24},{20,4},{24,16},{28,12},{1,9},{5... | collective-permute-start | bytes 786440 | tf_op jit(solution)/shard_map/ppermute | solution.py:415
  46.7 9.1 %collective-permute-start.17 = (f32[128,512]{1,0:T(8,128)S(1)}, f32[128,512]{1,0:T(8,128)S(1)}, u32[]{:S(2)}, u32[]{:S(2)}) collective-permute-start(f32[128,512]{1,0:T(8,128)S(1)} %get-tuple-element.33), channel_id=1, source_target_pairs={{0,20},{4,8},{8,28},{12,0},{16,4},{20,24},{24,12},{28,16},{1,21},{... | collective-permute-start | bytes 786440 | tf_op jit(solution)/shard_map/ppermute | solution.py:415
  46.7 13.1 %collective-permute-start.14 = (f32[512,128]{1,0:T(8,128)S(1)}, f32[512,128]{1,0:T(8,128)S(1)}, u32[]{:S(2)}, u32[]{:S(2)}) collective-permute-start(f32[512,128]{1,0:T(8,128)S(1)} %get-tuple-element.29.refs_0_), channel_id=1, source_target_pairs={{0,20},{4,8},{8,28},{12,0},{16,4},{20,24},{24,12},{28,16},{1,21},{... | collective-permute-start | bytes 786440 | tf_op jit(solution)/shard_map/ppermute | solution.py:414
  51.1 11.3 %collective-permute-start.13 = (f32[512,128]{1,0:T(8,128)S(1)}, f32[512,128]{1,0:T(8,128)S(1)}, u32[]{:S(2)}, u32[]{:S(2)}) collective-permute-start(f32[512,128]{1,0:T(8,128)S(1)} %get-tuple-element.29.refs_0_), channel_id=1, source_target_pairs={{0,8},{4,20},{8,0},{12,28},{16,24},{20,4},{24,16},{28,12},{1,9},{5... | collective-permute-start | bytes 786440 | tf_op jit(solution)/shard_map/ppermute | solution.py:414
  53.0 9.4 %collective-permute-start.12 = (f32[512,128]{1,0:T(8,128)S(1)}, f32[512,128]{1,0:T(8,128)S(1)}, u32[]{:S(2)}, u32[]{:S(2)}) collective-permute-start(f32[512,128]{1,0:T(8,128)S(1)} %get-tuple-element.29.refs_0_), channel_id=1, source_target_pairs={{0,4},{4,0},{8,12},{12,8},{16,20},{20,16},{24,28},{28,24},{1,5},{5... | collective-permute-start | bytes 786440 | tf_op jit(solution)/shard_map/ppermute | solution.py:414
  53.7 9.9 %collective-permute-start.9 = (f32[128,256]{1,0:T(8,128)S(1)}, f32[128,256]{1,0:T(8,128)S(1)}, u32[]{:S(2)}, u32[]{:S(2)}) collective-permute-start(f32[128,256]{1,0:T(8,128)S(1)} %get-tuple-element.36), channel_id=1, source_target_pairs={{0,8},{4,12},{8,0},{12,4},{16,24},{20,28},{24,16},{28,20},{1,9},{5... | collective-permute-start | bytes 393224 | tf_op jit(solution)/shard_map/ppermute | solution.py:369
  55.8 10.2 %collective-permute-start.11 = (f32[128,256]{1,0:T(8,128)S(1)}, f32[128,256]{1,0:T(8,128)S(1)}, u32[]{:S(2)}, u32[]{:S(2)}) collective-permute-start(f32[128,256]{1,0:T(8,128)S(1)} %get-tuple-element.37), channel_id=1, source_target_pairs={{0,24},{4,28},{8,16},{12,20},{16,8},{20,12},{24,0},{28,4},{1,25},{... | collective-permute-start | bytes 393224 | tf_op jit(solution)/shard_map/ppermute | solution.py:369
  59.9 7.9 %collective-permute-start.10 = (f32[128,256]{1,0:T(8,128)S(1)}, f32[128,256]{1,0:T(8,128)S(1)}, u32[]{:S(2)}, u32[]{:S(2)}) collective-permute-start(f32[128,256]{1,0:T(8,128)S(1)} %get-tuple-element.38), channel_id=1, source_target_pairs={{0,16},{4,20},{8,24},{12,28},{16,0},{20,4},{24,8},{28,12},{1,17},{... | collective-permute-start | bytes 393224 | tf_op jit(solution)/shard_map/ppermute | solution.py:369
  63.4 9.9 %collective-permute-start.18 = (f32[512,256]{1,0:T(8,128)S(1)}, f32[512,256]{1,0:T(8,128)S(1)}, u32[]{:S(2)}, u32[]{:S(2)}) collective-permute-start(f32[512,256]{1,0:T(8,128)S(1)} %get-tuple-element.35), channel_id=1, source_target_pairs={{0,16},{4,12},{8,24},{12,4},{16,0},{20,28},{24,8},{28,20},{1,17},{... | collective-permute-start | bytes 1572872 | tf_op jit(solution)/shard_map/ppermute | solution.py:432
where the time goes:
time: 74.5 us; the launch traced here: 74.2 us
  waiting for transfers between devices  26.4 us (35%)
  starting transfers between devices  24.2 us (32%)
  Pallas kernels  17.1 us (23%)
  local copies, waits for them, and re-layouts  4.69 us (6%)
  other arithmetic  1 us (1%)
  between operations  0.78 us (1%)
    ppermute x4, waiting for transfers between devices, along(): lax.ppermute(block, 'head', [(i, (i + step) % heads) for i in range(heads)])  12.2 us
    ppermute x6, starting transfers between devices, to_chip(): return lax.ppermute(block, 'seq', [(i, i ^ CORES * j) for i in range(seq)])  10.7 us
    ppermute x4, starting transfers between devices, along(): lax.ppermute(block, 'head', [(i, (i + step) % heads) for i in range(heads)])  7.67 us
    ppermute x6, waiting for transfers between devices, to_chip(): return lax.ppermute(block, 'seq', [(i, i ^ CORES * j) for i in range(seq)])  6.12 us
    ppermute x1, waiting for transfers between devices, body(): moved = lax.ppermute(partial[t], 'seq', final_routes(t))  4.92 us
    pallas_call x1, Pallas kernels, backward_far(): pl.pallas_call(functools.partial(backward_far_kernel, score_scale), out_s...  4.73 us
    pallas_call x1, Pallas kernels, forward(): pl.pallas_call(functools.partial(forward_kernel, score_scale), out_shape=...  4.54 us
    pallas_call x1, Pallas kernels, project(): pl.pallas_call(functools.partial(project_kernel, side, width), out_shape=...  4.31 us
  transfers between devices with their start and end apart: 19, of which 11 were waited for; matrix products, arithmetic and copies ran while one was open for 1% of the time, Pallas kernels for 11%

commit v1 on v0

--- a/solution.py
+++ b/solution.py
@@ -39,8 +39,8 @@
     return pl.CostEstimate(flops=flops, transcendentals=0, bytes_accessed=size)
 
 
-def params():
-    return pltpu.CompilerParams(vmem_limit_bytes=48 * 1024 * 1024)
+def params(held=0):
+    return pltpu.CompilerParams(vmem_limit_bytes=(12 << 20) + held)
 
 
 def load_blocks(refs, dst, column):
@@ -49,6 +49,27 @@
         count = ref.shape[0]
         dst[row : row + count, :] = ref[:, column : column + HD]
         row += count
+
+
+def pack_kernel(keys_ref, values_ref, out_ref, sem):
+    copies = [
+        pltpu.make_async_copy(ref, out_ref.at[:, i * HD : (i + 1) * HD], sem.at[i])
+        for i, ref in enumerate((keys_ref, values_ref))
+    ]
+    for copy in copies:
+        copy.start()
+    for copy in copies:
+        copy.wait()
+
+
+def pack(keys, values):
+    return pl.pallas_call(
+        pack_kernel,
+        out_shape=jax.ShapeDtypeStruct((keys.shape[0], 2 * HD), F32),
+        in_specs=[pl.BlockSpec(memory_space=pl.ANY)] * 2,
+        scratch_shapes=[pltpu.SemaphoreType.DMA((2,))],
+        name="pack",
+    )(keys, values)
 
 
 def forward_kernel(score_scale, q_ref, *refs):
@@ -120,7 +141,7 @@
             pltpu.VMEM((total, HD), F32),
             pltpu.VMEM((total, rows), F32),
         ],
-        compiler_params=params(),
+        compiler_params=params(12 * total * rows),
         cost_estimate=cost(36 * total * rows * HD, 8 * total * rows),
         name="attn_fwd",
     )(q, *pieces)
@@ -234,7 +255,7 @@
             jax.ShapeDtypeStruct((half, 2 * HD), F32),
         ),
         scratch_shapes=[pltpu.VMEM((half, HD), F32), pltpu.VMEM((total, HD), F32)],
-        compiler_params=params(),
+        compiler_params=params(12 * total * rows),
         cost_estimate=cost(24 * total * rows * HD, 8 * total * rows),
         name="attn_bwd_far",
     )(q, d_attn, weights, inv, *pieces)
@@ -250,34 +271,47 @@
             jax.ShapeDtypeStruct((half, 2 * HD), F32),
         ),
         scratch_shapes=[pltpu.VMEM((half, HD), F32)],
-        compiler_params=params(),
+        compiler_params=params(12 * total * rows),
         cost_estimate=cost(18 * total * rows * HD, 8 * total * rows),
         name="attn_bwd_near",
     )(q, d_attn, weights, inv, *carried, *pieces)
 
 
-def project_kernel(side, width, w_ref, *refs):
-    heads = lax.axis_size("head")
-    blocks = ring_pieces(heads)
-    pieces = refs[: len(blocks)]
-    d_ref = refs[len(blocks)]
-    outs = refs[len(blocks) + 1 : -1]
-    full = refs[-1]
-    tokens, columns = full.shape
-    part = columns // heads
+def project_kernel(new, old, side, width, *refs):
+    refs = list(refs)
+
+    def take(count):
+        taken = refs[:count]
+        del refs[:count]
+        return taken
+
+    (w_ref,) = take(1)
+    fresh = [take(count) for _, count in new]
+    stale = [take(count) for _, count in old] if side else []
+    carried = take(1) if old else []
+    (d_ref,) = take(1)
+    outs = take(len(column_sets(side))) if side else []
+    weights, sem = take(2)
+    rows, tokens = d_ref.shape
+    part = weights.shape[2]
     me = lax.axis_index("head")
-    for piece, (offset, first, count) in zip(pieces, blocks):
-        at = pl.ds(pl.multiple_of(((me + offset) % heads) * part, part), part)
-        first, count = first * tokens // 2, count * tokens // 2
-        full[first : first + count, at] = piece[...]
-    g_hi, g_lo = two(full[...])
-    g_both = jnp.concatenate([g_hi, g_lo], axis=0)
-    step = 128
-    for row in range(0, w_ref.shape[0], step):
-        w_hi, w_lo = two(w_ref[row : row + step, :])
-        both = mm(w_hi, g_both, NT)
-        d_ref[row : row + step, :] = both[:, :tokens] + both[:, tokens:] + mm(w_lo, g_hi, NT)
-    if outs:
+
+    def block(copies):
+        return functools.reduce(jnp.add, [ref[...] for ref in copies])
+
+    def column(offset):
+        return pl.ds(pl.multiple_of((me ^ offset) * part, part), part)
+
+    copies = [
+        pltpu.make_async_copy(w_ref.at[:, column(offset)], weights.at[i], sem.at[i])
+        for i, (offset, _) in enumerate(new)
+    ]
+    for copy in copies:
+        copy.start()
+    if side:
+        (full,) = take(1)
+        for piece, offset in zip(stale + fresh, [o for o, _ in old + new]):
+            full[:, column(offset)] = block(piece)
         seq = lax.axis_index("seq")
         core = seq % CORES
         chip = seq // CORES
@@ -291,16 +325,19 @@
                 index = jnp.where(kind == 0, i * side + fixed, fixed * side + i)
                 at = pl.multiple_of((index * CORES + kind) * width, width)
                 out[:, t * width : (t + 1) * width] = full[:, pl.ds(at, width)]
-
-
-def ring_pieces(heads):
-    found = [(0, 0, 2)]
-    for step in range(1, heads // 2 + 1):
-        if 2 * step == heads:
-            found += [(heads - step, 0, 1), (step, 1, 1)]
-        else:
-            found += [(heads - step, 0, 2), (step, 0, 2)]
-    return found
+    step = rows // 2
+    for i, piece in enumerate(fresh):
+        g_hi, g_lo = two(block(piece))
+        g_both = jnp.concatenate([g_hi, g_lo], axis=0)
+        copies[i].wait()
+        for row in range(0, rows, step):
+            at = slice(row, row + step)
+            w_hi, w_lo = two(weights[i, at, :])
+            both = mm(w_hi, g_both, NT)
+            value = both[:, :tokens] + both[:, tokens:] + mm(w_lo, g_hi, NT)
+            if i or carried:
+                value = value + (d_ref if i else carried[0])[at, :]
+            d_ref[at, :] = value
 
 
 def column_sets(side):
@@ -312,20 +349,38 @@
     return sets
 
 
-def project(out_weight, pieces, side, width):
-    tokens = pieces[0].shape[0]
+def project(out_weight, blocks, new, old, carried, side, width):
+    heads = lax.axis_size("head")
     rows, columns = out_weight.shape
+    tokens = blocks[0][0].shape[0]
+    part = columns // heads
+    offsets = len(new)
     shapes = [jax.ShapeDtypeStruct((rows, tokens), F32)]
+    scratch = [
+        pltpu.VMEM((offsets, rows, part), F32),
+        pltpu.SemaphoreType.DMA((offsets,)),
+    ]
+    operands = [copy for d in new for copy in blocks[d]]
     if side:
         shapes += [jax.ShapeDtypeStruct((tokens, side * width), F32)] * len(column_sets(side))
+        scratch.append(pltpu.VMEM((tokens, columns), F32))
+        operands += [copy for d in old for copy in blocks[d]]
+    if old:
+        operands.append(carried)
+
+    def counted(distances):
+        return [(d, len(blocks[d])) for d in distances]
+
     return pl.pallas_call(
-        functools.partial(project_kernel, side, width),
+        functools.partial(project_kernel, counted(new), counted(old), side, width),
         out_shape=tuple(shapes),
-        scratch_shapes=[pltpu.VMEM((tokens, columns), F32)],
+        in_specs=[pl.BlockSpec(memory_space=pltpu.HBM)]
+        + [pl.BlockSpec(memory_space=pltpu.VMEM)] * len(operands),
+        scratch_shapes=scratch,
         compiler_params=params(),
-        cost_estimate=cost(24 * tokens * rows * columns, 4 * rows * columns),
+        cost_estimate=cost(24 * tokens * rows * part * offsets, 4 * rows * part * offsets),
         name="project",
-    )(out_weight, *pieces)
+    )(out_weight, *operands)
 
 
 def weight_kernel(count, *refs):
@@ -368,30 +423,41 @@
     def to_chip(block, j):
         return lax.ppermute(block, "seq", [(i, i ^ (CORES * j)) for i in range(seq)])
 
-    def along(block, step):
-        return lax.ppermute(block, "head", [(i, (i + step) % heads) for i in range(heads)])
-
-    upper = tokens // 2
-    grad_pieces = [grad_out]
-    right = left = grad_out
-    for step in range(1, heads // 2 + 1):
-        if 2 * step == heads:
-            right = along(right[:upper], 1)
-            left = along(left[upper:], -1)
-            grad_pieces += [right, left]
-        else:
-            right = along(right, 1)
-            left = along(left, -1)
-            grad_pieces += [right, left]
-
-    own = jnp.concatenate([keys, values], axis=1)
+    def along(block, route):
+        return lax.ppermute(block, "head", route)
+
+    by_distance = {0: (grad_out,)}
+    for d in range(1, heads):
+        if d + 1 < heads or heads != GROUP:
+            by_distance[d] = (along(grad_out, [(i, i ^ d) for i in range(heads)]),)
+    if heads == GROUP:
+        middle = along(grad_out, [(1, 2), (2, 1)])
+        ends = along(by_distance[2][0], [(1, 0), (2, 3)])
+        by_distance[3] = middle, ends
+
+    own = pack(keys, values)
     same = [own]
     for j in range(1, chips):
         same.append(to_chip(own, j))
     pieces = same + [swap(jnp.concatenate(same, axis=0))]
 
     attn, weights, inv = forward(queries, pieces, total, score_scale)
-    d_attn, *column = project(out_weight, grad_pieces, side if exchange else 0, width)
+    d_attn, column = None, ()
+    seen = []
+    for fresh in ([0], [1], list(range(2, heads))):
+        final = fresh[-1] == heads - 1
+        d_attn, *column = project(
+            out_weight,
+            by_distance,
+            fresh,
+            seen,
+            d_attn,
+            side if exchange and final else 0,
+            width,
+        )
+        seen = seen + fresh
+        if final:
+            break
 
     if exchange:
 

time: 74.5 us -> 71.3 us (0.957)
  starting transfers between devices: 24.2 us -> 22.4 us
  Pallas kernels: 17.1 us -> 15.6 us
  other arithmetic: 1 us -> 1.9 us
  local copies, waits for them, and re-layouts: 4.69 us -> 3.83 us
    ppermute x4, waiting for transfers between devices: 12.2 us -> 10.2 us  [along(): return lax.ppermute(block, 'head', route)]
    pallas_call x1, Pallas kernels: 4.73 us -> 3 us  [backward_far(): pl.pallas_call(functools.partial(backward_far_kernel, score_scale), out_s...]
    ppermute x6, waiting for transfers between devices: 6.12 us -> 7.51 us  [to_chip(): return lax.ppermute(block, 'seq', [(i, i ^ CORES * j) for i in range(seq)])]
    ppermute x4, starting transfers between devices: 7.67 us -> 6.58 us  [along(): return lax.ppermute(block, 'head', route)]
    concatenate x1, other arithmetic: 0.03 us -> 0.94 us  [body(): pieces = same + [swap(jnp.concatenate(same, axis=0))]]
    concatenate x1 -> x0, local copies, waits for them, and re-layouts: 0.84 us -> none  [body(): own = jnp.concatenate([keys, values], axis=1)]
    pallas_call x1 -> x4, Pallas kernels: 4.31 us -> 4.53 us  [the longest x3 2.98 us: project(): pl.pallas_call(functools.partial(project_kernel, counted(new), counted(ol...]
    unnamed x9 -> x8, local copies, waits for them, and re-layouts: 3.14 us -> 3.15 us
  transfers between devices with their start and end apart: 19 -> 19, of which waited for: 11 -> 11; matrix products, arithmetic and copies ran while one was open for 1% -> 2% of each run, Pallas kernels for 11% -> 9%
where the time goes in v1:
time: 71.3 us; the launch traced here: 71 us
  waiting for transfers between devices  26.5 us (37%)
  starting transfers between devices  22.4 us (31%)
  Pallas kernels  15.6 us (22%)
  local copies, waits for them, and re-layouts  3.83 us (5%)
  other arithmetic  1.9 us (3%)
  between operations  0.83 us (1%)
    ppermute x6, starting transfers between devices, to_chip(): return lax.ppermute(block, 'seq', [(i, i ^ CORES * j) for i in range(seq)])  10.5 us
    ppermute x4, waiting for transfers between devices, along(): return lax.ppermute(block, 'head', route)  10.2 us
    ppermute x6, waiting for transfers between devices, to_chip(): return lax.ppermute(block, 'seq', [(i, i ^ CORES * j) for i in range(seq)])  7.51 us
    ppermute x4, starting transfers between devices, along(): return lax.ppermute(block, 'head', route)  6.58 us
    ppermute x1, waiting for transfers between devices, body(): moved = lax.ppermute(partial[t], 'seq', final_routes(t))  4.92 us
    pallas_call x1, Pallas kernels, forward(): pl.pallas_call(functools.partial(forward_kernel, score_scale), out_shape=...  4.54 us
    unnamed x8, local copies, waits for them, and re-layouts  3.15 us
    ppermute x3, starting transfers between devices, body(): moved_attn.append(lax.ppermute(attn, 'seq', routes(*sets[i])))  3.06 us
  transfers between devices with their start and end apart: 19, of which 11 were waited for; matrix products, arithmetic and copies ran while one was open for 2% of the time, Pallas kernels for 9%

profile of v1, /device:TPU:0, one launch (start us, length us, event | category | flops | bytes accessed | tf_op | source)
XLA Modules:
  0.0 71.0 jit_solution(15116692809990048814)
XLA Ops:
  0.6 1.5 %pack.1.refs_0_ = f32[128,256]{1,0:T(8,128)} custom-call(f32[128,128]{1,0:T(8,128)} %keys_ref.1, f32[128,128]{1,0:T(8,128)} %values_ref.1), custom_call_target="tpu_custom_call" | custom-call | tf_op jit(solution)/shard_map/pack/pallas_call | solution.py:66
  2.2 4.0 %collective-permute-start.6 = (f32[128,256]{1,0:T(8,128)}, f32[128,256]{1,0:T(8,128)S(1)}, u32[]{:S(2)}, u32[]{:S(2)}) collective-permute-start(f32[128,256]{1,0:T(8,128)} %pack.1.refs_0_), channel_id=1, source_target_pairs={{0,24},{4,28},{8,16},{12,20},{16,8},{20,12},{24,0},{28,4},{1,25},{... | collective-permute-start | bytes 393224 | tf_op jit(solution)/shard_map/ppermute | solution.py:424
  6.8 3.0 %collective-permute-start = (f32[128,512]{1,0:T(8,128)}, f32[128,512]{1,0:T(8,128)S(1)}, u32[]{:S(2)}, u32[]{:S(2)}) collective-permute-start(f32[128,512]{1,0:T(8,128)} %refs_4_.1), channel_id=1, source_target_pairs={{0,2},{1,3},{2,0},{3,1},{4,6},{5,7},{6,4},{7,5},{8,10},{9,11},{10,... | collective-permute-start | bytes 786440 | tf_op jit(solution)/shard_map/ppermute | solution.py:427
  10.4 2.3 %collective-permute-done.5.refs_2_ = f32[128,256]{1,0:T(8,128)S(1)} collective-permute-done((f32[128,256]{1,0:T(8,128)}, f32[128,256]{1,0:T(8,128)S(1)}, u32[]{:S(2)}, u32[]{:S(2)}) %collective-permute-start.5) | collective-permute-done | bytes 131104 | tf_op jit(solution)/shard_map/ppermute | solution.py:424
  14.0 1.6 %collective-permute-start.3 = (f32[128,512]{1,0:T(8,128)}, f32[128,512]{1,0:T(8,128)S(1)}, u32[]{:S(2)}, u32[]{:S(2)}) collective-permute-start(f32[128,512]{1,0:T(8,128)} %refs_4_.1), channel_id=1, source_target_pairs={{0,1},{1,0},{2,3},{3,2},{4,5},{5,4},{6,7},{7,6},{8,9},{9,8},{10,11... | collective-permute-start | bytes 786440 | tf_op jit(solution)/shard_map/ppermute | solution.py:427
  16.3 4.9 %collective-permute-done.refs_1_ = f32[128,512]{1,0:T(8,128)S(1)} collective-permute-done((f32[128,512]{1,0:T(8,128)}, f32[128,512]{1,0:T(8,128)S(1)}, u32[]{:S(2)}, u32[]{:S(2)}) %collective-permute-start) | collective-permute-done | bytes 262176 | tf_op jit(solution)/shard_map/ppermute | solution.py:427
  21.2 1.3 %collective-permute-start.2 = (f32[128,512]{1,0:T(8,128)S(1)}, f32[128,512]{1,0:T(8,128)S(1)}, u32[]{:S(2)}, u32[]{:S(2)}) collective-permute-start(f32[128,512]{1,0:T(8,128)S(1)} %collective-permute-done.refs_1_), channel_id=1, source_target_pairs={{1,0},{2,3},{5,4},{6,7},{9,8},{10,11},{13,12},{14,15},{17,16},{18,... | collective-permute-start | bytes 786440 | tf_op jit(solution)/shard_map/ppermute | solution.py:427
  22.5 2.2 %copy-done = f32[512,2048]{1,0:T(8,128)S(1)} copy-done((f32[512,2048]{1,0:T(8,128)S(1)}, f32[512,2048]{1,0:T(8,128)}, u32[]{:S(2)}) %copy-start) | copy-done | bytes 4194328
  27.5 4.8 %collective-permute-done.2.refs_3_ = f32[128,512]{1,0:T(8,128)S(1)} collective-permute-done((f32[128,512]{1,0:T(8,128)S(1)}, f32[128,512]{1,0:T(8,128)S(1)}, u32[]{:S(2)}, u32[]{:S(2)}) %collective-permute-start.2) | collective-permute-done | bytes 262176 | tf_op jit(solution)/shard_map/ppermute | solution.py:427
  32.3 1.6 %project.5 = (f32[512,128]{1,0:T(8,128)S(1)}, f32[128,512]{1,0:T(8,128)S(1)}, f32[128,512]{1,0:T(8,128)S(1)}, f32[128,512]{1,0:T(8,128)S(1)}, f32[128,512]{1,0:T(8,128)S(1)}) custom-call(f32[512,2048]{1,0:T(8,128)S(1)} %copy-done, f32[128,512]{1,0:T(8,128)S(1)} %collective-permute-done.refs_1_, f32[128,512]{1,0:T(8,128)S(1)} %collective-permute-done.1.refs_2_, ...), custom_call_target="tpu_custom_call" | custom-call | flops 1610612736 | bytes 2097152 | tf_op jit(solution)/shard_map/project/pallas_call | solution.py:374
  33.9 4.5 %attn_fwd.1 = (f32[512,128]{1,0:T(8,128)S(1)}, f32[1024,512]{1,0:T(8,128)S(1)}, f32[8,512]{1,0:T(8,128)S(1)}) custom-call(f32[128,512]{1,0:T(8,128)S(1)} %copy-done.3, f32[128,256]{1,0:T(8,128)S(1)} %copy-done.1, f32[128,256]{1,0:T(8,128)S(1)} %collective-permute-done.4.refs_1_, f32[128,256]{1,0:T(8,128)S(1)} %collective-permute-done.5.refs_2_, ...), custom_call_target="tpu_custom_call" | custom-call | flops 2415919104 | bytes 4194304 | tf_op jit(solution)/shard_map/attn_fwd/pallas_call | solution.py:132
  38.5 3.0 %attn_bwd_far.1 = (f32[128,512]{1,0:T(8,128)S(1)}, f32[1024,512]{1,0:T(8,128)S(1)}, f32[8,512]{1,0:T(8,128)S(1)}, f32[512,256]{1,0:T(8,128)S(1)}) custom-call(f32[128,512]{1,0:T(8,128)S(1)} %copy-done.3, f32[512,128]{1,0:T(8,128)S(1)} %get-tuple-element.20.d_ref, f32[1024,512]{1,0:T(8,128)S(1)} %get-tuple-element.21.exp_ref, ...), custom_call_target="tpu_custom_call" | custom-call | flops 1610612736 | bytes 4194304 | tf_op jit(solution)/shard_map/attn_bwd_far/pallas_call | solution.py:249
  42.1 1.5 %collective-permute-start.16 = (f32[128,512]{1,0:T(8,128)S(1)}, f32[128,512]{1,0:T(8,128)S(1)}, u32[]{:S(2)}, u32[]{:S(2)}) collective-permute-start(f32[128,512]{1,0:T(8,128)S(1)} %get-tuple-element.32), channel_id=1, source_target_pairs={{0,8},{4,20},{8,0},{12,28},{16,24},{20,4},{24,16},{28,12},{1,9},{5... | collective-permute-start | bytes 786440 | tf_op jit(solution)/shard_map/ppermute | solution.py:481
  43.6 1.8 %collective-permute-start.14 = (f32[512,128]{1,0:T(8,128)S(1)}, f32[512,128]{1,0:T(8,128)S(1)}, u32[]{:S(2)}, u32[]{:S(2)}) collective-permute-start(f32[512,128]{1,0:T(8,128)S(1)} %get-tuple-element.29.refs_0_), channel_id=1, source_target_pairs={{0,20},{4,8},{8,28},{12,0},{16,4},{20,24},{24,12},{28,16},{1,21},{... | collective-permute-start | bytes 786440 | tf_op jit(solution)/shard_map/ppermute | solution.py:480
  45.4 2.6 %attn_bwd_near.1 = (f32[128,512]{1,0:T(8,128)}, f32[512,256]{1,0:T(8,128)S(1)}) custom-call(f32[128,512]{1,0:T(8,128)S(1)} %copy-done.3, f32[512,128]{1,0:T(8,128)S(1)} %get-tuple-element.20.d_ref, f32[1024,512]{1,0:T(8,128)S(1)} %get-tuple-element.21.exp_ref, f32[8,512]{1,0:T(8,128)S(1)} %get-tuple-element.22.inv_ref, ...), custom_call_target="tpu_custom_call" | custom-call | flops 1207959552 | bytes 4194304 | tf_op jit(solution)/shard_map/attn_bwd_near/pallas_call | solution.py:267
  48.0 1.2 %collective-permute-start.13 = (f32[512,128]{1,0:T(8,128)S(1)}, f32[512,128]{1,0:T(8,128)S(1)}, u32[]{:S(2)}, u32[]{:S(2)}) collective-permute-start(f32[512,128]{1,0:T(8,128)S(1)} %get-tuple-element.29.refs_0_), channel_id=1, source_target_pairs={{0,8},{4,20},{8,0},{12,28},{16,24},{20,4},{24,16},{28,12},{1,9},{5... | collective-permute-start | bytes 786440 | tf_op jit(solution)/shard_map/ppermute | solution.py:480
  49.4 0.9 %collective-permute-done.16.refs_6_ = f32[128,512]{1,0:T(8,128)S(1)} collective-permute-done((f32[128,512]{1,0:T(8,128)S(1)}, f32[128,512]{1,0:T(8,128)S(1)}, u32[]{:S(2)}, u32[]{:S(2)}) %collective-permute-start.16) | collective-permute-done | bytes 262176 | tf_op jit(solution)/shard_map/ppermute | solution.py:481
  50.3 2.5 %collective-permute-start.9 = (f32[128,256]{1,0:T(8,128)S(1)}, f32[128,256]{1,0:T(8,128)S(1)}, u32[]{:S(2)}, u32[]{:S(2)}) collective-permute-start(f32[128,256]{1,0:T(8,128)S(1)} %get-tuple-element.36), channel_id=1, source_target_pairs={{0,8},{4,12},{8,0},{12,4},{16,24},{20,28},{24,16},{28,20},{1,9},{5... | collective-permute-start | bytes 393224 | tf_op jit(solution)/shard_map/ppermute | solution.py:424
  53.7 2.9 %collective-permute-done.14.refs_3_ = f32[512,128]{1,0:T(8,128)S(1)} collective-permute-done((f32[512,128]{1,0:T(8,128)S(1)}, f32[512,128]{1,0:T(8,128)S(1)}, u32[]{:S(2)}, u32[]{:S(2)}) %collective-permute-start.14) | collective-permute-done | bytes 262176 | tf_op jit(solution)/shard_map/ppermute | solution.py:480
  56.6 2.5 %collective-permute-start.10 = (f32[128,256]{1,0:T(8,128)S(1)}, f32[128,256]{1,0:T(8,128)S(1)}, u32[]{:S(2)}, u32[]{:S(2)}) collective-permute-start(f32[128,256]{1,0:T(8,128)S(1)} %get-tuple-element.38), channel_id=1, source_target_pairs={{0,16},{4,20},{8,24},{12,28},{16,0},{20,4},{24,8},{28,12},{1,17},{... | collective-permute-start | bytes 393224 | tf_op jit(solution)/shard_map/ppermute | solution.py:424
  59.1 1.0 %weight_grad.1 = (f32[512,256]{1,0:T(8,128)S(1)}, f32[512,256]{1,0:T(8,128)S(1)}) custom-call(f32[512,128]{1,0:T(8,128)S(1)} %get-tuple-element.29.refs_0_, f32[512,128]{1,0:T(8,128)S(1)} %collective-permute-done.12.refs_1_, f32[512,128]{1,0:T(8,128)S(1)} %collective-permute-done.13.refs_2_, f32[512,128]{1,0:T(8,128)S(1)} %collective-permute-done.14.refs_3_, ...), custom_call_target="tpu_custom_call" | custom-call | flops 268435456 | bytes 2097152 | tf_op jit(solution)/shard_map/weight_grad/pallas_call | solution.py:400
  60.2 2.8 %collective-permute-done.11 = f32[128,256]{1,0:T(8,128)S(1)} collective-permute-done((f32[128,256]{1,0:T(8,128)S(1)}, f32[128,256]{1,0:T(8,128)S(1)}, u32[]{:S(2)}, u32[]{:S(2)}) %collective-permute-start.11) | collective-permute-done | bytes 131104 | tf_op jit(solution)/shard_map/ppermute | solution.py:424
  63.0 1.6 %collective-permute-done.10 = f32[128,256]{1,0:T(8,128)S(1)} collective-permute-done((f32[128,256]{1,0:T(8,128)S(1)}, f32[128,256]{1,0:T(8,128)S(1)}, u32[]{:S(2)}, u32[]{:S(2)}) %collective-permute-start.10) | collective-permute-done | bytes 131104 | tf_op jit(solution)/shard_map/ppermute | solution.py:424
  65.2 4.9 %collective-permute-done.18 = f32[512,256]{1,0:T(8,128)S(1)} collective-permute-done((f32[512,256]{1,0:T(8,128)S(1)}, f32[512,256]{1,0:T(8,128)S(1)}, u32[]{:S(2)}, u32[]{:S(2)}) %collective-permute-start.18) | collective-permute-done | bytes 524320 | tf_op jit(solution)/shard_map/ppermute | solution.py:498
  (36 shorter events, 9.2 us)
Async XLA Ops:
  2.2 8.2 %collective-permute-start.6 = (f32[128,256]{1,0:T(8,128)}, f32[128,256]{1,0:T(8,128)S(1)}, u32[]{:S(2)}, u32[]{:S(2)}) collective-permute-start(f32[128,256]{1,0:T(8,128)} %pack.1.refs_0_), channel_id=1, source_target_pairs={{0,24},{4,28},{8,16},{12,20},{16,8},{20,12},{24,0},{28,4},{1,25},{... | collective-permute-start | bytes 393224 | tf_op jit(solution)/shard_map/ppermute | solution.py:424
  6.2 6.5 %collective-permute-start.5 = (f32[128,256]{1,0:T(8,128)}, f32[128,256]{1,0:T(8,128)S(1)}, u32[]{:S(2)}, u32[]{:S(2)}) collective-permute-start(f32[128,256]{1,0:T(8,128)} %pack.1.refs_0_), channel_id=1, source_target_pairs={{0,16},{4,20},{8,24},{12,28},{16,0},{20,4},{24,8},{28,12},{1,17},{... | collective-permute-start | bytes 393224 | tf_op jit(solution)/shard_map/ppermute | solution.py:424
  6.7 6.3 %collective-permute-start.4 = (f32[128,256]{1,0:T(8,128)}, f32[128,256]{1,0:T(8,128)S(1)}, u32[]{:S(2)}, u32[]{:S(2)}) collective-permute-start(f32[128,256]{1,0:T(8,128)} %pack.1.refs_0_), channel_id=1, source_target_pairs={{0,8},{4,12},{8,0},{12,4},{16,24},{20,28},{24,16},{28,20},{1,9},{5... | collective-permute-start | bytes 393224 | tf_op jit(solution)/shard_map/ppermute | solution.py:424
  6.8 14.4 %collective-permute-start = (f32[128,512]{1,0:T(8,128)}, f32[128,512]{1,0:T(8,128)S(1)}, u32[]{:S(2)}, u32[]{:S(2)}) collective-permute-start(f32[128,512]{1,0:T(8,128)} %refs_4_.1), channel_id=1, source_target_pairs={{0,2},{1,3},{2,0},{3,1},{4,6},{5,7},{6,4},{7,5},{8,10},{9,11},{10,... | collective-permute-start | bytes 786440 | tf_op jit(solution)/shard_map/ppermute | solution.py:427
  13.9 20.0 %collective-permute-start.7 = (f32[512,256]{1,0:T(8,128)S(1)}, f32[512,256]{1,0:T(8,128)S(1)}, u32[]{:S(2)}, u32[]{:S(2)}) collective-permute-start(f32[512,256]{1,0:T(8,128)S(1)} %pad_maximum_fusion), channel_id=1, source_target_pairs={{0,4},{4,0},{8,12},{12,8},{16,20},{20,16},{24,28},{28,24},{1,5},{5... | collective-permute-start | bytes 1572872 | tf_op jit(solution)/shard_map/ppermute | solution.py:421
  14.0 12.8 %collective-permute-start.3 = (f32[128,512]{1,0:T(8,128)}, f32[128,512]{1,0:T(8,128)S(1)}, u32[]{:S(2)}, u32[]{:S(2)}) collective-permute-start(f32[128,512]{1,0:T(8,128)} %refs_4_.1), channel_id=1, source_target_pairs={{0,1},{1,0},{2,3},{3,2},{4,5},{5,4},{6,7},{7,6},{8,9},{9,8},{10,11... | collective-permute-start | bytes 786440 | tf_op jit(solution)/shard_map/ppermute | solution.py:427
  15.6 11.9 %collective-permute-start.1 = (f32[128,512]{1,0:T(8,128)}, f32[128,512]{1,0:T(8,128)S(1)}, u32[]{:S(2)}, u32[]{:S(2)}) collective-permute-start(f32[128,512]{1,0:T(8,128)} %refs_4_.1), channel_id=1, source_target_pairs={{1,2},{2,1},{5,6},{6,5},{9,10},{10,9},{13,14},{14,13},{17,18},{18,... | collective-permute-start | bytes 786440 | tf_op jit(solution)/shard_map/ppermute | solution.py:427
  21.2 11.1 %collective-permute-start.2 = (f32[128,512]{1,0:T(8,128)S(1)}, f32[128,512]{1,0:T(8,128)S(1)}, u32[]{:S(2)}, u32[]{:S(2)}) collective-permute-start(f32[128,512]{1,0:T(8,128)S(1)} %collective-permute-done.refs_1_), channel_id=1, source_target_pairs={{1,0},{2,3},{5,4},{6,7},{9,8},{10,11},{13,12},{14,15},{17,16},{18,... | collective-permute-start | bytes 786440 | tf_op jit(solution)/shard_map/ppermute | solution.py:427
  22.5 2.2 %copy-start = (f32[512,2048]{1,0:T(8,128)S(1)}, f32[512,2048]{1,0:T(8,128)}, u32[]{:S(2)}) copy-start(f32[512,2048]{1,0:T(8,128)} %refs_0_.5) | copy-start | bytes 12582916
  24.7 0.9 %copy-start.2 = (f32[128,512]{1,0:T(8,128)S(1)}, f32[128,512]{1,0:T(8,128)}, u32[]{:S(2)}) copy-start(f32[128,512]{1,0:T(8,128)} %refs_4_.1) | copy-start | bytes 786436
  27.5 6.5 %copy-start.1 = (f32[128,256]{1,0:T(8,128)S(1)}, f32[128,256]{1,0:T(8,128)}, u32[]{:S(2)}) copy-start(f32[128,256]{1,0:T(8,128)} %pack.1.refs_0_) | copy-start | bytes 393220
  27.5 6.5 %copy-start.3 = (f32[128,512]{1,0:T(8,128)S(1)}, f32[128,512]{1,0:T(8,128)}, u32[]{:S(2)}) copy-start(f32[128,512]{1,0:T(8,128)} %q_ref.5) | copy-start | bytes 786436
  41.5 6.5 %collective-permute-start.8 = (f32[512,256]{1,0:T(8,128)S(1)}, f32[512,256]{1,0:T(8,128)S(1)}, u32[]{:S(2)}, u32[]{:S(2)}) collective-permute-start(f32[512,256]{1,0:T(8,128)S(1)} %get-tuple-element.28), channel_id=1, source_target_pairs={{0,4},{4,0},{8,12},{12,8},{16,20},{20,16},{24,28},{28,24},{1,5},{5... | collective-permute-start | bytes 1572872 | tf_op jit(solution)/shard_map/ppermute | solution.py:421
  41.6 7.6 %collective-permute-start.15 = (f32[128,512]{1,0:T(8,128)S(1)}, f32[128,512]{1,0:T(8,128)S(1)}, u32[]{:S(2)}, u32[]{:S(2)}) collective-permute-start(f32[128,512]{1,0:T(8,128)S(1)} %get-tuple-element.31), channel_id=1, source_target_pairs={{0,4},{4,0},{8,12},{12,8},{16,20},{20,16},{24,28},{28,24},{1,5},{5... | collective-permute-start | bytes 786440 | tf_op jit(solution)/shard_map/ppermute | solution.py:481
  42.1 8.2 %collective-permute-start.16 = (f32[128,512]{1,0:T(8,128)S(1)}, f32[128,512]{1,0:T(8,128)S(1)}, u32[]{:S(2)}, u32[]{:S(2)}) collective-permute-start(f32[128,512]{1,0:T(8,128)S(1)} %get-tuple-element.32), channel_id=1, source_target_pairs={{0,8},{4,20},{8,0},{12,28},{16,24},{20,4},{24,16},{28,12},{1,9},{5... | collective-permute-start | bytes 786440 | tf_op jit(solution)/shard_map/ppermute | solution.py:481
  43.6 9.2 %collective-permute-start.17 = (f32[128,512]{1,0:T(8,128)S(1)}, f32[128,512]{1,0:T(8,128)S(1)}, u32[]{:S(2)}, u32[]{:S(2)}) collective-permute-start(f32[128,512]{1,0:T(8,128)S(1)} %get-tuple-element.33), channel_id=1, source_target_pairs={{0,20},{4,8},{8,28},{12,0},{16,4},{20,24},{24,12},{28,16},{1,21},{... | collective-permute-start | bytes 786440 | tf_op jit(solution)/shard_map/ppermute | solution.py:481
  43.6 13.0 %collective-permute-start.14 = (f32[512,128]{1,0:T(8,128)S(1)}, f32[512,128]{1,0:T(8,128)S(1)}, u32[]{:S(2)}, u32[]{:S(2)}) collective-permute-start(f32[512,128]{1,0:T(8,128)S(1)} %get-tuple-element.29.refs_0_), channel_id=1, source_target_pairs={{0,20},{4,8},{8,28},{12,0},{16,4},{20,24},{24,12},{28,16},{1,21},{... | collective-permute-start | bytes 786440 | tf_op jit(solution)/shard_map/ppermute | solution.py:480
  48.0 11.1 %collective-permute-start.13 = (f32[512,128]{1,0:T(8,128)S(1)}, f32[512,128]{1,0:T(8,128)S(1)}, u32[]{:S(2)}, u32[]{:S(2)}) collective-permute-start(f32[512,128]{1,0:T(8,128)S(1)} %get-tuple-element.29.refs_0_), channel_id=1, source_target_pairs={{0,8},{4,20},{8,0},{12,28},{16,24},{20,4},{24,16},{28,12},{1,9},{5... | collective-permute-start | bytes 786440 | tf_op jit(solution)/shard_map/ppermute | solution.py:480
  49.2 9.8 %collective-permute-start.12 = (f32[512,128]{1,0:T(8,128)S(1)}, f32[512,128]{1,0:T(8,128)S(1)}, u32[]{:S(2)}, u32[]{:S(2)}) collective-permute-start(f32[512,128]{1,0:T(8,128)S(1)} %get-tuple-element.29.refs_0_), channel_id=1, source_target_pairs={{0,4},{4,0},{8,12},{12,8},{16,20},{20,16},{24,28},{28,24},{1,5},{5... | collective-permute-start | bytes 786440 | tf_op jit(solution)/shard_map/ppermute | solution.py:480
  50.3 9.8 %collective-permute-start.9 = (f32[128,256]{1,0:T(8,128)S(1)}, f32[128,256]{1,0:T(8,128)S(1)}, u32[]{:S(2)}, u32[]{:S(2)}) collective-permute-start(f32[128,256]{1,0:T(8,128)S(1)} %get-tuple-element.36), channel_id=1, source_target_pairs={{0,8},{4,12},{8,0},{12,4},{16,24},{20,28},{24,16},{28,20},{1,9},{5... | collective-permute-start | bytes 393224 | tf_op jit(solution)/shard_map/ppermute | solution.py:424
  52.8 10.2 %collective-permute-start.11 = (f32[128,256]{1,0:T(8,128)S(1)}, f32[128,256]{1,0:T(8,128)S(1)}, u32[]{:S(2)}, u32[]{:S(2)}) collective-permute-start(f32[128,256]{1,0:T(8,128)S(1)} %get-tuple-element.37), channel_id=1, source_target_pairs={{0,24},{4,28},{8,16},{12,20},{16,8},{20,12},{24,0},{28,4},{1,25},{... | collective-permute-start | bytes 393224 | tf_op jit(solution)/shard_map/ppermute | solution.py:424
  56.6 7.9 %collective-permute-start.10 = (f32[128,256]{1,0:T(8,128)S(1)}, f32[128,256]{1,0:T(8,128)S(1)}, u32[]{:S(2)}, u32[]{:S(2)}) collective-permute-start(f32[128,256]{1,0:T(8,128)S(1)} %get-tuple-element.38), channel_id=1, source_target_pairs={{0,16},{4,20},{8,24},{12,28},{16,0},{20,4},{24,8},{28,12},{1,17},{... | collective-permute-start | bytes 393224 | tf_op jit(solution)/shard_map/ppermute | solution.py:424
  60.1 10.1 %collective-permute-start.18 = (f32[512,256]{1,0:T(8,128)S(1)}, f32[512,256]{1,0:T(8,128)S(1)}, u32[]{:S(2)}, u32[]{:S(2)}) collective-permute-start(f32[512,256]{1,0:T(8,128)S(1)} %get-tuple-element.35), channel_id=1, source_target_pairs={{0,16},{4,12},{8,24},{12,4},{16,0},{20,28},{24,8},{28,20},{1,17},{... | collective-permute-start | bytes 1572872 | tf_op jit(solution)/shard_map/ppermute | solution.py:498

commit v2 on v1

v2 whole, which is shorter than its diff:
```python
import functools
import math

import jax
import jax.numpy as jnp
from jax import lax
from jax.experimental import pallas as pl
from jax.experimental.pallas import tpu as pltpu
from jax.sharding import PartitionSpec as P

HD = 128
GROUP = 4
CORES = 2
MASKED = -1e30
F32 = jnp.float32
BF16 = jnp.bfloat16

NN = (((1,), (0,)), ((), ()))
NT = (((1,), (1,)), ((), ()))


def mm(a, b, dims=NN):
    return lax.dot_general(a, b, dims, preferred_element_type=F32)


def two(x):
    hi = x.astype(BF16)
    return hi, (x - hi.astype(F32)).astype(BF16)


def three(x):
    first = x.astype(BF16)
    rest = x - first.astype(F32)
    second = rest.astype(BF16)
    return first, second, (rest - second.astype(F32)).astype(BF16)


def cost(flops, size):
    return pl.CostEstimate(flops=flops, transcendentals=0, bytes_accessed=size)


def params(held=0):
    return pltpu.CompilerParams(vmem_limit_bytes=(12 << 20) + held)


def in_hbm(x):
    return pltpu.with_memory_space_constraint(x, pltpu.HBM)


def load_blocks(refs, dst, column):
    row = 0
    for ref in refs:
        count = ref.shape[0]
        dst[row : row + count, :] = ref[:, column : column + HD]
        row += count


def pack_kernel(keys_ref, values_ref, grad_ref, out_ref, upper_ref, lower_ref, sem):
    count = upper_ref.shape[0]
    pairs = (
        (keys_ref, out_ref.at[:, :HD]),
        (values_ref, out_ref.at[:, HD:]),
        (grad_ref.at[:count], upper_ref),
        (grad_ref.at[count:], lower_ref),
    )
    copies = [pltpu.make_async_copy(a, b, sem.at[i]) for i, (a, b) in enumerate(pairs)]
    for copy in copies:
        copy.start()
    for copy in copies:
        copy.wait()


def pack(keys, values, grad_out):
    tokens, columns = grad_out.shape
    part = jax.ShapeDtypeStruct((tokens // 2, columns), F32)
    return pl.pallas_call(
        pack_kernel,
        out_shape=(jax.ShapeDtypeStruct((tokens, 2 * HD), F32), part, part),
        in_specs=[pl.BlockSpec(memory_space=pltpu.HBM)] * 3,
        scratch_shapes=[pltpu.SemaphoreType.DMA((4,))],
        compiler_params=params(),
        name="pack",
    )(*(in_hbm(x) for x in (keys, values, grad_out)))


def forward_kernel(score_scale, other, q_ref, *refs):
    if other:
        *pieces, top_ref, norm_ref, acc_ref, attn_ref, exp_ref, inv_ref, keys, values, score = refs
    else:
        *pieces, top_ref, norm_ref, acc_ref, exp_ref, keys, values, score = refs
    tokens = q_ref.shape[0]
    rows = GROUP * tokens
    blocks = keys.shape[0] // tokens
    me = lax.axis_index("seq")
    load_blocks(pieces, keys, 0)
    load_blocks(pieces, values, HD)
    q1, q2, q3 = three(stacked_queries(q_ref))
    q11 = jnp.concatenate([q1, q1], axis=1)
    q22 = jnp.concatenate([q2, q2], axis=1)
    q13 = jnp.concatenate([q1, q3], axis=1)
    key_row = lax.broadcasted_iota(jnp.int32, (tokens, rows), 0)
    query_row = lax.broadcasted_iota(jnp.int32, (tokens, rows), 1) % tokens
    offset = key_row - query_row

    def scores(b, top):
        block = ((me // CORES) ^ b) * CORES + ((me % CORES) ^ other)
        at = pl.ds(pl.multiple_of(b * tokens, tokens), tokens)
        k1, k2, k3 = three(keys[at, :])
        k12 = jnp.concatenate([k1, k2], axis=1)
        k31 = jnp.concatenate([k3, k1], axis=1)
        s = mm(k31, q13, NT) + mm(k12, q22, NT) + mm(k12, q11, NT)
        s = jnp.where(offset <= (me - block) * tokens, s * score_scale, MASKED)
        score[at, :] = s
        return jnp.maximum(top, jnp.max(s, axis=0, keepdims=True))

    before = top_ref[0:1, :] if other else jnp.full((1, rows), MASKED, F32)
    top = lax.fori_loop(0, blocks, scores, before, unroll=2)

    def weigh(b, state):
        norm, acc = state
        at = pl.ds(pl.multiple_of(b * tokens, tokens), tokens)
        e = jnp.exp(score[at, :] - top)
        exp_ref[at, :] = e
        eh, el = two(e)
        vh, vl = two(values[at, :].T)
        both = mm(jnp.concatenate([vh, vl], axis=0), eh)
        acc = acc + (both[:HD] + both[HD:] + mm(vh, el))
        return norm + jnp.sum(e, axis=0, keepdims=True), acc

    if other:
        factor = jnp.exp(before - top)
        start = norm_ref[0:1, :] * factor, acc_ref[...] * factor
    else:
        start = jnp.zeros((1, rows), F32), jnp.zeros((HD, rows), F32)
    norm, acc = lax.fori_loop(0, blocks, weigh, start, unroll=2)
    if other:
        inv = 1.0 / norm
        inv_ref[0:8, :] = jnp.broadcast_to(inv * factor, (8, rows))
        inv_ref[8:16, :] = jnp.broadcast_to(inv, (8, rows))
        out = acc * inv
        for g in range(GROUP):
            attn_ref[g * HD : (g + 1) * HD, :] = out[:, g * tokens : (g + 1) * tokens]
    else:
        top_ref[...] = jnp.broadcast_to(top, top_ref.shape)
        norm_ref[...] = jnp.broadcast_to(norm, norm_ref.shape)
        acc_ref[...] = acc


def forward(q, pieces, carried, score_scale):
    tokens = q.shape[0]
    rows = GROUP * tokens
    half = sum(piece.shape[0] for piece in pieces)
    weights = jax.ShapeDtypeStruct((half, rows), F32)
    row = jax.ShapeDtypeStruct((8, rows), F32)
    if carried:
        shapes = (
            jax.ShapeDtypeStruct((GROUP * HD, tokens), F32),
            weights,
            jax.ShapeDtypeStruct((16, rows), F32),
        )
    else:
        shapes = row, row, jax.ShapeDtypeStruct((HD, rows), F32), weights
    return pl.pallas_call(
        functools.partial(forward_kernel, score_scale, 1 if carried else 0),
        out_shape=shapes,
        scratch_shapes=[
            pltpu.VMEM((half, HD), F32),
            pltpu.VMEM((half, HD), F32),
            pltpu.VMEM((half, rows), F32),
        ],
        compiler_params=params(12 * half * rows),
        cost_estimate=cost(36 * half * rows * HD, 8 * half * rows),
        name="attn_fwd",
    )(q, *pieces, *carried)


def stacked_queries(q_ref):
    return jnp.concatenate([q_ref[:, g * HD : (g + 1) * HD] for g in range(GROUP)], axis=0)


def stacked_grads(d_ref):
    return jnp.concatenate([d_ref[g * HD : (g + 1) * HD, :] for g in range(GROUP)], axis=1)


def key_grads(score_scale, q, d, exp_ref, inv, dp_ref, delta, keys, out_ref, acc):
    rows = q.shape[0]
    tokens = rows // GROUP
    qh, ql = two(q)
    qhl = jnp.concatenate([qh, ql], axis=1)
    dh, dl = two(d)
    dhl = jnp.concatenate([dh, dl], axis=0)

    def grads(b, acc):
        at = pl.ds(pl.multiple_of(b * tokens, tokens), tokens)
        p = exp_ref[at, :] * inv
        ds = p * (dp_ref[at, :] - delta) * score_scale
        ph, plo = two(p)
        sh, sl = two(ds)
        kh, kl = two(keys[at, :].T)
        both = mm(jnp.concatenate([kh, kl], axis=0), sh)
        acc = acc + (both[:HD] + both[HD:] + mm(kh, sl))
        dk = mm(sh, qhl)
        out_ref[at, 0:HD] = dk[:, :HD] + dk[:, HD:] + mm(sl, qh)
        dv = mm(ph, dhl, NT)
        out_ref[at, HD : 2 * HD] = dv[:, :HD] + dv[:, HD:] + mm(plo, dh, NT)
        return acc

    return lax.fori_loop(0, out_ref.shape[0] // tokens, grads, acc, unroll=2)


def backward_far_kernel(score_scale, q_ref, d_ref, near_ref, far_ref, inv_ref, *refs):
    *pieces, acc_ref, dp_ref, delta_ref, send_ref, keys, values, far_dp = refs
    tokens = q_ref.shape[0]
    rows = GROUP * tokens
    half = keys.shape[0]
    load_blocks(pieces[-1:], keys, 0)
    load_blocks(pieces, values, HD)
    d = stacked_grads(d_ref)
    dh, dl = two(d)
    dhh = jnp.concatenate([dh, dh], axis=0)

    def probs(exp_ref, out_ref, first):
        def one(b, total):
            at = pl.ds(pl.multiple_of(b * tokens, tokens), tokens)
            vh, vl = two(values[pl.ds(pl.multiple_of(first + b * tokens, tokens), tokens), :])
            dp = mm(vh, dl) + mm(jnp.concatenate([vh, vl], axis=1), dhh)
            out_ref[at, :] = dp
            return total + jnp.sum(exp_ref[at, :] * dp, axis=0, keepdims=True)

        return lax.fori_loop(0, half // tokens, one, jnp.zeros((1, rows), F32), unroll=2)

    inv = inv_ref[8:9, :]
    delta = probs(near_ref, dp_ref, 0) * inv_ref[0:1, :] + probs(far_ref, far_dp, half) * inv
    delta_ref[...] = jnp.broadcast_to(delta, delta_ref.shape)
    acc_ref[...] = key_grads(
        score_scale,
        stacked_queries(q_ref),
        d,
        far_ref,
        inv,
        far_dp,
        delta,
        keys,
        send_ref,
        jnp.zeros((HD, rows), F32),
    )


def backward_near_kernel(
    score_scale, q_ref, d_ref, near_ref, inv_ref, acc_ref, dp_ref, delta_ref, *refs
):
    *pieces, dq_ref, keep_ref, keys = refs
    tokens = q_ref.shape[0]
    load_blocks(pieces, keys, 0)
    acc = key_grads(
        score_scale,
        stacked_queries(q_ref),
        stacked_grads(d_ref),
        near_ref,
        inv_ref[0:1, :],
        dp_ref,
        delta_ref[0:1, :],
        keys,
        keep_ref,
        acc_ref[...],
    )
    for g in range(GROUP):
        dq_ref[:, g * HD : (g + 1) * HD] = acc[:, g * tokens : (g + 1) * tokens].T


def backward_far(q, d_attn, near, far, inv, pieces, score_scale):
    half, rows = far.shape
    return pl.pallas_call(
        functools.partial(backward_far_kernel, score_scale),
        out_shape=(
            jax.ShapeDtypeStruct((HD, rows), F32),
            jax.ShapeDtypeStruct((half, rows), F32),
            jax.ShapeDtypeStruct((8, rows), F32),
            jax.ShapeDtypeStruct((half, 2 * HD), F32),
        ),
        scratch_shapes=[
            pltpu.VMEM((half, HD), F32),
            pltpu.VMEM((2 * half, HD), F32),
            pltpu.VMEM((half, rows), F32),
        ],
        compiler_params=params(24 * half * rows),
        cost_estimate=cost(48 * half * rows * HD, 16 * half * rows),
        name="attn_bwd_far",
    )(q, d_attn, near, far, inv, *pieces)


def backward_near(q, d_attn, near, inv, carried, pieces, score_scale):
    half, rows = near.shape
    return pl.pallas_call(
        functools.partial(backward_near_kernel, score_scale),
        out_shape=(
            jax.ShapeDtypeStruct(q.shape, F32),
            jax.ShapeDtypeStruct((half, 2 * HD), F32),
        ),
        scratch_shapes=[pltpu.VMEM((half, HD), F32)],
        compiler_params=params(12 * half * rows),
        cost_estimate=cost(36 * half * rows * HD, 8 * half * rows),
        name="attn_bwd_near",
    )(q, d_attn, near, inv, *carried, *pieces)


def project_kernel(new, old, side, width, *refs):
    refs = list(refs)

    def take(count):
        taken = refs[:count]
        del refs[:count]
        return taken

    (w_ref,) = take(1)
    fresh = [[take(n) for n in counts] for _, counts in new]
    stale = [[take(n) for n in counts] for _, counts in old] if side else []
    carried = take(1) if old else []
    (d_ref,) = take(1)
    outs = take(len(column_sets(side))) if side else []
    weights, sem = (w_ref, None) if old else take(2)
    heads, rows, part = weights.shape
    tokens = d_ref.shape[1]
    me = lax.axis_index("head")

    def block(copies):
        whole = [
            jnp.concatenate([ref[...] for ref in rows], axis=0) if len(rows) > 1 else rows[0][...]
            for rows in copies
        ]
        return functools.reduce(jnp.add, whole)

    def column(offset):
        return pl.ds(pl.multiple_of((me ^ offset) * part, part), part)

    copies = {}
    if not old:
        for d in range(heads):
            copies[d] = pltpu.make_async_copy(w_ref.at[:, column(d)], weights.at[d], sem.at[d])
            copies[d].start()
    if side:
        (full,) = take(1)
        for piece, offset in zip(stale + fresh, [o for o, _ in old + new]):
            full[:, column(offset)] = block(piece)
        seq = lax.axis_index("seq")
        core = seq % CORES
        chip = seq // CORES
        x, y = chip % side, chip // side
        for out, (other_core, j) in zip(outs, column_sets(side)):
            kind = core ^ other_core
            fixed = jnp.where(kind == 0, x, y) ^ j
            moving = jnp.where(kind == 0, y, x)
            for t in range(side):
                i = moving ^ t
                index = jnp.where(kind == 0, i * side + fixed, fixed * side + i)
                at = pl.multiple_of((index * CORES + kind) * width, width)
                out[:, t * width : (t + 1) * width] = full[:, pl.ds(at, width)]
    step = rows // 2
    for i, (piece, (d, _)) in enumerate(zip(fresh, new)):
        g_hi, g_lo = two(block(piece))
        g_both = jnp.concatenate([g_hi, g_lo], axis=0)
        if d in copies:
            copies.pop(d).wait()
        for row in range(0, rows, step):
            at = slice(row, row + step)
            w_hi, w_lo = two(weights[d, at, :])
            both = mm(w_hi, g_both, NT)
            value = both[:, :tokens] + both[:, tokens:] + mm(w_lo, g_hi, NT)
            if i or carried:
                value = value + (d_ref if i else carried[0])[at, :]
            d_ref[at, :] = value
    for copy in copies.values():
        copy.wait()


def column_sets(side):
    sets = [(0, 0)]
    for j in range(side):
        if j:
            sets.append((0, j))
        sets.append((1, j))
    return sets


def project(weight, blocks, new, old, carried, side, width):
    heads = lax.axis_size("head")
    tokens = sum(piece.shape[0] for piece in blocks[0][0])
    if old:
        _, rows, part = weight.shape
    else:
        rows, part = weight.shape[0], weight.shape[1] // heads
    shapes = [jax.ShapeDtypeStruct((rows, tokens), F32)]
    scratch = []
    operands = [piece for d in new for copy in blocks[d] for piece in copy]
    if side:
        shapes += [jax.ShapeDtypeStruct((tokens, side * width), F32)] * len(column_sets(side))
        scratch.append(pltpu.VMEM((tokens, heads * part), F32))
        operands += [piece for d in old for copy in blocks[d] for piece in copy]
    if old:
        operands.append(carried)
    else:
        weight = in_hbm(weight)
        shapes.append(jax.ShapeDtypeStruct((heads, rows, part), F32))
        scratch.append(pltpu.SemaphoreType.DMA((heads,)))

    def counted(distances):
        return [(d, tuple(len(copy) for copy in blocks[d])) for d in distances]

    return pl.pallas_call(
        functools.partial(project_kernel, counted(new), counted(old), side, width),
        out_shape=tuple(shapes),
        in_specs=[pl.BlockSpec(memory_space=pltpu.VMEM if old else pltpu.HBM)]
        + [pl.BlockSpec(memory_space=pltpu.VMEM)] * len(operands),
        scratch_shapes=scratch,
        compiler_params=params(8 * heads * rows * part),
        cost_estimate=cost(24 * tokens * rows * part * len(new), 4 * rows * part * len(new)),
        name="project",
    )(weight, *operands)


def weight_kernel(count, *refs):
    attn = refs[:count]
    grad = refs[count : 2 * count]
    outs = refs[2 * count :]
    width = outs[0].shape[1]
    a_hi, a_lo = two(jnp.concatenate([ref[...] for ref in attn], axis=1))
    for t, out in enumerate(outs):
        cut = slice(t * width, (t + 1) * width)
        g_hi, g_lo = two(jnp.concatenate([ref[:, cut] for ref in grad], axis=0))
        out[...] = mm(a_hi, g_lo) + mm(a_lo, g_hi) + mm(a_hi, g_hi)


def weight_grad(attn, grad, side, width):
    rows = attn[0].shape[0]
    return pl.pallas_call(
        functools.partial(weight_kernel, len(attn)),
        out_shape=(jax.ShapeDtypeStruct((rows, width), F32),) * side,
        compiler_params=params(),
        cost_estimate=cost(2 * rows * rows * width * side, 8 * rows * width * side),
        name="weight_grad",
    )(*attn, *grad)


def body(queries, keys, values, grad_out, out_weight):
    tokens = queries.shape[0]
    seq = lax.axis_size("seq")
    heads = lax.axis_size("head")
    chips = seq // CORES
    width = out_weight.shape[1] // seq
    score_scale = 1.0 / math.sqrt(HD)
    side = math.isqrt(chips)
    exchange = side * side == chips and width % 128 == 0

    def swap(block):
        return lax.ppermute(block, "seq", [(i, i ^ 1) for i in range(seq)])

    def to_chip(block, j):
        return lax.ppermute(block, "seq", [(i, i ^ (CORES * j)) for i in range(seq)])

    def along(block, route):
        return lax.ppermute(block, "head", route)

    own, upper, lower = pack(keys, values, grad_out)
    by_distance = {0: ((upper, lower),)}
    for d in range(1, heads):
        pairs = [(i, i ^ d) for i in range(heads)]
        if heads != GROUP or d == 1:
            by_distance[d] = ((along(grad_out, pairs),),)
        elif d == 2:
            by_distance[d] = ((along(upper, pairs), along(lower, pairs)),)
        else:
            ends = [(1, 0), (2, 3)]
            ((near_upper, near_lower),) = by_distance[2]
            by_distance[d] = (
                (along(grad_out, [(1, 2), (2, 1)]),),
                (along(near_upper, ends), along(near_lower, ends)),
            )

    same = [own]
    for j in range(1, chips):
        same.append(to_chip(own, j))
    pieces = same + [swap(jnp.concatenate(same, axis=0))]

    *carried, near = forward(queries, same, (), score_scale)
    attn, far, inv = forward(queries, pieces[-1:], carried, score_scale)
    weight, d_attn, column = out_weight, None, ()
    seen = []
    for fresh in ([0], [1], list(range(2, heads))):
        final = fresh[-1] == heads - 1
        d_attn, *column = project(
            weight, by_distance, fresh, seen, d_attn, side if exchange and final else 0, width
        )
        if not seen:
            weight = column.pop()
        seen = seen + fresh
        if final:
            break

    if exchange:

        def routes(cross, j):
            found = []
            for i in range(seq):
                core, chip = i % CORES, i // CORES
                kind = core ^ cross
                x, y = chip % side, chip // side
                if kind == 0:
                    x ^= j
                else:
                    y ^= j
                found.append((i, (y * side + x) * CORES + kind))
            return found

        sets = column_sets(side)
        moved_grad, moved_attn = [column[0]], [attn]
        for i in range(1, len(sets)):
            moved_attn.append(lax.ppermute(attn, "seq", routes(*sets[i])))
            moved_grad.append(lax.ppermute(column[i], "seq", routes(*sets[i])))
        partial = weight_grad(moved_attn, moved_grad, side, width)

        def final_routes(t):
            found = []
            for i in range(seq):
                core, chip = i % CORES, i // CORES
                x, y = chip % side, chip // side
                if core == 0:
                    y ^= t
                else:
                    x ^= t
                found.append((i, (y * side + x) * CORES + core))
            return found

        grad_wo = partial[0]
        for t in range(1, side):
            moved = lax.ppermute(partial[t], "seq", final_routes(t))
            grad_wo = grad_wo + moved
    else:
        grad_full = lax.all_gather(grad_out, "head", axis=1, tiled=True)
        grad_wo = lax.psum_scatter(
            jnp.dot(grad_full.T, attn.T, precision=lax.Precision.HIGHEST),
            "seq",
            scatter_dimension=0,
            tiled=True,
        ).T

    *carried, send = backward_far(queries, d_attn, near, far, inv, pieces, score_scale)
    swapped = swap(send)
    grad_q, keep = backward_near(queries, d_attn, near, inv, carried, same, score_scale)
    summed = (keep + swapped).reshape(chips, tokens, 2 * HD)
    grad_kv = summed[0]
    for j in range(1, chips):
        moved = to_chip(summed[j], j)
        grad_kv = grad_kv + moved
    return (grad_q, grad_kv[:, :HD], grad_kv[:, HD:], grad_wo)


def solution(mesh):
    in_specs = (
        P("seq", "head"),
        P("seq", "head"),
        P("seq", "head"),
        P("seq", "head"),
        P("head", None),
    )
    out_specs = (P("seq", "head"), P("seq", "head"), P("seq", "head"), P("head", "seq"))
    return jax.shard_map(
        body,
        mesh=mesh,
        in_specs=in_specs,
        out_specs=out_specs,
        check_vma=False,
    )
```

time: 71.3 us -> 70.2 us (0.985)
  waiting for transfers between devices: 26.5 us -> 30.5 us
  local copies, waits for them, and re-layouts: 3.83 us -> 0.69 us
  starting transfers between devices: 22.4 us -> 21.1 us
  other arithmetic: 1.9 us -> 1 us
    unnamed x8 -> x2, local copies, waits for them, and re-layouts: 3.15 us -> 0.01 us
    ppermute x6, starting transfers between devices: 10.5 us -> 8.21 us  [to_chip(): return lax.ppermute(block, 'seq', [(i, i ^ CORES * j) for i in range(seq)])]
    ppermute x3, waiting for transfers between devices: 0.96 us -> 2.37 us  [body(): moved_grad.append(lax.ppermute(column[i], 'seq', routes(*sets[i])))]
    ppermute x4 -> x6, starting transfers between devices: 6.58 us -> 7.79 us  [along(): return lax.ppermute(block, 'head', route)]
    ppermute x6, waiting for transfers between devices: 7.51 us -> 8.67 us  [to_chip(): return lax.ppermute(block, 'seq', [(i, i ^ CORES * j) for i in range(seq)])]
    ppermute x3, starting transfers between devices: 3.06 us -> 2.12 us  [body(): moved_attn.append(lax.ppermute(attn, 'seq', routes(*sets[i])))]
    ppermute x4 -> x6, waiting for transfers between devices: 10.2 us -> 11.1 us  [along(): return lax.ppermute(block, 'head', route)]
    concatenate x1, other arithmetic: 0.94 us -> 0.03 us  [body(): pieces = same + [swap(jnp.concatenate(same, axis=0))]]
  transfers between devices with their start and end apart: 19 -> 21, of which waited for: 11 -> 13; matrix products, arithmetic and copies ran while one was open for 2% -> 1% of each run, Pallas kernels for 9% -> 13%
where the time goes in v2:
time: 70.2 us; the launch traced here: 70 us
  waiting for transfers between devices  30.5 us (43%)
  starting transfers between devices  21.1 us (30%)
  Pallas kernels  15.9 us (23%)
  other arithmetic  1 us (1%)
  between operations  0.81 us (1%)
    ppermute x6, waiting for transfers between devices, along(): return lax.ppermute(block, 'head', route)  11.1 us
    ppermute x6, waiting for transfers between devices, to_chip(): return lax.ppermute(block, 'seq', [(i, i ^ CORES * j) for i in range(seq)])  8.67 us
    ppermute x6, starting transfers between devices, to_chip(): return lax.ppermute(block, 'seq', [(i, i ^ CORES * j) for i in range(seq)])  8.21 us
    ppermute x6, starting transfers between devices, along(): return lax.ppermute(block, 'head', route)  7.79 us
    ppermute x1, waiting for transfers between devices, body(): moved = lax.ppermute(partial[t], 'seq', final_routes(t))  5.19 us
    pallas_call x2, Pallas kernels, forward(): pl.pallas_call(functools.partial(forward_kernel, score_scale, 1 if carrie...  4.69 us
    pallas_call x3, Pallas kernels, project(): pl.pallas_call(functools.partial(project_kernel, counted(new), counted(ol...  3.52 us
    ppermute x3, waiting for transfers between devices, body(): moved_attn.append(lax.ppermute(attn, 'seq', routes(*sets[i])))  3.22 us
  transfers between devices with their start and end apart: 21, of which 13 were waited for; matrix products, arithmetic and copies ran while one was open for 1% of the time, Pallas kernels for 13%

profile of v2, /device:TPU:0, one launch (start us, length us, event | category | flops | bytes accessed | tf_op | source)
XLA Modules:
  0.0 70.0 jit_solution(3349015412763853042)
XLA Ops:
  1.8 3.0 %collective-permute-start.6 = (f32[128,256]{1,0:T(8,128)S(1)}, f32[128,256]{1,0:T(8,128)S(1)}, u32[]{:S(2)}, u32[]{:S(2)}) collective-permute-start(f32[128,256]{1,0:T(8,128)S(1)} %get-tuple-element.34.refs_0_), channel_id=1, source_target_pairs={{0,8},{4,12},{8,0},{12,4},{16,24},{20,28},{24,16},{28,20},{1,9},{5... | collective-permute-start | bytes 393224 | tf_op jit(solution)/shard_map/ppermute | solution.py:458
  4.8 1.5 %collective-permute-start.7 = (f32[128,256]{1,0:T(8,128)S(1)}, f32[128,256]{1,0:T(8,128)S(1)}, u32[]{:S(2)}, u32[]{:S(2)}) collective-permute-start(f32[128,256]{1,0:T(8,128)S(1)} %get-tuple-element.34.refs_0_), channel_id=1, source_target_pairs={{0,16},{4,20},{8,24},{12,28},{16,0},{20,4},{24,8},{28,12},{1,17},{... | collective-permute-start | bytes 393224 | tf_op jit(solution)/shard_map/ppermute | solution.py:458
  6.3 2.3 %collective-permute-done.6.refs_1_ = f32[128,256]{1,0:T(8,128)S(1)} collective-permute-done((f32[128,256]{1,0:T(8,128)S(1)}, f32[128,256]{1,0:T(8,128)S(1)}, u32[]{:S(2)}, u32[]{:S(2)}) %collective-permute-start.6) | collective-permute-done | bytes 131104 | tf_op jit(solution)/shard_map/ppermute | solution.py:458
  8.7 3.9 %collective-permute-done.7.refs_2_ = f32[128,256]{1,0:T(8,128)S(1)} collective-permute-done((f32[128,256]{1,0:T(8,128)S(1)}, f32[128,256]{1,0:T(8,128)S(1)}, u32[]{:S(2)}, u32[]{:S(2)}) %collective-permute-start.7) | collective-permute-done | bytes 131104 | tf_op jit(solution)/shard_map/ppermute | solution.py:458
  12.7 1.6 %collective-permute-start.5 = (f32[128,512]{1,0:T(8,128)}, f32[128,512]{1,0:T(8,128)S(1)}, u32[]{:S(2)}, u32[]{:S(2)}) collective-permute-start(f32[128,512]{1,0:T(8,128)} %grad_ref.1), channel_id=1, source_target_pairs={{0,1},{1,0},{2,3},{3,2},{4,5},{5,4},{6,7},{7,6},{8,9},{9,8},{10,11... | collective-permute-start | bytes 786440 | tf_op jit(solution)/shard_map/ppermute | solution.py:461
  14.3 2.6 %collective-permute-start = (f32[64,512]{1,0:T(8,128)S(1)}, f32[64,512]{1,0:T(8,128)S(1)}, u32[]{:S(2)}, u32[]{:S(2)}) collective-permute-start(f32[64,512]{1,0:T(8,128)S(1)} %get-tuple-element.29.refs_1_.refs_6_), channel_id=1, source_target_pairs={{0,2},{1,3},{2,0},{3,1},{4,6},{5,7},{6,4},{7,5},{8,10},{9,11},{10,... | collective-permute-start | bytes 393224 | tf_op jit(solution)/shard_map/ppermute | solution.py:461
  17.9 2.2 %project.3 = (f32[512,128]{1,0:T(8,128)S(1)}, f32[4,512,512]{2,1,0:T(8,128)S(1)}) custom-call(f32[512,2048]{1,0:T(8,128)} %refs_0_.1, f32[64,512]{1,0:T(8,128)S(1)} %get-tuple-element.29.refs_1_.refs_6_, f32[64,512]{1,0:T(8,128)S(1)} %get-tuple-element.30.refs_2_.refs_7_), custom_call_target="tpu_custom_call" | custom-call | flops 805306368 | bytes 1048576 | tf_op jit(solution)/shard_map/project/pallas_call | solution.py:409
  20.2 3.9 %collective-permute-done.refs_1_ = f32[64,512]{1,0:T(8,128)S(1)} collective-permute-done((f32[64,512]{1,0:T(8,128)S(1)}, f32[64,512]{1,0:T(8,128)S(1)}, u32[]{:S(2)}, u32[]{:S(2)}) %collective-permute-start) | collective-permute-done | bytes 131104 | tf_op jit(solution)/shard_map/ppermute | solution.py:461
  24.1 1.3 %collective-permute-start.3 = (f32[64,512]{1,0:T(8,128)S(1)}, f32[64,512]{1,0:T(8,128)S(1)}, u32[]{:S(2)}, u32[]{:S(2)}) collective-permute-start(f32[64,512]{1,0:T(8,128)S(1)} %collective-permute-done.refs_1_), channel_id=1, source_target_pairs={{1,0},{2,3},{5,4},{6,7},{9,8},{10,11},{13,12},{14,15},{17,16},{18,... | collective-permute-start | bytes 393224 | tf_op jit(solution)/shard_map/ppermute | solution.py:461
  25.4 4.4 %collective-permute-done.1.refs_2_ = f32[64,512]{1,0:T(8,128)S(1)} collective-permute-done((f32[64,512]{1,0:T(8,128)S(1)}, f32[64,512]{1,0:T(8,128)S(1)}, u32[]{:S(2)}, u32[]{:S(2)}) %collective-permute-start.1) | collective-permute-done | bytes 131104 | tf_op jit(solution)/shard_map/ppermute | solution.py:461
  29.8 1.3 %collective-permute-start.4 = (f32[64,512]{1,0:T(8,128)S(1)}, f32[64,512]{1,0:T(8,128)S(1)}, u32[]{:S(2)}, u32[]{:S(2)}) collective-permute-start(f32[64,512]{1,0:T(8,128)S(1)} %collective-permute-done.1.refs_2_), channel_id=1, source_target_pairs={{1,0},{2,3},{5,4},{6,7},{9,8},{10,11},{13,12},{14,15},{17,16},{18,... | collective-permute-start | bytes 393224 | tf_op jit(solution)/shard_map/ppermute | solution.py:461
  31.1 2.3 %attn_fwd.2 = (f32[8,512]{1,0:T(8,128)S(1)}, f32[8,512]{1,0:T(8,128)S(1)}, f32[128,512]{1,0:T(8,128)S(1)}, f32[512,512]{1,0:T(8,128)S(1)}) custom-call(f32[128,512]{1,0:T(8,128)S(1)} %copy-done, f32[128,256]{1,0:T(8,128)S(1)} %get-tuple-element.34.refs_0_, f32[128,256]{1,0:T(8,128)S(1)} %collective-permute-done.6.refs_1_, ...), custom_call_target="tpu_custom_call" | custom-call | flops 1207959552 | bytes 2097152 | tf_op jit(solution)/shard_map/attn_fwd/pallas_call | solution.py:163
  33.9 2.7 %collective-permute-done.4.refs_5_ = f32[64,512]{1,0:T(8,128)S(1)} collective-permute-done((f32[64,512]{1,0:T(8,128)S(1)}, f32[64,512]{1,0:T(8,128)S(1)}, u32[]{:S(2)}, u32[]{:S(2)}) %collective-permute-start.4) | collective-permute-done | bytes 131104 | tf_op jit(solution)/shard_map/ppermute | solution.py:461
  37.5 2.4 %attn_fwd.3 = (f32[512,128]{1,0:T(8,128)S(1)}, f32[512,512]{1,0:T(8,128)S(1)}, f32[16,512]{1,0:T(8,128)S(1)}) custom-call(f32[128,512]{1,0:T(8,128)S(1)} %copy-done, f32[512,256]{1,0:T(8,128)S(1)} %collective-permute-done.9.refs_0_.refs_4_, f32[8,512]{1,0:T(8,128)S(1)} %get-tuple-element.36.refs_1_, f32[8,512]{1,0:T(8,128)S(1)} %get-tuple-element.37.refs_2_, ...), custom_call_target="tpu_custom_call" | custom-call | flops 1207959552 | bytes 2097152 | tf_op jit(solution)/shard_map/attn_fwd/pallas_call | solution.py:163
  39.9 3.0 %attn_bwd_far.1 = (f32[128,512]{1,0:T(8,128)S(1)}, f32[512,512]{1,0:T(8,128)S(1)}, f32[8,512]{1,0:T(8,128)S(1)}, f32[512,256]{1,0:T(8,128)S(1)}) custom-call(f32[128,512]{1,0:T(8,128)S(1)} %copy-done, f32[512,128]{1,0:T(8,128)S(1)} %get-tuple-element.33.d_ref, f32[512,512]{1,0:T(8,128)S(1)} %get-tuple-element.35.near_ref, ...), custom_call_target="tpu_custom_call" | custom-call | flops 1610612736 | bytes 4194304 | tf_op jit(solution)/shard_map/attn_bwd_far/pallas_call | solution.py:273
  43.5 1.2 %collective-permute-start.18 = (f32[128,512]{1,0:T(8,128)S(1)}, f32[128,512]{1,0:T(8,128)S(1)}, u32[]{:S(2)}, u32[]{:S(2)}) collective-permute-start(f32[128,512]{1,0:T(8,128)S(1)} %get-tuple-element.50), channel_id=1, source_target_pairs={{0,8},{4,20},{8,0},{12,28},{16,24},{20,4},{24,16},{28,12},{1,9},{5... | collective-permute-start | bytes 786440 | tf_op jit(solution)/shard_map/ppermute | solution.py:518
  45.6 2.6 %attn_bwd_near.1 = (f32[128,512]{1,0:T(8,128)}, f32[512,256]{1,0:T(8,128)S(1)}) custom-call(f32[128,512]{1,0:T(8,128)S(1)} %copy-done, f32[512,128]{1,0:T(8,128)S(1)} %get-tuple-element.33.d_ref, f32[512,512]{1,0:T(8,128)S(1)} %get-tuple-element.35.near_ref, f32[16,512]{1,0:T(8,128)S(1)} %get-tuple-element.39.inv_ref, ...), custom_call_target="tpu_custom_call" | custom-call | flops 1207959552 | bytes 2097152 | tf_op jit(solution)/shard_map/attn_bwd_near/pallas_call | solution.py:294
  49.7 2.3 %collective-permute-done.18.refs_6_ = f32[128,512]{1,0:T(8,128)S(1)} collective-permute-done((f32[128,512]{1,0:T(8,128)S(1)}, f32[128,512]{1,0:T(8,128)S(1)}, u32[]{:S(2)}, u32[]{:S(2)}) %collective-permute-start.18) | collective-permute-done | bytes 262176 | tf_op jit(solution)/shard_map/ppermute | solution.py:518
  52.0 1.2 %collective-permute-start.13 = (f32[128,256]{1,0:T(8,128)S(1)}, f32[128,256]{1,0:T(8,128)S(1)}, u32[]{:S(2)}, u32[]{:S(2)}) collective-permute-start(f32[128,256]{1,0:T(8,128)S(1)} %get-tuple-element.55), channel_id=1, source_target_pairs={{0,24},{4,28},{8,16},{12,20},{16,8},{20,12},{24,0},{28,4},{1,25},{... | collective-permute-start | bytes 393224 | tf_op jit(solution)/shard_map/ppermute | solution.py:458
  53.3 1.8 %collective-permute-start.12 = (f32[128,256]{1,0:T(8,128)S(1)}, f32[128,256]{1,0:T(8,128)S(1)}, u32[]{:S(2)}, u32[]{:S(2)}) collective-permute-start(f32[128,256]{1,0:T(8,128)S(1)} %get-tuple-element.56), channel_id=1, source_target_pairs={{0,16},{4,20},{8,24},{12,28},{16,0},{20,4},{24,8},{28,12},{1,17},{... | collective-permute-start | bytes 393224 | tf_op jit(solution)/shard_map/ppermute | solution.py:458
  55.7 1.9 %collective-permute-done.15.refs_2_ = f32[512,128]{1,0:T(8,128)S(1)} collective-permute-done((f32[512,128]{1,0:T(8,128)S(1)}, f32[512,128]{1,0:T(8,128)S(1)}, u32[]{:S(2)}, u32[]{:S(2)}) %collective-permute-start.15) | collective-permute-done | bytes 262176 | tf_op jit(solution)/shard_map/ppermute | solution.py:517
  57.6 1.3 %collective-permute-done.16.refs_3_ = f32[512,128]{1,0:T(8,128)S(1)} collective-permute-done((f32[512,128]{1,0:T(8,128)S(1)}, f32[512,128]{1,0:T(8,128)S(1)}, u32[]{:S(2)}, u32[]{:S(2)}) %collective-permute-start.16) | collective-permute-done | bytes 262176 | tf_op jit(solution)/shard_map/ppermute | solution.py:517
  60.8 1.3 %collective-permute-done.13 = f32[128,256]{1,0:T(8,128)S(1)} collective-permute-done((f32[128,256]{1,0:T(8,128)S(1)}, f32[128,256]{1,0:T(8,128)S(1)}, u32[]{:S(2)}, u32[]{:S(2)}) %collective-permute-start.13) | collective-permute-done | bytes 131104 | tf_op jit(solution)/shard_map/ppermute | solution.py:458
  64.0 5.2 %collective-permute-done.20 = f32[512,256]{1,0:T(8,128)S(1)} collective-permute-done((f32[512,256]{1,0:T(8,128)S(1)}, f32[512,256]{1,0:T(8,128)S(1)}, u32[]{:S(2)}, u32[]{:S(2)}) %collective-permute-start.20) | collective-permute-done | bytes 524320 | tf_op jit(solution)/shard_map/ppermute | solution.py:535
  (35 shorter events, 11.8 us)
Async XLA Ops:
  0.6 30.5 %copy-start = (f32[128,512]{1,0:T(8,128)S(1)}, f32[128,512]{1,0:T(8,128)}, u32[]{:S(2)}) copy-start(f32[128,512]{1,0:T(8,128)} %q_ref.7) | copy-start | bytes 786436
  1.8 6.9 %collective-permute-start.6 = (f32[128,256]{1,0:T(8,128)S(1)}, f32[128,256]{1,0:T(8,128)S(1)}, u32[]{:S(2)}, u32[]{:S(2)}) collective-permute-start(f32[128,256]{1,0:T(8,128)S(1)} %get-tuple-element.34.refs_0_), channel_id=1, source_target_pairs={{0,8},{4,12},{8,0},{12,4},{16,24},{20,28},{24,16},{28,20},{1,9},{5... | collective-permute-start | bytes 393224 | tf_op jit(solution)/shard_map/ppermute | solution.py:458
  4.8 7.8 %collective-permute-start.7 = (f32[128,256]{1,0:T(8,128)S(1)}, f32[128,256]{1,0:T(8,128)S(1)}, u32[]{:S(2)}, u32[]{:S(2)}) collective-permute-start(f32[128,256]{1,0:T(8,128)S(1)} %get-tuple-element.34.refs_0_), channel_id=1, source_target_pairs={{0,16},{4,20},{8,24},{12,28},{16,0},{20,4},{24,8},{28,12},{1,17},{... | collective-permute-start | bytes 393224 | tf_op jit(solution)/shard_map/ppermute | solution.py:458
  6.3 6.3 %collective-permute-start.8 = (f32[128,256]{1,0:T(8,128)S(1)}, f32[128,256]{1,0:T(8,128)S(1)}, u32[]{:S(2)}, u32[]{:S(2)}) collective-permute-start(f32[128,256]{1,0:T(8,128)S(1)} %get-tuple-element.34.refs_0_), channel_id=1, source_target_pairs={{0,24},{4,28},{8,16},{12,20},{16,8},{20,12},{24,0},{28,4},{1,25},{... | collective-permute-start | bytes 393224 | tf_op jit(solution)/shard_map/ppermute | solution.py:458
  12.6 24.9 %collective-permute-start.9 = (f32[512,256]{1,0:T(8,128)S(1)}, f32[512,256]{1,0:T(8,128)S(1)}, u32[]{:S(2)}, u32[]{:S(2)}) collective-permute-start(f32[512,256]{1,0:T(8,128)S(1)} %pad_maximum_fusion), channel_id=1, source_target_pairs={{0,4},{4,0},{8,12},{12,8},{16,20},{20,16},{24,28},{28,24},{1,5},{5... | collective-permute-start | bytes 1572872 | tf_op jit(solution)/shard_map/ppermute | solution.py:455
  12.7 20.8 %collective-permute-start.5 = (f32[128,512]{1,0:T(8,128)}, f32[128,512]{1,0:T(8,128)S(1)}, u32[]{:S(2)}, u32[]{:S(2)}) collective-permute-start(f32[128,512]{1,0:T(8,128)} %grad_ref.1), channel_id=1, source_target_pairs={{0,1},{1,0},{2,3},{3,2},{4,5},{5,4},{6,7},{7,6},{8,9},{9,8},{10,11... | collective-permute-start | bytes 786440 | tf_op jit(solution)/shard_map/ppermute | solution.py:461
  14.3 9.8 %collective-permute-start = (f32[64,512]{1,0:T(8,128)S(1)}, f32[64,512]{1,0:T(8,128)S(1)}, u32[]{:S(2)}, u32[]{:S(2)}) collective-permute-start(f32[64,512]{1,0:T(8,128)S(1)} %get-tuple-element.29.refs_1_.refs_6_), channel_id=1, source_target_pairs={{0,2},{1,3},{2,0},{3,1},{4,6},{5,7},{6,4},{7,5},{8,10},{9,11},{10,... | collective-permute-start | bytes 393224 | tf_op jit(solution)/shard_map/ppermute | solution.py:461
  16.9 12.9 %collective-permute-start.1 = (f32[64,512]{1,0:T(8,128)S(1)}, f32[64,512]{1,0:T(8,128)S(1)}, u32[]{:S(2)}, u32[]{:S(2)}) collective-permute-start(f32[64,512]{1,0:T(8,128)S(1)} %get-tuple-element.30.refs_2_.refs_7_), channel_id=1, source_target_pairs={{0,2},{1,3},{2,0},{3,1},{4,6},{5,7},{6,4},{7,5},{8,10},{9,11},{10,... | collective-permute-start | bytes 393224 | tf_op jit(solution)/shard_map/ppermute | solution.py:461
  17.3 16.7 %collective-permute-start.2 = (f32[128,512]{1,0:T(8,128)}, f32[128,512]{1,0:T(8,128)S(1)}, u32[]{:S(2)}, u32[]{:S(2)}) collective-permute-start(f32[128,512]{1,0:T(8,128)} %grad_ref.1), channel_id=1, source_target_pairs={{1,2},{2,1},{5,6},{6,5},{9,10},{10,9},{13,14},{14,13},{17,18},{18,... | collective-permute-start | bytes 786440 | tf_op jit(solution)/shard_map/ppermute | solution.py:461
  24.1 9.8 %collective-permute-start.3 = (f32[64,512]{1,0:T(8,128)S(1)}, f32[64,512]{1,0:T(8,128)S(1)}, u32[]{:S(2)}, u32[]{:S(2)}) collective-permute-start(f32[64,512]{1,0:T(8,128)S(1)} %collective-permute-done.refs_1_), channel_id=1, source_target_pairs={{1,0},{2,3},{5,4},{6,7},{9,8},{10,11},{13,12},{14,15},{17,16},{18,... | collective-permute-start | bytes 393224 | tf_op jit(solution)/shard_map/ppermute | solution.py:461
  29.8 6.8 %collective-permute-start.4 = (f32[64,512]{1,0:T(8,128)S(1)}, f32[64,512]{1,0:T(8,128)S(1)}, u32[]{:S(2)}, u32[]{:S(2)}) collective-permute-start(f32[64,512]{1,0:T(8,128)S(1)} %collective-permute-done.1.refs_2_), channel_id=1, source_target_pairs={{1,0},{2,3},{5,4},{6,7},{9,8},{10,11},{13,12},{14,15},{17,16},{18,... | collective-permute-start | bytes 393224 | tf_op jit(solution)/shard_map/ppermute | solution.py:461
  42.9 5.3 %collective-permute-start.10 = (f32[512,256]{1,0:T(8,128)S(1)}, f32[512,256]{1,0:T(8,128)S(1)}, u32[]{:S(2)}, u32[]{:S(2)}) collective-permute-start(f32[512,256]{1,0:T(8,128)S(1)} %get-tuple-element.46), channel_id=1, source_target_pairs={{0,4},{4,0},{8,12},{12,8},{16,20},{20,16},{24,28},{28,24},{1,5},{5... | collective-permute-start | bytes 1572872 | tf_op jit(solution)/shard_map/ppermute | solution.py:455
  43.0 6.5 %collective-permute-start.17 = (f32[128,512]{1,0:T(8,128)S(1)}, f32[128,512]{1,0:T(8,128)S(1)}, u32[]{:S(2)}, u32[]{:S(2)}) collective-permute-start(f32[128,512]{1,0:T(8,128)S(1)} %get-tuple-element.49), channel_id=1, source_target_pairs={{0,4},{4,0},{8,12},{12,8},{16,20},{20,16},{24,28},{28,24},{1,5},{5... | collective-permute-start | bytes 786440 | tf_op jit(solution)/shard_map/ppermute | solution.py:518
  43.5 8.5 %collective-permute-start.18 = (f32[128,512]{1,0:T(8,128)S(1)}, f32[128,512]{1,0:T(8,128)S(1)}, u32[]{:S(2)}, u32[]{:S(2)}) collective-permute-start(f32[128,512]{1,0:T(8,128)S(1)} %get-tuple-element.50), channel_id=1, source_target_pairs={{0,8},{4,20},{8,0},{12,28},{16,24},{20,4},{24,16},{28,12},{1,9},{5... | collective-permute-start | bytes 786440 | tf_op jit(solution)/shard_map/ppermute | solution.py:518
  44.7 8.6 %collective-permute-start.19 = (f32[128,512]{1,0:T(8,128)S(1)}, f32[128,512]{1,0:T(8,128)S(1)}, u32[]{:S(2)}, u32[]{:S(2)}) collective-permute-start(f32[128,512]{1,0:T(8,128)S(1)} %get-tuple-element.51), channel_id=1, source_target_pairs={{0,20},{4,8},{8,28},{12,0},{16,4},{20,24},{24,12},{28,16},{1,21},{... | collective-permute-start | bytes 786440 | tf_op jit(solution)/shard_map/ppermute | solution.py:518
  44.9 10.2 %collective-permute-start.14 = (f32[512,128]{1,0:T(8,128)S(1)}, f32[512,128]{1,0:T(8,128)S(1)}, u32[]{:S(2)}, u32[]{:S(2)}) collective-permute-start(f32[512,128]{1,0:T(8,128)S(1)} %get-tuple-element.47.refs_0_), channel_id=1, source_target_pairs={{0,4},{4,0},{8,12},{12,8},{16,20},{20,16},{24,28},{28,24},{1,5},{5... | collective-permute-start | bytes 786440 | tf_op jit(solution)/shard_map/ppermute | solution.py:517
  48.2 9.4 %collective-permute-start.15 = (f32[512,128]{1,0:T(8,128)S(1)}, f32[512,128]{1,0:T(8,128)S(1)}, u32[]{:S(2)}, u32[]{:S(2)}) collective-permute-start(f32[512,128]{1,0:T(8,128)S(1)} %get-tuple-element.47.refs_0_), channel_id=1, source_target_pairs={{0,8},{4,20},{8,0},{12,28},{16,24},{20,4},{24,16},{28,12},{1,9},{5... | collective-permute-start | bytes 786440 | tf_op jit(solution)/shard_map/ppermute | solution.py:517
  49.5 9.4 %collective-permute-start.16 = (f32[512,128]{1,0:T(8,128)S(1)}, f32[512,128]{1,0:T(8,128)S(1)}, u32[]{:S(2)}, u32[]{:S(2)}) collective-permute-start(f32[512,128]{1,0:T(8,128)S(1)} %get-tuple-element.47.refs_0_), channel_id=1, source_target_pairs={{0,20},{4,8},{8,28},{12,0},{16,4},{20,24},{24,12},{28,16},{1,21},{... | collective-permute-start | bytes 786440 | tf_op jit(solution)/shard_map/ppermute | solution.py:517
  52.0 10.1 %collective-permute-start.13 = (f32[128,256]{1,0:T(8,128)S(1)}, f32[128,256]{1,0:T(8,128)S(1)}, u32[]{:S(2)}, u32[]{:S(2)}) collective-permute-start(f32[128,256]{1,0:T(8,128)S(1)} %get-tuple-element.55), channel_id=1, source_target_pairs={{0,24},{4,28},{8,16},{12,20},{16,8},{20,12},{24,0},{28,4},{1,25},{... | collective-permute-start | bytes 393224 | tf_op jit(solution)/shard_map/ppermute | solution.py:458
  53.3 9.7 %collective-permute-start.12 = (f32[128,256]{1,0:T(8,128)S(1)}, f32[128,256]{1,0:T(8,128)S(1)}, u32[]{:S(2)}, u32[]{:S(2)}) collective-permute-start(f32[128,256]{1,0:T(8,128)S(1)} %get-tuple-element.56), channel_id=1, source_target_pairs={{0,16},{4,20},{8,24},{12,28},{16,0},{20,4},{24,8},{28,12},{1,17},{... | collective-permute-start | bytes 393224 | tf_op jit(solution)/shard_map/ppermute | solution.py:458
  55.1 8.1 %collective-permute-start.11 = (f32[128,256]{1,0:T(8,128)S(1)}, f32[128,256]{1,0:T(8,128)S(1)}, u32[]{:S(2)}, u32[]{:S(2)}) collective-permute-start(f32[128,256]{1,0:T(8,128)S(1)} %get-tuple-element.54), channel_id=1, source_target_pairs={{0,8},{4,12},{8,0},{12,4},{16,24},{20,28},{24,16},{28,20},{1,9},{5... | collective-permute-start | bytes 393224 | tf_op jit(solution)/shard_map/ppermute | solution.py:458
  59.9 9.2 %collective-permute-start.20 = (f32[512,256]{1,0:T(8,128)S(1)}, f32[512,256]{1,0:T(8,128)S(1)}, u32[]{:S(2)}, u32[]{:S(2)}) collective-permute-start(f32[512,256]{1,0:T(8,128)S(1)} %get-tuple-element.53), channel_id=1, source_target_pairs={{0,16},{4,12},{8,24},{12,4},{16,0},{20,28},{24,8},{28,20},{1,17},{... | collective-permute-start | bytes 1572872 | tf_op jit(solution)/shard_map/ppermute | solution.py:535

commit v3 on v2

--- a/solution.py
+++ b/solution.py
@@ -12,6 +12,7 @@
 GROUP = 4
 CORES = 2
 MASKED = -1e30
+STEP = 4
 F32 = jnp.float32
 BF16 = jnp.bfloat16
 
@@ -45,6 +46,10 @@
 
 def in_hbm(x):
     return pltpu.with_memory_space_constraint(x, pltpu.HBM)
+
+
+def key_step(count, tokens):
+    return next(tokens * n for n in (STEP, 2, 1) if count % (tokens * n) == 0)
 
 
 def load_blocks(refs, dst, column):
@@ -90,7 +95,8 @@
         *pieces, top_ref, norm_ref, acc_ref, exp_ref, keys, values, score = refs
     tokens = q_ref.shape[0]
     rows = GROUP * tokens
-    blocks = keys.shape[0] // tokens
+    step = key_step(keys.shape[0], tokens)
+    steps = keys.shape[0] // step
     me = lax.axis_index("seq")
     load_blocks(pieces, keys, 0)
     load_blocks(pieces, values, HD)
@@ -103,22 +109,25 @@
     offset = key_row - query_row
 
     def scores(b, top):
-        block = ((me // CORES) ^ b) * CORES + ((me % CORES) ^ other)
-        at = pl.ds(pl.multiple_of(b * tokens, tokens), tokens)
-        k1, k2, k3 = three(keys[at, :])
+        k1, k2, k3 = three(keys[pl.ds(pl.multiple_of(b * step, step), step), :])
         k12 = jnp.concatenate([k1, k2], axis=1)
         k31 = jnp.concatenate([k3, k1], axis=1)
-        s = mm(k31, q13, NT) + mm(k12, q22, NT) + mm(k12, q11, NT)
-        s = jnp.where(offset <= (me - block) * tokens, s * score_scale, MASKED)
-        score[at, :] = s
-        return jnp.maximum(top, jnp.max(s, axis=0, keepdims=True))
+        found = mm(k31, q13, NT) + mm(k12, q22, NT) + mm(k12, q11, NT)
+        for i in range(step // tokens):
+            which = b * (step // tokens) + i
+            block = ((me // CORES) ^ which) * CORES + ((me % CORES) ^ other)
+            s = found[i * tokens : (i + 1) * tokens] * score_scale
+            s = jnp.where(offset <= (me - block) * tokens, s, MASKED)
+            score[pl.ds(pl.multiple_of(which * tokens, tokens), tokens), :] = s
+            top = jnp.maximum(top, jnp.max(s, axis=0, keepdims=True))
+        return top
 
     before = top_ref[0:1, :] if other else jnp.full((1, rows), MASKED, F32)
-    top = lax.fori_loop(0, blocks, scores, before, unroll=2)
+    top = lax.fori_loop(0, steps, scores, before)
 
     def weigh(b, state):
         norm, acc = state
-        at = pl.ds(pl.multiple_of(b * tokens, tokens), tokens)
+        at = pl.ds(pl.multiple_of(b * step, step), step)
         e = jnp.exp(score[at, :] - top)
         exp_ref[at, :] = e
         eh, el = two(e)
@@ -132,7 +141,7 @@
         start = norm_ref[0:1, :] * factor, acc_ref[...] * factor
     else:
         start = jnp.zeros((1, rows), F32), jnp.zeros((HD, rows), F32)
-    norm, acc = lax.fori_loop(0, blocks, weigh, start, unroll=2)
+    norm, acc = lax.fori_loop(0, steps, weigh, start)
     if other:
         inv = 1.0 / norm
         inv_ref[0:8, :] = jnp.broadcast_to(inv * factor, (8, rows))
@@ -183,15 +192,15 @@
 
 
 def key_grads(score_scale, q, d, exp_ref, inv, dp_ref, delta, keys, out_ref, acc):
-    rows = q.shape[0]
-    tokens = rows // GROUP
+    tokens = q.shape[0] // GROUP
+    step = key_step(keys.shape[0], tokens)
     qh, ql = two(q)
     qhl = jnp.concatenate([qh, ql], axis=1)
     dh, dl = two(d)
     dhl = jnp.concatenate([dh, dl], axis=0)
 
     def grads(b, acc):
-        at = pl.ds(pl.multiple_of(b * tokens, tokens), tokens)
+        at = pl.ds(pl.multiple_of(b * step, step), step)
         p = exp_ref[at, :] * inv
         ds = p * (dp_ref[at, :] - delta) * score_scale
         ph, plo = two(p)
@@ -205,7 +214,7 @@
         out_ref[at, HD : 2 * HD] = dv[:, :HD] + dv[:, HD:] + mm(plo, dh, NT)
         return acc
 
-    return lax.fori_loop(0, out_ref.shape[0] // tokens, grads, acc, unroll=2)
+    return lax.fori_loop(0, keys.shape[0] // step, grads, acc)
 
 
 def backward_far_kernel(score_scale, q_ref, d_ref, near_ref, far_ref, inv_ref, *refs):
@@ -213,6 +222,7 @@
     tokens = q_ref.shape[0]
     rows = GROUP * tokens
     half = keys.shape[0]
+    step = key_step(half, tokens)
     load_blocks(pieces[-1:], keys, 0)
     load_blocks(pieces, values, HD)
     d = stacked_grads(d_ref)
@@ -221,13 +231,13 @@
 
     def probs(exp_ref, out_ref, first):
         def one(b, total):
-            at = pl.ds(pl.multiple_of(b * tokens, tokens), tokens)
-            vh, vl = two(values[pl.ds(pl.multiple_of(first + b * tokens, tokens), tokens), :])
+            at = pl.ds(pl.multiple_of(b * step, step), step)
+            vh, vl = two(values[pl.ds(pl.multiple_of(first + b * step, step), step), :])
             dp = mm(vh, dl) + mm(jnp.concatenate([vh, vl], axis=1), dhh)
             out_ref[at, :] = dp
             return total + jnp.sum(exp_ref[at, :] * dp, axis=0, keepdims=True)
 
-        return lax.fori_loop(0, half // tokens, one, jnp.zeros((1, rows), F32), unroll=2)
+        return lax.fori_loop(0, half // step, one, jnp.zeros((1, rows), F32))
 
     inv = inv_ref[8:9, :]
     delta = probs(near_ref, dp_ref, 0) * inv_ref[0:1, :] + probs(far_ref, far_dp, half) * inv
@@ -418,25 +428,26 @@
     )(weight, *operands)
 
 
-def weight_kernel(count, *refs):
+def weight_kernel(first, count, *refs):
     attn = refs[:count]
     grad = refs[count : 2 * count]
     outs = refs[2 * count :]
     width = outs[0].shape[1]
     a_hi, a_lo = two(jnp.concatenate([ref[...] for ref in attn], axis=1))
-    for t, out in enumerate(outs):
+    for t, out in enumerate(outs, first):
         cut = slice(t * width, (t + 1) * width)
         g_hi, g_lo = two(jnp.concatenate([ref[:, cut] for ref in grad], axis=0))
         out[...] = mm(a_hi, g_lo) + mm(a_lo, g_hi) + mm(a_hi, g_hi)
 
 
-def weight_grad(attn, grad, side, width):
+def weight_grad(attn, grad, first, last, width):
     rows = attn[0].shape[0]
+    outs = last - first
     return pl.pallas_call(
-        functools.partial(weight_kernel, len(attn)),
-        out_shape=(jax.ShapeDtypeStruct((rows, width), F32),) * side,
+        functools.partial(weight_kernel, first, len(attn)),
+        out_shape=(jax.ShapeDtypeStruct((rows, width), F32),) * outs,
         compiler_params=params(),
-        cost_estimate=cost(2 * rows * rows * width * side, 8 * rows * width * side),
+        cost_estimate=cost(6 * rows * rows * width * outs, 8 * rows * width * outs),
         name="weight_grad",
     )(*attn, *grad)
 
@@ -516,7 +527,7 @@
         for i in range(1, len(sets)):
             moved_attn.append(lax.ppermute(attn, "seq", routes(*sets[i])))
             moved_grad.append(lax.ppermute(column[i], "seq", routes(*sets[i])))
-        partial = weight_grad(moved_attn, moved_grad, side, width)
+        partial = weight_grad(moved_attn, moved_grad, 1, side, width)
 
         def final_routes(t):
             found = []
@@ -530,9 +541,11 @@
                 found.append((i, (y * side + x) * CORES + core))
             return found
 
-        grad_wo = partial[0]
+        arrived = []
         for t in range(1, side):
-            moved = lax.ppermute(partial[t], "seq", final_routes(t))
+            arrived.append(lax.ppermute(partial[t - 1], "seq", final_routes(t)))
+        (grad_wo,) = weight_grad(moved_attn, moved_grad, 0, 1, width)
+        for moved in arrived:
             grad_wo = grad_wo + moved
     else:
         grad_full = lax.all_gather(grad_out, "head", axis=1, tiled=True)

time: 70.2 us -> 67.7 us (0.964)
  Pallas kernels: 15.9 us -> 11.8 us
  waiting for transfers between devices: 30.5 us -> 31.9 us
    pallas_call x2, Pallas kernels: 4.69 us -> 2.41 us  [forward(): pl.pallas_call(functools.partial(forward_kernel, score_scale, 1 if carrie...]
    pallas_call x1, Pallas kernels: 3 us -> 1.87 us  [backward_far(): pl.pallas_call(functools.partial(backward_far_kernel, score_scale), out_s...]
    ppermute x6, waiting for transfers between devices: 11.1 us -> 12.2 us  [along(): return lax.ppermute(block, 'head', route)]
    pallas_call x1, Pallas kernels: 2.56 us -> 1.71 us  [backward_near(): pl.pallas_call(functools.partial(backward_near_kernel, score_scale), out_...]
    ppermute x3, waiting for transfers between devices: 2.37 us -> 3.21 us  [body(): moved_grad.append(lax.ppermute(column[i], 'seq', routes(*sets[i])))]
  transfers between devices with their start and end apart: 21 -> 21, of which waited for: 13 -> 13; matrix products, arithmetic and copies ran while one was open for 1% -> 1% of each run, Pallas kernels for 13% -> 11%
where the time goes in v3:
time: 67.7 us; the launch traced here: 67.3 us
  waiting for transfers between devices  31.9 us (47%)
  starting transfers between devices  21.1 us (31%)
  Pallas kernels  11.8 us (17%)
  other arithmetic  1 us (1%)
  between operations  0.82 us (1%)
  local copies, waits for them, and re-layouts  0.69 us (1%)
    ppermute x6, waiting for transfers between devices, along(): return lax.ppermute(block, 'head', route)  12.2 us
    ppermute x6, waiting for transfers between devices, to_chip(): return lax.ppermute(block, 'seq', [(i, i ^ CORES * j) for i in range(seq)])  8.46 us
    ppermute x6, starting transfers between devices, to_chip(): return lax.ppermute(block, 'seq', [(i, i ^ CORES * j) for i in range(seq)])  8.21 us
    ppermute x6, starting transfers between devices, along(): return lax.ppermute(block, 'head', route)  7.79 us
    ppermute x1, waiting for transfers between devices, body(): arrived.append(lax.ppermute(partial[t - 1], 'seq', final_routes(t)))  4.79 us
    pallas_call x3, Pallas kernels, project(): pl.pallas_call(functools.partial(project_kernel, counted(new), counted(ol...  3.52 us
    ppermute x3, waiting for transfers between devices, body(): moved_attn.append(lax.ppermute(attn, 'seq', routes(*sets[i])))  3.23 us
    ppermute x3, waiting for transfers between devices, body(): moved_grad.append(lax.ppermute(column[i], 'seq', routes(*sets[i])))  3.21 us
  transfers between devices with their start and end apart: 21, of which 13 were waited for; matrix products, arithmetic and copies ran while one was open for 1% of the time, Pallas kernels for 11%

profile of v3, /device:TPU:0, one launch (start us, length us, event | category | flops | bytes accessed | tf_op | source)
XLA Modules:
  0.0 67.3 jit_solution(9372616204434344787)
XLA Ops:
  1.8 3.0 %collective-permute-start.6 = (f32[128,256]{1,0:T(8,128)S(1)}, f32[128,256]{1,0:T(8,128)S(1)}, u32[]{:S(2)}, u32[]{:S(2)}) collective-permute-start(f32[128,256]{1,0:T(8,128)S(1)} %get-tuple-element.32.refs_0_), channel_id=1, source_target_pairs={{0,8},{4,12},{8,0},{12,4},{16,24},{20,28},{24,16},{28,20},{1,9},{5... | collective-permute-start | bytes 393224 | tf_op jit(solution)/shard_map/ppermute | solution.py:469
  4.8 1.5 %collective-permute-start.7 = (f32[128,256]{1,0:T(8,128)S(1)}, f32[128,256]{1,0:T(8,128)S(1)}, u32[]{:S(2)}, u32[]{:S(2)}) collective-permute-start(f32[128,256]{1,0:T(8,128)S(1)} %get-tuple-element.32.refs_0_), channel_id=1, source_target_pairs={{0,16},{4,20},{8,24},{12,28},{16,0},{20,4},{24,8},{28,12},{1,17},{... | collective-permute-start | bytes 393224 | tf_op jit(solution)/shard_map/ppermute | solution.py:469
  6.3 2.3 %collective-permute-done.6.refs_1_ = f32[128,256]{1,0:T(8,128)S(1)} collective-permute-done((f32[128,256]{1,0:T(8,128)S(1)}, f32[128,256]{1,0:T(8,128)S(1)}, u32[]{:S(2)}, u32[]{:S(2)}) %collective-permute-start.6) | collective-permute-done | bytes 131104 | tf_op jit(solution)/shard_map/ppermute | solution.py:469
  8.7 3.9 %collective-permute-done.7.refs_2_ = f32[128,256]{1,0:T(8,128)S(1)} collective-permute-done((f32[128,256]{1,0:T(8,128)S(1)}, f32[128,256]{1,0:T(8,128)S(1)}, u32[]{:S(2)}, u32[]{:S(2)}) %collective-permute-start.7) | collective-permute-done | bytes 131104 | tf_op jit(solution)/shard_map/ppermute | solution.py:469
  12.7 1.6 %collective-permute-start.5 = (f32[128,512]{1,0:T(8,128)}, f32[128,512]{1,0:T(8,128)S(1)}, u32[]{:S(2)}, u32[]{:S(2)}) collective-permute-start(f32[128,512]{1,0:T(8,128)} %grad_ref.1), channel_id=1, source_target_pairs={{0,1},{1,0},{2,3},{3,2},{4,5},{5,4},{6,7},{7,6},{8,9},{9,8},{10,11... | collective-permute-start | bytes 786440 | tf_op jit(solution)/shard_map/ppermute | solution.py:472
  14.3 2.6 %collective-permute-start = (f32[64,512]{1,0:T(8,128)S(1)}, f32[64,512]{1,0:T(8,128)S(1)}, u32[]{:S(2)}, u32[]{:S(2)}) collective-permute-start(f32[64,512]{1,0:T(8,128)S(1)} %get-tuple-element.27.refs_1_.refs_6_), channel_id=1, source_target_pairs={{0,2},{1,3},{2,0},{3,1},{4,6},{5,7},{6,4},{7,5},{8,10},{9,11},{10,... | collective-permute-start | bytes 393224 | tf_op jit(solution)/shard_map/ppermute | solution.py:472
  17.9 2.2 %project.3 = (f32[512,128]{1,0:T(8,128)S(1)}, f32[4,512,512]{2,1,0:T(8,128)S(1)}) custom-call(f32[512,2048]{1,0:T(8,128)} %refs_0_.1, f32[64,512]{1,0:T(8,128)S(1)} %get-tuple-element.27.refs_1_.refs_6_, f32[64,512]{1,0:T(8,128)S(1)} %get-tuple-element.28.refs_2_.refs_7_), custom_call_target="tpu_custom_call" | custom-call | flops 805306368 | bytes 1048576 | tf_op jit(solution)/shard_map/project/pallas_call | solution.py:419
  20.2 3.9 %collective-permute-done.refs_1_ = f32[64,512]{1,0:T(8,128)S(1)} collective-permute-done((f32[64,512]{1,0:T(8,128)S(1)}, f32[64,512]{1,0:T(8,128)S(1)}, u32[]{:S(2)}, u32[]{:S(2)}) %collective-permute-start) | collective-permute-done | bytes 131104 | tf_op jit(solution)/shard_map/ppermute | solution.py:472
  24.1 1.3 %collective-permute-start.3 = (f32[64,512]{1,0:T(8,128)S(1)}, f32[64,512]{1,0:T(8,128)S(1)}, u32[]{:S(2)}, u32[]{:S(2)}) collective-permute-start(f32[64,512]{1,0:T(8,128)S(1)} %collective-permute-done.refs_1_), channel_id=1, source_target_pairs={{1,0},{2,3},{5,4},{6,7},{9,8},{10,11},{13,12},{14,15},{17,16},{18,... | collective-permute-start | bytes 393224 | tf_op jit(solution)/shard_map/ppermute | solution.py:472
  25.4 4.4 %collective-permute-done.1.refs_2_ = f32[64,512]{1,0:T(8,128)S(1)} collective-permute-done((f32[64,512]{1,0:T(8,128)S(1)}, f32[64,512]{1,0:T(8,128)S(1)}, u32[]{:S(2)}, u32[]{:S(2)}) %collective-permute-start.1) | collective-permute-done | bytes 131104 | tf_op jit(solution)/shard_map/ppermute | solution.py:472
  29.8 1.3 %collective-permute-start.4 = (f32[64,512]{1,0:T(8,128)S(1)}, f32[64,512]{1,0:T(8,128)S(1)}, u32[]{:S(2)}, u32[]{:S(2)}) collective-permute-start(f32[64,512]{1,0:T(8,128)S(1)} %collective-permute-done.1.refs_2_), channel_id=1, source_target_pairs={{1,0},{2,3},{5,4},{6,7},{9,8},{10,11},{13,12},{14,15},{17,16},{18,... | collective-permute-start | bytes 393224 | tf_op jit(solution)/shard_map/ppermute | solution.py:472
  31.1 1.2 %attn_fwd.2 = (f32[8,512]{1,0:T(8,128)S(1)}, f32[8,512]{1,0:T(8,128)S(1)}, f32[128,512]{1,0:T(8,128)S(1)}, f32[512,512]{1,0:T(8,128)S(1)}) custom-call(f32[128,512]{1,0:T(8,128)S(1)} %copy-done, f32[128,256]{1,0:T(8,128)S(1)} %get-tuple-element.32.refs_0_, f32[128,256]{1,0:T(8,128)S(1)} %collective-permute-done.6.refs_1_, ...), custom_call_target="tpu_custom_call" | custom-call | flops 1207959552 | bytes 2097152 | tf_op jit(solution)/shard_map/attn_fwd/pallas_call | solution.py:172
  32.8 3.8 %collective-permute-done.4.refs_5_ = f32[64,512]{1,0:T(8,128)S(1)} collective-permute-done((f32[64,512]{1,0:T(8,128)S(1)}, f32[64,512]{1,0:T(8,128)S(1)}, u32[]{:S(2)}, u32[]{:S(2)}) %collective-permute-start.4) | collective-permute-done | bytes 131104 | tf_op jit(solution)/shard_map/ppermute | solution.py:472
  37.5 1.2 %attn_fwd.3 = (f32[512,128]{1,0:T(8,128)S(1)}, f32[512,512]{1,0:T(8,128)S(1)}, f32[16,512]{1,0:T(8,128)S(1)}) custom-call(f32[128,512]{1,0:T(8,128)S(1)} %copy-done, f32[512,256]{1,0:T(8,128)S(1)} %collective-permute-done.9.refs_0_.refs_4_, f32[8,512]{1,0:T(8,128)S(1)} %get-tuple-element.34.refs_1_, f32[8,512]{1,0:T(8,128)S(1)} %get-tuple-element.35.refs_2_, ...), custom_call_target="tpu_custom_call" | custom-call | flops 1207959552 | bytes 2097152 | tf_op jit(solution)/shard_map/attn_fwd/pallas_call | solution.py:172
  38.7 1.9 %attn_bwd_far.1 = (f32[128,512]{1,0:T(8,128)S(1)}, f32[512,512]{1,0:T(8,128)S(1)}, f32[8,512]{1,0:T(8,128)S(1)}, f32[512,256]{1,0:T(8,128)S(1)}) custom-call(f32[128,512]{1,0:T(8,128)S(1)} %copy-done, f32[512,128]{1,0:T(8,128)S(1)} %get-tuple-element.31.d_ref, f32[512,512]{1,0:T(8,128)S(1)} %get-tuple-element.33.near_ref, ...), custom_call_target="tpu_custom_call" | custom-call | flops 1610612736 | bytes 4194304 | tf_op jit(solution)/shard_map/attn_bwd_far/pallas_call | solution.py:283
  41.2 1.2 %collective-permute-start.18 = (f32[128,512]{1,0:T(8,128)S(1)}, f32[128,512]{1,0:T(8,128)S(1)}, u32[]{:S(2)}, u32[]{:S(2)}) collective-permute-start(f32[128,512]{1,0:T(8,128)S(1)} %get-tuple-element.48), channel_id=1, source_target_pairs={{0,8},{4,20},{8,0},{12,28},{16,24},{20,4},{24,16},{28,12},{1,9},{5... | collective-permute-start | bytes 786440 | tf_op jit(solution)/shard_map/ppermute | solution.py:529
  43.3 1.7 %attn_bwd_near.1 = (f32[128,512]{1,0:T(8,128)}, f32[512,256]{1,0:T(8,128)S(1)}) custom-call(f32[128,512]{1,0:T(8,128)S(1)} %copy-done, f32[512,128]{1,0:T(8,128)S(1)} %get-tuple-element.31.d_ref, f32[512,512]{1,0:T(8,128)S(1)} %get-tuple-element.33.near_ref, f32[16,512]{1,0:T(8,128)S(1)} %get-tuple-element.37.inv_ref, ...), custom_call_target="tpu_custom_call" | custom-call | flops 1207959552 | bytes 2097152 | tf_op jit(solution)/shard_map/attn_bwd_near/pallas_call | solution.py:304
  45.0 1.2 %collective-permute-start.15 = (f32[512,128]{1,0:T(8,128)S(1)}, f32[512,128]{1,0:T(8,128)S(1)}, u32[]{:S(2)}, u32[]{:S(2)}) collective-permute-start(f32[512,128]{1,0:T(8,128)S(1)} %get-tuple-element.45.refs_0_), channel_id=1, source_target_pairs={{0,8},{4,20},{8,0},{12,28},{16,24},{20,4},{24,16},{28,12},{1,9},{5... | collective-permute-start | bytes 786440 | tf_op jit(solution)/shard_map/ppermute | solution.py:528
  46.6 3.1 %collective-permute-done.18.refs_6_ = f32[128,512]{1,0:T(8,128)S(1)} collective-permute-done((f32[128,512]{1,0:T(8,128)S(1)}, f32[128,512]{1,0:T(8,128)S(1)}, u32[]{:S(2)}, u32[]{:S(2)}) %collective-permute-start.18) | collective-permute-done | bytes 262176 | tf_op jit(solution)/shard_map/ppermute | solution.py:529
  49.7 1.2 %collective-permute-start.13 = (f32[128,256]{1,0:T(8,128)S(1)}, f32[128,256]{1,0:T(8,128)S(1)}, u32[]{:S(2)}, u32[]{:S(2)}) collective-permute-start(f32[128,256]{1,0:T(8,128)S(1)} %get-tuple-element.51), channel_id=1, source_target_pairs={{0,24},{4,28},{8,16},{12,20},{16,8},{20,12},{24,0},{28,4},{1,25},{... | collective-permute-start | bytes 393224 | tf_op jit(solution)/shard_map/ppermute | solution.py:469
  51.0 1.8 %collective-permute-start.12 = (f32[128,256]{1,0:T(8,128)S(1)}, f32[128,256]{1,0:T(8,128)S(1)}, u32[]{:S(2)}, u32[]{:S(2)}) collective-permute-start(f32[128,256]{1,0:T(8,128)S(1)} %get-tuple-element.52), channel_id=1, source_target_pairs={{0,16},{4,20},{8,24},{12,28},{16,0},{20,4},{24,8},{28,12},{1,17},{... | collective-permute-start | bytes 393224 | tf_op jit(solution)/shard_map/ppermute | solution.py:469
  53.4 1.9 %collective-permute-done.15.refs_2_ = f32[512,128]{1,0:T(8,128)S(1)} collective-permute-done((f32[512,128]{1,0:T(8,128)S(1)}, f32[512,128]{1,0:T(8,128)S(1)}, u32[]{:S(2)}, u32[]{:S(2)}) %collective-permute-start.15) | collective-permute-done | bytes 262176 | tf_op jit(solution)/shard_map/ppermute | solution.py:528
  55.3 1.3 %collective-permute-done.16.refs_3_ = f32[512,128]{1,0:T(8,128)S(1)} collective-permute-done((f32[512,128]{1,0:T(8,128)S(1)}, f32[512,128]{1,0:T(8,128)S(1)}, u32[]{:S(2)}, u32[]{:S(2)}) %collective-permute-start.16) | collective-permute-done | bytes 262176 | tf_op jit(solution)/shard_map/ppermute | solution.py:528
  61.7 4.8 %collective-permute-done.20 = f32[512,256]{1,0:T(8,128)S(1)} collective-permute-done((f32[512,256]{1,0:T(8,128)S(1)}, f32[512,256]{1,0:T(8,128)S(1)}, u32[]{:S(2)}, u32[]{:S(2)}) %collective-permute-start.20) | collective-permute-done | bytes 524320 | tf_op jit(solution)/shard_map/ppermute | solution.py:546
  (36 shorter events, 11.8 us)
Async XLA Ops:
  0.6 30.5 %copy-start = (f32[128,512]{1,0:T(8,128)S(1)}, f32[128,512]{1,0:T(8,128)}, u32[]{:S(2)}) copy-start(f32[128,512]{1,0:T(8,128)} %q_ref.7) | copy-start | bytes 786436
  1.8 6.9 %collective-permute-start.6 = (f32[128,256]{1,0:T(8,128)S(1)}, f32[128,256]{1,0:T(8,128)S(1)}, u32[]{:S(2)}, u32[]{:S(2)}) collective-permute-start(f32[128,256]{1,0:T(8,128)S(1)} %get-tuple-element.32.refs_0_), channel_id=1, source_target_pairs={{0,8},{4,12},{8,0},{12,4},{16,24},{20,28},{24,16},{28,20},{1,9},{5... | collective-permute-start | bytes 393224 | tf_op jit(solution)/shard_map/ppermute | solution.py:469
  4.8 7.8 %collective-permute-start.7 = (f32[128,256]{1,0:T(8,128)S(1)}, f32[128,256]{1,0:T(8,128)S(1)}, u32[]{:S(2)}, u32[]{:S(2)}) collective-permute-start(f32[128,256]{1,0:T(8,128)S(1)} %get-tuple-element.32.refs_0_), channel_id=1, source_target_pairs={{0,16},{4,20},{8,24},{12,28},{16,0},{20,4},{24,8},{28,12},{1,17},{... | collective-permute-start | bytes 393224 | tf_op jit(solution)/shard_map/ppermute | solution.py:469
  6.3 6.3 %collective-permute-start.8 = (f32[128,256]{1,0:T(8,128)S(1)}, f32[128,256]{1,0:T(8,128)S(1)}, u32[]{:S(2)}, u32[]{:S(2)}) collective-permute-start(f32[128,256]{1,0:T(8,128)S(1)} %get-tuple-element.32.refs_0_), channel_id=1, source_target_pairs={{0,24},{4,28},{8,16},{12,20},{16,8},{20,12},{24,0},{28,4},{1,25},{... | collective-permute-start | bytes 393224 | tf_op jit(solution)/shard_map/ppermute | solution.py:469
  12.6 24.9 %collective-permute-start.9 = (f32[512,256]{1,0:T(8,128)S(1)}, f32[512,256]{1,0:T(8,128)S(1)}, u32[]{:S(2)}, u32[]{:S(2)}) collective-permute-start(f32[512,256]{1,0:T(8,128)S(1)} %pad_maximum_fusion), channel_id=1, source_target_pairs={{0,4},{4,0},{8,12},{12,8},{16,20},{20,16},{24,28},{28,24},{1,5},{5... | collective-permute-start | bytes 1572872 | tf_op jit(solution)/shard_map/ppermute | solution.py:466
  12.7 19.6 %collective-permute-start.5 = (f32[128,512]{1,0:T(8,128)}, f32[128,512]{1,0:T(8,128)S(1)}, u32[]{:S(2)}, u32[]{:S(2)}) collective-permute-start(f32[128,512]{1,0:T(8,128)} %grad_ref.1), channel_id=1, source_target_pairs={{0,1},{1,0},{2,3},{3,2},{4,5},{5,4},{6,7},{7,6},{8,9},{9,8},{10,11... | collective-permute-start | bytes 786440 | tf_op jit(solution)/shard_map/ppermute | solution.py:472
  14.3 9.8 %collective-permute-start = (f32[64,512]{1,0:T(8,128)S(1)}, f32[64,512]{1,0:T(8,128)S(1)}, u32[]{:S(2)}, u32[]{:S(2)}) collective-permute-start(f32[64,512]{1,0:T(8,128)S(1)} %get-tuple-element.27.refs_1_.refs_6_), channel_id=1, source_target_pairs={{0,2},{1,3},{2,0},{3,1},{4,6},{5,7},{6,4},{7,5},{8,10},{9,11},{10,... | collective-permute-start | bytes 393224 | tf_op jit(solution)/shard_map/ppermute | solution.py:472
  16.9 12.9 %collective-permute-start.1 = (f32[64,512]{1,0:T(8,128)S(1)}, f32[64,512]{1,0:T(8,128)S(1)}, u32[]{:S(2)}, u32[]{:S(2)}) collective-permute-start(f32[64,512]{1,0:T(8,128)S(1)} %get-tuple-element.28.refs_2_.refs_7_), channel_id=1, source_target_pairs={{0,2},{1,3},{2,0},{3,1},{4,6},{5,7},{6,4},{7,5},{8,10},{9,11},{10,... | collective-permute-start | bytes 393224 | tf_op jit(solution)/shard_map/ppermute | solution.py:472
  17.3 15.5 %collective-permute-start.2 = (f32[128,512]{1,0:T(8,128)}, f32[128,512]{1,0:T(8,128)S(1)}, u32[]{:S(2)}, u32[]{:S(2)}) collective-permute-start(f32[128,512]{1,0:T(8,128)} %grad_ref.1), channel_id=1, source_target_pairs={{1,2},{2,1},{5,6},{6,5},{9,10},{10,9},{13,14},{14,13},{17,18},{18,... | collective-permute-start | bytes 786440 | tf_op jit(solution)/shard_map/ppermute | solution.py:472
  24.1 8.7 %collective-permute-start.3 = (f32[64,512]{1,0:T(8,128)S(1)}, f32[64,512]{1,0:T(8,128)S(1)}, u32[]{:S(2)}, u32[]{:S(2)}) collective-permute-start(f32[64,512]{1,0:T(8,128)S(1)} %collective-permute-done.refs_1_), channel_id=1, source_target_pairs={{1,0},{2,3},{5,4},{6,7},{9,8},{10,11},{13,12},{14,15},{17,16},{18,... | collective-permute-start | bytes 393224 | tf_op jit(solution)/shard_map/ppermute | solution.py:472
  29.8 6.8 %collective-permute-start.4 = (f32[64,512]{1,0:T(8,128)S(1)}, f32[64,512]{1,0:T(8,128)S(1)}, u32[]{:S(2)}, u32[]{:S(2)}) collective-permute-start(f32[64,512]{1,0:T(8,128)S(1)} %collective-permute-done.1.refs_2_), channel_id=1, source_target_pairs={{1,0},{2,3},{5,4},{6,7},{9,8},{10,11},{13,12},{14,15},{17,16},{18,... | collective-permute-start | bytes 393224 | tf_op jit(solution)/shard_map/ppermute | solution.py:472
  40.6 4.4 %collective-permute-start.10 = (f32[512,256]{1,0:T(8,128)S(1)}, f32[512,256]{1,0:T(8,128)S(1)}, u32[]{:S(2)}, u32[]{:S(2)}) collective-permute-start(f32[512,256]{1,0:T(8,128)S(1)} %get-tuple-element.44), channel_id=1, source_target_pairs={{0,4},{4,0},{8,12},{12,8},{16,20},{20,16},{24,28},{28,24},{1,5},{5... | collective-permute-start | bytes 1572872 | tf_op jit(solution)/shard_map/ppermute | solution.py:466
  40.7 5.7 %collective-permute-start.17 = (f32[128,512]{1,0:T(8,128)S(1)}, f32[128,512]{1,0:T(8,128)S(1)}, u32[]{:S(2)}, u32[]{:S(2)}) collective-permute-start(f32[128,512]{1,0:T(8,128)S(1)} %get-tuple-element.47), channel_id=1, source_target_pairs={{0,4},{4,0},{8,12},{12,8},{16,20},{20,16},{24,28},{28,24},{1,5},{5... | collective-permute-start | bytes 786440 | tf_op jit(solution)/shard_map/ppermute | solution.py:529
  41.2 8.5 %collective-permute-start.18 = (f32[128,512]{1,0:T(8,128)S(1)}, f32[128,512]{1,0:T(8,128)S(1)}, u32[]{:S(2)}, u32[]{:S(2)}) collective-permute-start(f32[128,512]{1,0:T(8,128)S(1)} %get-tuple-element.48), channel_id=1, source_target_pairs={{0,8},{4,20},{8,0},{12,28},{16,24},{20,4},{24,16},{28,12},{1,9},{5... | collective-permute-start | bytes 786440 | tf_op jit(solution)/shard_map/ppermute | solution.py:529
  42.4 8.6 %collective-permute-start.19 = (f32[128,512]{1,0:T(8,128)S(1)}, f32[128,512]{1,0:T(8,128)S(1)}, u32[]{:S(2)}, u32[]{:S(2)}) collective-permute-start(f32[128,512]{1,0:T(8,128)S(1)} %get-tuple-element.49), channel_id=1, source_target_pairs={{0,20},{4,8},{8,28},{12,0},{16,4},{20,24},{24,12},{28,16},{1,21},{... | collective-permute-start | bytes 786440 | tf_op jit(solution)/shard_map/ppermute | solution.py:529
  42.6 10.2 %collective-permute-start.14 = (f32[512,128]{1,0:T(8,128)S(1)}, f32[512,128]{1,0:T(8,128)S(1)}, u32[]{:S(2)}, u32[]{:S(2)}) collective-permute-start(f32[512,128]{1,0:T(8,128)S(1)} %get-tuple-element.45.refs_0_), channel_id=1, source_target_pairs={{0,4},{4,0},{8,12},{12,8},{16,20},{20,16},{24,28},{28,24},{1,5},{5... | collective-permute-start | bytes 786440 | tf_op jit(solution)/shard_map/ppermute | solution.py:528
  45.0 10.3 %collective-permute-start.15 = (f32[512,128]{1,0:T(8,128)S(1)}, f32[512,128]{1,0:T(8,128)S(1)}, u32[]{:S(2)}, u32[]{:S(2)}) collective-permute-start(f32[512,128]{1,0:T(8,128)S(1)} %get-tuple-element.45.refs_0_), channel_id=1, source_target_pairs={{0,8},{4,20},{8,0},{12,28},{16,24},{20,4},{24,16},{28,12},{1,9},{5... | collective-permute-start | bytes 786440 | tf_op jit(solution)/shard_map/ppermute | solution.py:528
  46.4 10.3 %collective-permute-start.16 = (f32[512,128]{1,0:T(8,128)S(1)}, f32[512,128]{1,0:T(8,128)S(1)}, u32[]{:S(2)}, u32[]{:S(2)}) collective-permute-start(f32[512,128]{1,0:T(8,128)S(1)} %get-tuple-element.45.refs_0_), channel_id=1, source_target_pairs={{0,20},{4,8},{8,28},{12,0},{16,4},{20,24},{24,12},{28,16},{1,21},{... | collective-permute-start | bytes 786440 | tf_op jit(solution)/shard_map/ppermute | solution.py:528
  49.7 10.1 %collective-permute-start.13 = (f32[128,256]{1,0:T(8,128)S(1)}, f32[128,256]{1,0:T(8,128)S(1)}, u32[]{:S(2)}, u32[]{:S(2)}) collective-permute-start(f32[128,256]{1,0:T(8,128)S(1)} %get-tuple-element.51), channel_id=1, source_target_pairs={{0,24},{4,28},{8,16},{12,20},{16,8},{20,12},{24,0},{28,4},{1,25},{... | collective-permute-start | bytes 393224 | tf_op jit(solution)/shard_map/ppermute | solution.py:469
  51.0 9.7 %collective-permute-start.12 = (f32[128,256]{1,0:T(8,128)S(1)}, f32[128,256]{1,0:T(8,128)S(1)}, u32[]{:S(2)}, u32[]{:S(2)}) collective-permute-start(f32[128,256]{1,0:T(8,128)S(1)} %get-tuple-element.52), channel_id=1, source_target_pairs={{0,16},{4,20},{8,24},{12,28},{16,0},{20,4},{24,8},{28,12},{1,17},{... | collective-permute-start | bytes 393224 | tf_op jit(solution)/shard_map/ppermute | solution.py:469
  52.8 8.2 %collective-permute-start.11 = (f32[128,256]{1,0:T(8,128)S(1)}, f32[128,256]{1,0:T(8,128)S(1)}, u32[]{:S(2)}, u32[]{:S(2)}) collective-permute-start(f32[128,256]{1,0:T(8,128)S(1)} %get-tuple-element.50), channel_id=1, source_target_pairs={{0,8},{4,12},{8,0},{12,4},{16,24},{20,28},{24,16},{28,20},{1,9},{5... | collective-permute-start | bytes 393224 | tf_op jit(solution)/shard_map/ppermute | solution.py:469
  57.2 9.2 %collective-permute-start.20 = (f32[512,256]{1,0:T(8,128)S(1)}, f32[512,256]{1,0:T(8,128)S(1)}, u32[]{:S(2)}, u32[]{:S(2)}) collective-permute-start(f32[512,256]{1,0:T(8,128)S(1)} %weight_grad.3), channel_id=1, source_target_pairs={{0,16},{4,12},{8,24},{12,4},{16,0},{20,28},{24,8},{28,20},{1,17},{... | collective-permute-start | bytes 1572872 | tf_op jit(solution)/shard_map/ppermute | solution.py:546

commit v4 on v3

--- a/solution.py
+++ b/solution.py
@@ -13,6 +13,7 @@
 CORES = 2
 MASKED = -1e30
 STEP = 4
+FIRST = 6
 F32 = jnp.float32
 BF16 = jnp.bfloat16
 
@@ -58,6 +59,10 @@
         count = ref.shape[0]
         dst[row : row + count, :] = ref[:, column : column + HD]
         row += count
+
+
+def first_part(tokens):
+    return tokens * FIRST // 8
 
 
 def pack_kernel(keys_ref, values_ref, grad_ref, out_ref, upper_ref, lower_ref, sem):
@@ -77,10 +82,11 @@
 
 def pack(keys, values, grad_out):
     tokens, columns = grad_out.shape
-    part = jax.ShapeDtypeStruct((tokens // 2, columns), F32)
+    upper = first_part(tokens)
+    parts = [jax.ShapeDtypeStruct((n, columns), F32) for n in (upper, tokens - upper)]
     return pl.pallas_call(
         pack_kernel,
-        out_shape=(jax.ShapeDtypeStruct((tokens, 2 * HD), F32), part, part),
+        out_shape=(jax.ShapeDtypeStruct((tokens, 2 * HD), F32), *parts),
         in_specs=[pl.BlockSpec(memory_space=pltpu.HBM)] * 3,
         scratch_shapes=[pltpu.SemaphoreType.DMA((4,))],
         compiler_params=params(),

time: 67.7 us -> 65.7 us (0.970)
  waiting for transfers between devices: 31.9 us -> 25.9 us
  starting transfers between devices: 21.1 us -> 25.1 us
    ppermute x6, starting transfers between devices: 7.79 us -> 11.8 us  [along(): return lax.ppermute(block, 'head', route)]
    ppermute x6, waiting for transfers between devices: 8.46 us -> 5.42 us  [to_chip(): return lax.ppermute(block, 'seq', [(i, i ^ CORES * j) for i in range(seq)])]
    ppermute x6, waiting for transfers between devices: 12.2 us -> 9.29 us  [along(): return lax.ppermute(block, 'head', route)]
  transfers between devices with their start and end apart: 21 -> 21, of which waited for: 13 -> 11; matrix products, arithmetic and copies ran while one was open for 1% -> 1% of each run, Pallas kernels for 11% -> 12%
where the time goes in v4:
time: 65.7 us; the launch traced here: 65.4 us
  waiting for transfers between devices  25.9 us (39%)
  starting transfers between devices  25.1 us (38%)
  Pallas kernels  11.8 us (18%)
  other arithmetic  1 us (2%)
  between operations  0.8 us (1%)
  local copies, waits for them, and re-layouts  0.69 us (1%)
    ppermute x6, starting transfers between devices, along(): return lax.ppermute(block, 'head', route)  11.8 us
    ppermute x6, waiting for transfers between devices, along(): return lax.ppermute(block, 'head', route)  9.29 us
    ppermute x6, starting transfers between devices, to_chip(): return lax.ppermute(block, 'seq', [(i, i ^ CORES * j) for i in range(seq)])  8.19 us
    ppermute x6, waiting for transfers between devices, to_chip(): return lax.ppermute(block, 'seq', [(i, i ^ CORES * j) for i in range(seq)])  5.42 us
    ppermute x1, waiting for transfers between devices, body(): arrived.append(lax.ppermute(partial[t - 1], 'seq', final_routes(t)))  4.78 us
    pallas_call x3, Pallas kernels, project(): pl.pallas_call(functools.partial(project_kernel, counted(new), counted(ol...  3.54 us
    ppermute x3, waiting for transfers between devices, body(): moved_grad.append(lax.ppermute(column[i], 'seq', routes(*sets[i])))  3.23 us
    ppermute x3, waiting for transfers between devices, body(): moved_attn.append(lax.ppermute(attn, 'seq', routes(*sets[i])))  3.21 us
  transfers between devices with their start and end apart: 21, of which 11 were waited for; matrix products, arithmetic and copies ran while one was open for 1% of the time, Pallas kernels for 12%

profile of v4, /device:TPU:0, one launch (start us, length us, event | category | flops | bytes accessed | tf_op | source)
XLA Modules:
  0.0 65.4 jit_solution(10447886159789259526)
XLA Ops:
  0.6 1.1 %pack.1 = (f32[128,256]{1,0:T(8,128)S(1)}, f32[96,512]{1,0:T(8,128)S(1)}, f32[32,512]{1,0:T(8,128)S(1)}) custom-call(f32[128,128]{1,0:T(8,128)} %keys_ref.1, f32[128,128]{1,0:T(8,128)} %values_ref.1, f32[128,512]{1,0:T(8,128)} %grad_ref.1), custom_call_target="tpu_custom_call" | custom-call | tf_op jit(solution)/shard_map/pack/pallas_call | solution.py:87
  1.7 3.0 %collective-permute-start.6 = (f32[128,256]{1,0:T(8,128)S(1)}, f32[128,256]{1,0:T(8,128)S(1)}, u32[]{:S(2)}, u32[]{:S(2)}) collective-permute-start(f32[128,256]{1,0:T(8,128)S(1)} %get-tuple-element.32.refs_0_), channel_id=1, source_target_pairs={{0,8},{4,12},{8,0},{12,4},{16,24},{20,28},{24,16},{28,20},{1,9},{5... | collective-permute-start | bytes 393224 | tf_op jit(solution)/shard_map/ppermute | solution.py:475
  4.8 1.5 %collective-permute-start.7 = (f32[128,256]{1,0:T(8,128)S(1)}, f32[128,256]{1,0:T(8,128)S(1)}, u32[]{:S(2)}, u32[]{:S(2)}) collective-permute-start(f32[128,256]{1,0:T(8,128)S(1)} %get-tuple-element.32.refs_0_), channel_id=1, source_target_pairs={{0,16},{4,20},{8,24},{12,28},{16,0},{20,4},{24,8},{28,12},{1,17},{... | collective-permute-start | bytes 393224 | tf_op jit(solution)/shard_map/ppermute | solution.py:475
  6.3 3.0 %collective-permute-start = (f32[96,512]{1,0:T(8,128)S(1)}, f32[96,512]{1,0:T(8,128)S(1)}, u32[]{:S(2)}, u32[]{:S(2)}) collective-permute-start(f32[96,512]{1,0:T(8,128)S(1)} %get-tuple-element.27.refs_1_.refs_6_), channel_id=1, source_target_pairs={{0,2},{1,3},{2,0},{3,1},{4,6},{5,7},{6,4},{7,5},{8,10},{9,11},{10,... | collective-permute-start | bytes 589832 | tf_op jit(solution)/shard_map/ppermute | solution.py:478
  9.3 3.2 %collective-permute-done.7.refs_2_ = f32[128,256]{1,0:T(8,128)S(1)} collective-permute-done((f32[128,256]{1,0:T(8,128)S(1)}, f32[128,256]{1,0:T(8,128)S(1)}, u32[]{:S(2)}, u32[]{:S(2)}) %collective-permute-start.7) | collective-permute-done | bytes 131104 | tf_op jit(solution)/shard_map/ppermute | solution.py:475
  12.7 1.6 %collective-permute-start.5 = (f32[128,512]{1,0:T(8,128)}, f32[128,512]{1,0:T(8,128)S(1)}, u32[]{:S(2)}, u32[]{:S(2)}) collective-permute-start(f32[128,512]{1,0:T(8,128)} %grad_ref.1), channel_id=1, source_target_pairs={{0,1},{1,0},{2,3},{3,2},{4,5},{5,4},{6,7},{7,6},{8,9},{9,8},{10,11... | collective-permute-start | bytes 786440 | tf_op jit(solution)/shard_map/ppermute | solution.py:478
  15.0 3.9 %collective-permute-start.1 = (f32[32,512]{1,0:T(8,128)S(1)}, f32[32,512]{1,0:T(8,128)S(1)}, u32[]{:S(2)}, u32[]{:S(2)}) collective-permute-start(f32[32,512]{1,0:T(8,128)S(1)} %get-tuple-element.28.refs_2_.refs_7_), channel_id=1, source_target_pairs={{0,2},{1,3},{2,0},{3,1},{4,6},{5,7},{6,4},{7,5},{8,10},{9,11},{10,... | collective-permute-start | bytes 196616 | tf_op jit(solution)/shard_map/ppermute | solution.py:478
  18.9 1.3 %collective-permute-start.3 = (f32[96,512]{1,0:T(8,128)S(1)}, f32[96,512]{1,0:T(8,128)S(1)}, u32[]{:S(2)}, u32[]{:S(2)}) collective-permute-start(f32[96,512]{1,0:T(8,128)S(1)} %collective-permute-done.refs_1_), channel_id=1, source_target_pairs={{1,0},{2,3},{5,4},{6,7},{9,8},{10,11},{13,12},{14,15},{17,16},{18,... | collective-permute-start | bytes 589832 | tf_op jit(solution)/shard_map/ppermute | solution.py:478
  20.2 2.2 %project.3 = (f32[512,128]{1,0:T(8,128)S(1)}, f32[4,512,512]{2,1,0:T(8,128)S(1)}) custom-call(f32[512,2048]{1,0:T(8,128)} %refs_0_.1, f32[96,512]{1,0:T(8,128)S(1)} %get-tuple-element.27.refs_1_.refs_6_, f32[32,512]{1,0:T(8,128)S(1)} %get-tuple-element.28.refs_2_.refs_7_), custom_call_target="tpu_custom_call" | custom-call | flops 805306368 | bytes 1048576 | tf_op jit(solution)/shard_map/project/pallas_call | solution.py:425
  22.4 6.1 %collective-permute-done.1.refs_2_ = f32[32,512]{1,0:T(8,128)S(1)} collective-permute-done((f32[32,512]{1,0:T(8,128)S(1)}, f32[32,512]{1,0:T(8,128)S(1)}, u32[]{:S(2)}, u32[]{:S(2)}) %collective-permute-start.1) | collective-permute-done | bytes 65568 | tf_op jit(solution)/shard_map/ppermute | solution.py:478
  28.5 1.3 %collective-permute-start.4 = (f32[32,512]{1,0:T(8,128)S(1)}, f32[32,512]{1,0:T(8,128)S(1)}, u32[]{:S(2)}, u32[]{:S(2)}) collective-permute-start(f32[32,512]{1,0:T(8,128)S(1)} %collective-permute-done.1.refs_2_), channel_id=1, source_target_pairs={{1,0},{2,3},{5,4},{6,7},{9,8},{10,11},{13,12},{14,15},{17,16},{18,... | collective-permute-start | bytes 196616 | tf_op jit(solution)/shard_map/ppermute | solution.py:478
  29.8 1.2 %attn_fwd.2 = (f32[8,512]{1,0:T(8,128)S(1)}, f32[8,512]{1,0:T(8,128)S(1)}, f32[128,512]{1,0:T(8,128)S(1)}, f32[512,512]{1,0:T(8,128)S(1)}) custom-call(f32[128,512]{1,0:T(8,128)S(1)} %copy-done, f32[128,256]{1,0:T(8,128)S(1)} %get-tuple-element.32.refs_0_, f32[128,256]{1,0:T(8,128)S(1)} %collective-permute-done.6.refs_1_, ...), custom_call_target="tpu_custom_call" | custom-call | flops 1207959552 | bytes 2097152 | tf_op jit(solution)/shard_map/attn_fwd/pallas_call | solution.py:178
  31.5 3.2 %collective-permute-done.4.refs_5_ = f32[32,512]{1,0:T(8,128)S(1)} collective-permute-done((f32[32,512]{1,0:T(8,128)S(1)}, f32[32,512]{1,0:T(8,128)S(1)}, u32[]{:S(2)}, u32[]{:S(2)}) %collective-permute-start.4) | collective-permute-done | bytes 65568 | tf_op jit(solution)/shard_map/ppermute | solution.py:478
  35.5 1.2 %attn_fwd.3 = (f32[512,128]{1,0:T(8,128)S(1)}, f32[512,512]{1,0:T(8,128)S(1)}, f32[16,512]{1,0:T(8,128)S(1)}) custom-call(f32[128,512]{1,0:T(8,128)S(1)} %copy-done, f32[512,256]{1,0:T(8,128)S(1)} %collective-permute-done.9.refs_0_.refs_4_, f32[8,512]{1,0:T(8,128)S(1)} %get-tuple-element.34.refs_1_, f32[8,512]{1,0:T(8,128)S(1)} %get-tuple-element.35.refs_2_, ...), custom_call_target="tpu_custom_call" | custom-call | flops 1207959552 | bytes 2097152 | tf_op jit(solution)/shard_map/attn_fwd/pallas_call | solution.py:178
  36.7 1.9 %attn_bwd_far.1 = (f32[128,512]{1,0:T(8,128)S(1)}, f32[512,512]{1,0:T(8,128)S(1)}, f32[8,512]{1,0:T(8,128)S(1)}, f32[512,256]{1,0:T(8,128)S(1)}) custom-call(f32[128,512]{1,0:T(8,128)S(1)} %copy-done, f32[512,128]{1,0:T(8,128)S(1)} %get-tuple-element.31.d_ref, f32[512,512]{1,0:T(8,128)S(1)} %get-tuple-element.33.near_ref, ...), custom_call_target="tpu_custom_call" | custom-call | flops 1610612736 | bytes 4194304 | tf_op jit(solution)/shard_map/attn_bwd_far/pallas_call | solution.py:289
  39.2 1.2 %collective-permute-start.18 = (f32[128,512]{1,0:T(8,128)S(1)}, f32[128,512]{1,0:T(8,128)S(1)}, u32[]{:S(2)}, u32[]{:S(2)}) collective-permute-start(f32[128,512]{1,0:T(8,128)S(1)} %get-tuple-element.48), channel_id=1, source_target_pairs={{0,8},{4,20},{8,0},{12,28},{16,24},{20,4},{24,16},{28,12},{1,9},{5... | collective-permute-start | bytes 786440 | tf_op jit(solution)/shard_map/ppermute | solution.py:535
  41.3 1.7 %attn_bwd_near.1 = (f32[128,512]{1,0:T(8,128)}, f32[512,256]{1,0:T(8,128)S(1)}) custom-call(f32[128,512]{1,0:T(8,128)S(1)} %copy-done, f32[512,128]{1,0:T(8,128)S(1)} %get-tuple-element.31.d_ref, f32[512,512]{1,0:T(8,128)S(1)} %get-tuple-element.33.near_ref, f32[16,512]{1,0:T(8,128)S(1)} %get-tuple-element.37.inv_ref, ...), custom_call_target="tpu_custom_call" | custom-call | flops 1207959552 | bytes 2097152 | tf_op jit(solution)/shard_map/attn_bwd_near/pallas_call | solution.py:310
  43.1 1.2 %collective-permute-start.15 = (f32[512,128]{1,0:T(8,128)S(1)}, f32[512,128]{1,0:T(8,128)S(1)}, u32[]{:S(2)}, u32[]{:S(2)}) collective-permute-start(f32[512,128]{1,0:T(8,128)S(1)} %get-tuple-element.45.refs_0_), channel_id=1, source_target_pairs={{0,8},{4,20},{8,0},{12,28},{16,24},{20,4},{24,16},{28,12},{1,9},{5... | collective-permute-start | bytes 786440 | tf_op jit(solution)/shard_map/ppermute | solution.py:534
  44.6 3.2 %collective-permute-done.18.refs_6_ = f32[128,512]{1,0:T(8,128)S(1)} collective-permute-done((f32[128,512]{1,0:T(8,128)S(1)}, f32[128,512]{1,0:T(8,128)S(1)}, u32[]{:S(2)}, u32[]{:S(2)}) %collective-permute-start.18) | collective-permute-done | bytes 262176 | tf_op jit(solution)/shard_map/ppermute | solution.py:535
  47.7 1.2 %collective-permute-start.13 = (f32[128,256]{1,0:T(8,128)S(1)}, f32[128,256]{1,0:T(8,128)S(1)}, u32[]{:S(2)}, u32[]{:S(2)}) collective-permute-start(f32[128,256]{1,0:T(8,128)S(1)} %get-tuple-element.51), channel_id=1, source_target_pairs={{0,24},{4,28},{8,16},{12,20},{16,8},{20,12},{24,0},{28,4},{1,25},{... | collective-permute-start | bytes 393224 | tf_op jit(solution)/shard_map/ppermute | solution.py:475
  49.0 1.8 %collective-permute-start.12 = (f32[128,256]{1,0:T(8,128)S(1)}, f32[128,256]{1,0:T(8,128)S(1)}, u32[]{:S(2)}, u32[]{:S(2)}) collective-permute-start(f32[128,256]{1,0:T(8,128)S(1)} %get-tuple-element.52), channel_id=1, source_target_pairs={{0,16},{4,20},{8,24},{12,28},{16,0},{20,4},{24,8},{28,12},{1,17},{... | collective-permute-start | bytes 393224 | tf_op jit(solution)/shard_map/ppermute | solution.py:475
  51.4 1.9 %collective-permute-done.15.refs_2_ = f32[512,128]{1,0:T(8,128)S(1)} collective-permute-done((f32[512,128]{1,0:T(8,128)S(1)}, f32[512,128]{1,0:T(8,128)S(1)}, u32[]{:S(2)}, u32[]{:S(2)}) %collective-permute-start.15) | collective-permute-done | bytes 262176 | tf_op jit(solution)/shard_map/ppermute | solution.py:534
  53.4 1.3 %collective-permute-done.16.refs_3_ = f32[512,128]{1,0:T(8,128)S(1)} collective-permute-done((f32[512,128]{1,0:T(8,128)S(1)}, f32[512,128]{1,0:T(8,128)S(1)}, u32[]{:S(2)}, u32[]{:S(2)}) %collective-permute-start.16) | collective-permute-done | bytes 262176 | tf_op jit(solution)/shard_map/ppermute | solution.py:534
  59.7 4.8 %collective-permute-done.20 = f32[512,256]{1,0:T(8,128)S(1)} collective-permute-done((f32[512,256]{1,0:T(8,128)S(1)}, f32[512,256]{1,0:T(8,128)S(1)}, u32[]{:S(2)}, u32[]{:S(2)}) %collective-permute-start.20) | collective-permute-done | bytes 524320 | tf_op jit(solution)/shard_map/ppermute | solution.py:552
  (36 shorter events, 10.5 us)
Async XLA Ops:
  0.6 29.2 %copy-start = (f32[128,512]{1,0:T(8,128)S(1)}, f32[128,512]{1,0:T(8,128)}, u32[]{:S(2)}) copy-start(f32[128,512]{1,0:T(8,128)} %q_ref.7) | copy-start | bytes 786436
  1.7 7.6 %collective-permute-start.6 = (f32[128,256]{1,0:T(8,128)S(1)}, f32[128,256]{1,0:T(8,128)S(1)}, u32[]{:S(2)}, u32[]{:S(2)}) collective-permute-start(f32[128,256]{1,0:T(8,128)S(1)} %get-tuple-element.32.refs_0_), channel_id=1, source_target_pairs={{0,8},{4,12},{8,0},{12,4},{16,24},{20,28},{24,16},{28,20},{1,9},{5... | collective-permute-start | bytes 393224 | tf_op jit(solution)/shard_map/ppermute | solution.py:475
  4.8 7.8 %collective-permute-start.7 = (f32[128,256]{1,0:T(8,128)S(1)}, f32[128,256]{1,0:T(8,128)S(1)}, u32[]{:S(2)}, u32[]{:S(2)}) collective-permute-start(f32[128,256]{1,0:T(8,128)S(1)} %get-tuple-element.32.refs_0_), channel_id=1, source_target_pairs={{0,16},{4,20},{8,24},{12,28},{16,0},{20,4},{24,8},{28,12},{1,17},{... | collective-permute-start | bytes 393224 | tf_op jit(solution)/shard_map/ppermute | solution.py:475
  6.3 6.3 %collective-permute-start.8 = (f32[128,256]{1,0:T(8,128)S(1)}, f32[128,256]{1,0:T(8,128)S(1)}, u32[]{:S(2)}, u32[]{:S(2)}) collective-permute-start(f32[128,256]{1,0:T(8,128)S(1)} %get-tuple-element.32.refs_0_), channel_id=1, source_target_pairs={{0,24},{4,28},{8,16},{12,20},{16,8},{20,12},{24,0},{28,4},{1,25},{... | collective-permute-start | bytes 393224 | tf_op jit(solution)/shard_map/ppermute | solution.py:475
  6.3 12.6 %collective-permute-start = (f32[96,512]{1,0:T(8,128)S(1)}, f32[96,512]{1,0:T(8,128)S(1)}, u32[]{:S(2)}, u32[]{:S(2)}) collective-permute-start(f32[96,512]{1,0:T(8,128)S(1)} %get-tuple-element.27.refs_1_.refs_6_), channel_id=1, source_target_pairs={{0,2},{1,3},{2,0},{3,1},{4,6},{5,7},{6,4},{7,5},{8,10},{9,11},{10,... | collective-permute-start | bytes 589832 | tf_op jit(solution)/shard_map/ppermute | solution.py:478
  12.6 23.0 %collective-permute-start.9 = (f32[512,256]{1,0:T(8,128)S(1)}, f32[512,256]{1,0:T(8,128)S(1)}, u32[]{:S(2)}, u32[]{:S(2)}) collective-permute-start(f32[512,256]{1,0:T(8,128)S(1)} %pad_maximum_fusion), channel_id=1, source_target_pairs={{0,4},{4,0},{8,12},{12,8},{16,20},{20,16},{24,28},{28,24},{1,5},{5... | collective-permute-start | bytes 1572872 | tf_op jit(solution)/shard_map/ppermute | solution.py:472
  12.7 18.4 %collective-permute-start.5 = (f32[128,512]{1,0:T(8,128)}, f32[128,512]{1,0:T(8,128)S(1)}, u32[]{:S(2)}, u32[]{:S(2)}) collective-permute-start(f32[128,512]{1,0:T(8,128)} %grad_ref.1), channel_id=1, source_target_pairs={{0,1},{1,0},{2,3},{3,2},{4,5},{5,4},{6,7},{7,6},{8,9},{9,8},{10,11... | collective-permute-start | bytes 786440 | tf_op jit(solution)/shard_map/ppermute | solution.py:478
  14.3 20.4 %collective-permute-start.2 = (f32[128,512]{1,0:T(8,128)}, f32[128,512]{1,0:T(8,128)S(1)}, u32[]{:S(2)}, u32[]{:S(2)}) collective-permute-start(f32[128,512]{1,0:T(8,128)} %grad_ref.1), channel_id=1, source_target_pairs={{1,2},{2,1},{5,6},{6,5},{9,10},{10,9},{13,14},{14,13},{17,18},{18,... | collective-permute-start | bytes 786440 | tf_op jit(solution)/shard_map/ppermute | solution.py:478
  15.0 13.6 %collective-permute-start.1 = (f32[32,512]{1,0:T(8,128)S(1)}, f32[32,512]{1,0:T(8,128)S(1)}, u32[]{:S(2)}, u32[]{:S(2)}) collective-permute-start(f32[32,512]{1,0:T(8,128)S(1)} %get-tuple-element.28.refs_2_.refs_7_), channel_id=1, source_target_pairs={{0,2},{1,3},{2,0},{3,1},{4,6},{5,7},{6,4},{7,5},{8,10},{9,11},{10,... | collective-permute-start | bytes 196616 | tf_op jit(solution)/shard_map/ppermute | solution.py:478
  18.9 15.8 %collective-permute-start.3 = (f32[96,512]{1,0:T(8,128)S(1)}, f32[96,512]{1,0:T(8,128)S(1)}, u32[]{:S(2)}, u32[]{:S(2)}) collective-permute-start(f32[96,512]{1,0:T(8,128)S(1)} %collective-permute-done.refs_1_), channel_id=1, source_target_pairs={{1,0},{2,3},{5,4},{6,7},{9,8},{10,11},{13,12},{14,15},{17,16},{18,... | collective-permute-start | bytes 589832 | tf_op jit(solution)/shard_map/ppermute | solution.py:478
  28.5 6.1 %collective-permute-start.4 = (f32[32,512]{1,0:T(8,128)S(1)}, f32[32,512]{1,0:T(8,128)S(1)}, u32[]{:S(2)}, u32[]{:S(2)}) collective-permute-start(f32[32,512]{1,0:T(8,128)S(1)} %collective-permute-done.1.refs_2_), channel_id=1, source_target_pairs={{1,0},{2,3},{5,4},{6,7},{9,8},{10,11},{13,12},{14,15},{17,16},{18,... | collective-permute-start | bytes 196616 | tf_op jit(solution)/shard_map/ppermute | solution.py:478
  38.6 4.4 %collective-permute-start.10 = (f32[512,256]{1,0:T(8,128)S(1)}, f32[512,256]{1,0:T(8,128)S(1)}, u32[]{:S(2)}, u32[]{:S(2)}) collective-permute-start(f32[512,256]{1,0:T(8,128)S(1)} %get-tuple-element.44), channel_id=1, source_target_pairs={{0,4},{4,0},{8,12},{12,8},{16,20},{20,16},{24,28},{28,24},{1,5},{5... | collective-permute-start | bytes 1572872 | tf_op jit(solution)/shard_map/ppermute | solution.py:472
  38.7 5.7 %collective-permute-start.17 = (f32[128,512]{1,0:T(8,128)S(1)}, f32[128,512]{1,0:T(8,128)S(1)}, u32[]{:S(2)}, u32[]{:S(2)}) collective-permute-start(f32[128,512]{1,0:T(8,128)S(1)} %get-tuple-element.47), channel_id=1, source_target_pairs={{0,4},{4,0},{8,12},{12,8},{16,20},{20,16},{24,28},{28,24},{1,5},{5... | collective-permute-start | bytes 786440 | tf_op jit(solution)/shard_map/ppermute | solution.py:535
  39.2 8.5 %collective-permute-start.18 = (f32[128,512]{1,0:T(8,128)S(1)}, f32[128,512]{1,0:T(8,128)S(1)}, u32[]{:S(2)}, u32[]{:S(2)}) collective-permute-start(f32[128,512]{1,0:T(8,128)S(1)} %get-tuple-element.48), channel_id=1, source_target_pairs={{0,8},{4,20},{8,0},{12,28},{16,24},{20,4},{24,16},{28,12},{1,9},{5... | collective-permute-start | bytes 786440 | tf_op jit(solution)/shard_map/ppermute | solution.py:535
  40.4 8.6 %collective-permute-start.19 = (f32[128,512]{1,0:T(8,128)S(1)}, f32[128,512]{1,0:T(8,128)S(1)}, u32[]{:S(2)}, u32[]{:S(2)}) collective-permute-start(f32[128,512]{1,0:T(8,128)S(1)} %get-tuple-element.49), channel_id=1, source_target_pairs={{0,20},{4,8},{8,28},{12,0},{16,4},{20,24},{24,12},{28,16},{1,21},{... | collective-permute-start | bytes 786440 | tf_op jit(solution)/shard_map/ppermute | solution.py:535
  40.6 10.2 %collective-permute-start.14 = (f32[512,128]{1,0:T(8,128)S(1)}, f32[512,128]{1,0:T(8,128)S(1)}, u32[]{:S(2)}, u32[]{:S(2)}) collective-permute-start(f32[512,128]{1,0:T(8,128)S(1)} %get-tuple-element.45.refs_0_), channel_id=1, source_target_pairs={{0,4},{4,0},{8,12},{12,8},{16,20},{20,16},{24,28},{28,24},{1,5},{5... | collective-permute-start | bytes 786440 | tf_op jit(solution)/shard_map/ppermute | solution.py:534
  43.1 10.3 %collective-permute-start.15 = (f32[512,128]{1,0:T(8,128)S(1)}, f32[512,128]{1,0:T(8,128)S(1)}, u32[]{:S(2)}, u32[]{:S(2)}) collective-permute-start(f32[512,128]{1,0:T(8,128)S(1)} %get-tuple-element.45.refs_0_), channel_id=1, source_target_pairs={{0,8},{4,20},{8,0},{12,28},{16,24},{20,4},{24,16},{28,12},{1,9},{5... | collective-permute-start | bytes 786440 | tf_op jit(solution)/shard_map/ppermute | solution.py:534
  44.4 10.3 %collective-permute-start.16 = (f32[512,128]{1,0:T(8,128)S(1)}, f32[512,128]{1,0:T(8,128)S(1)}, u32[]{:S(2)}, u32[]{:S(2)}) collective-permute-start(f32[512,128]{1,0:T(8,128)S(1)} %get-tuple-element.45.refs_0_), channel_id=1, source_target_pairs={{0,20},{4,8},{8,28},{12,0},{16,4},{20,24},{24,12},{28,16},{1,21},{... | collective-permute-start | bytes 786440 | tf_op jit(solution)/shard_map/ppermute | solution.py:534
  47.7 10.1 %collective-permute-start.13 = (f32[128,256]{1,0:T(8,128)S(1)}, f32[128,256]{1,0:T(8,128)S(1)}, u32[]{:S(2)}, u32[]{:S(2)}) collective-permute-start(f32[128,256]{1,0:T(8,128)S(1)} %get-tuple-element.51), channel_id=1, source_target_pairs={{0,24},{4,28},{8,16},{12,20},{16,8},{20,12},{24,0},{28,4},{1,25},{... | collective-permute-start | bytes 393224 | tf_op jit(solution)/shard_map/ppermute | solution.py:475
  49.0 9.7 %collective-permute-start.12 = (f32[128,256]{1,0:T(8,128)S(1)}, f32[128,256]{1,0:T(8,128)S(1)}, u32[]{:S(2)}, u32[]{:S(2)}) collective-permute-start(f32[128,256]{1,0:T(8,128)S(1)} %get-tuple-element.52), channel_id=1, source_target_pairs={{0,16},{4,20},{8,24},{12,28},{16,0},{20,4},{24,8},{28,12},{1,17},{... | collective-permute-start | bytes 393224 | tf_op jit(solution)/shard_map/ppermute | solution.py:475
  50.8 8.2 %collective-permute-start.11 = (f32[128,256]{1,0:T(8,128)S(1)}, f32[128,256]{1,0:T(8,128)S(1)}, u32[]{:S(2)}, u32[]{:S(2)}) collective-permute-start(f32[128,256]{1,0:T(8,128)S(1)} %get-tuple-element.50), channel_id=1, source_target_pairs={{0,8},{4,12},{8,0},{12,4},{16,24},{20,28},{24,16},{28,20},{1,9},{5... | collective-permute-start | bytes 393224 | tf_op jit(solution)/shard_map/ppermute | solution.py:475
  55.2 9.2 %collective-permute-start.20 = (f32[512,256]{1,0:T(8,128)S(1)}, f32[512,256]{1,0:T(8,128)S(1)}, u32[]{:S(2)}, u32[]{:S(2)}) collective-permute-start(f32[512,256]{1,0:T(8,128)S(1)} %weight_grad.3), channel_id=1, source_target_pairs={{0,16},{4,12},{8,24},{12,4},{16,0},{20,28},{24,8},{28,20},{1,17},{... | collective-permute-start | bytes 1572872 | tf_op jit(solution)/shard_map/ppermute | solution.py:552
